TPU v7x, 256 devices: a whole 4x4x8 slice. The times are simulated.
256 devices in a mesh: tok: 128 (over x_hi, y, z, core), head: 2 (over x_lo).
Axes of the slice: x: 4 (x_hi: 2, x_lo: 2; x = x_hi * 2 + x_lo), y: 4, z: 8, core: 2. Of those that a mesh axis runs over, the one named last changes fastest.
Arguments:
- tokens: bfloat16 [16384, 768], P('tok', 'head'), may hold values from -64 to 64
- view_ids: int32 [16384], P('tok'), may hold values from 0 to 19, never falling along the last dimension, each value on 1 to 1024 neighbouring positions
- query_weight: bfloat16 [768, 768], P(None, 'head'), may hold values from -0.21875 to 0.21875
- key_weight: bfloat16 [768, 768], P(None, 'head'), may hold values from -0.4375 to 0.4375
- value_weight: bfloat16 [768, 768], P(None, 'head'), may hold values from -0.21875 to 0.21875
- out_weight: bfloat16 [768, 768], P('head'), may hold values from -0.21875 to 0.21875
- rate_weight: bfloat16 [768, 4], P(None, 'head'), may hold values from -0.21875 to 0.21875
- fast_gate: float32 [4, 192, 384], P('head'), may hold values from -0.4375 to 0.4375
- fast_up: float32 [4, 192, 384], P('head'), may hold values from -0.4375 to 0.4375
- fast_down: float32 [4, 192, 384], P('head'), may hold values from -0.3125 to 0.3125
- step_size: float32 [4], P('head'), may hold values from 1 to 3
Outputs:
- layer_out: bfloat16 [16384, 768], P('tok', 'head')
Inputs may be any that keep to these rules, and one draw needn't show every extreme that they name: `view_ids`: Non-decreasing along the tokens; every view number appears, on one contiguous run of 1 to 1024 tokens, and some view has exactly 1024.
All inputs are finite; a program needn't handle non-finite values.
Results may differ from a plain program's by a relative error of at most 0.014.
The roundings to bfloat16 on the way count: a program that leaves them out, or rounds other values in their place, can miss the bound.
Values may be sent and summed in bfloat16 or wider, within the bound.
No kernel may reach another device: no remote copies, remote signals or barrier semaphores. Data moves between devices by JAX's collectives and lax.ppermute only.
A program may use at most 64 MiB of HBM per device.

v0:
```python
import jax
import jax.numpy as jnp
from jax import lax
from jax.sharding import PartitionSpec as P

NS_STEPS = 5


newton_a = 3.4445
newton_b = -4.775
newton_c = 2.0315
epsilon = 1e-06
masked_score = -1e30


def passed_along(value, axis, steps):
    count = lax.axis_size(axis)
    leading, last = (max(0, -steps), min(count, count - steps))
    return lax.ppermute(value, axis, [(source, source + steps) for source in range(leading, last)])


def normalize(values):
    widened = values.astype(jnp.float32)
    scale = lax.rsqrt(jnp.mean(widened * widened, axis=-1, keepdims=True) + epsilon)
    return (widened * scale).astype(jnp.bfloat16)


def orthogonalize(matrix):
    length = jnp.sqrt(jnp.sum(matrix * matrix, axis=(-2, -1), keepdims=True))
    current = matrix / (length + epsilon)
    for ns_step in range(NS_STEPS):
        square = jnp.einsum("...ik,...jk->...ij", current, current, precision=lax.Precision.HIGHEST)
        mixer = newton_b * square + newton_c * jnp.einsum(
            "...ik,...kj->...ij", square, square, precision=lax.Precision.HIGHEST
        )
        current = newton_a * current + jnp.einsum(
            "...ik,...kj->...ij", mixer, current, precision=lax.Precision.HIGHEST
        )
    return current


def fast_terms(keys_n, values, rates, lowered):
    gate = jnp.einsum("thd,hdf->thf", keys_n, lowered[:, 0], preferred_element_type=jnp.float32)
    upward = jnp.einsum("thd,hdf->thf", keys_n, lowered[:, 1], preferred_element_type=jnp.float32)
    active = jax.nn.silu(gate)
    product = (active * upward).astype(jnp.bfloat16)
    error = (-rates[:, :, None] * values.astype(jnp.float32)).astype(jnp.bfloat16)
    grad_down = jnp.einsum("thf,thd->hdf", product, error, preferred_element_type=jnp.float32)
    back = jnp.einsum("thd,hdf->thf", error, lowered[:, 2], preferred_element_type=jnp.float32)
    logistic = jax.nn.sigmoid(gate)
    grad_gate_in = (back * upward * logistic * (1.0 + gate * (1.0 - logistic))).astype(jnp.bfloat16)
    grad_up_in = (back * active).astype(jnp.bfloat16)
    grad_gate = jnp.einsum("thd,thf->hdf", keys_n, grad_gate_in, preferred_element_type=jnp.float32)
    grad_up = jnp.einsum("thd,thf->hdf", keys_n, grad_up_in, preferred_element_type=jnp.float32)
    return jnp.stack((grad_gate, grad_up, grad_down), 1)


def apply_fast(queries_n, fresh):
    gate = jnp.einsum("thd,hdf->thf", queries_n, fresh[:, 0], preferred_element_type=jnp.float32)
    upward = jnp.einsum("thd,hdf->thf", queries_n, fresh[:, 1], preferred_element_type=jnp.float32)
    product = (jax.nn.silu(gate) * upward).astype(jnp.bfloat16)
    return jnp.einsum("thf,hdf->thd", product, fresh[:, 2], preferred_element_type=jnp.float32)


def attend_head(query_rows, key_rows, value_rows, query_view, key_view):
    scores = jnp.dot(query_rows, key_rows.T, preferred_element_type=jnp.float32)
    scores = scores * query_rows.shape[1] ** (-0.5)
    allowed = query_view[:, None] == key_view[None, :]
    scores = jnp.where(allowed, scores, masked_score)
    peak = jnp.max(scores, axis=-1, keepdims=True)
    weights = jnp.exp(scores - peak)
    weights = (weights / jnp.sum(weights, axis=-1, keepdims=True)).astype(jnp.bfloat16)
    return jnp.dot(weights, value_rows, preferred_element_type=jnp.float32)


def body(
    tokens,
    view_ids,
    query_weight,
    key_weight,
    value_weight,
    out_weight,
    rate_weight,
    fast_gate,
    fast_up,
    fast_down,
    step_size,
):
    whole = lax.all_gather(tokens, "head", axis=1, tiled=True)
    tok_rows = whole.shape[0]
    head_count = fast_gate.shape[0]
    head_width = fast_gate.shape[1]
    queries = jnp.dot(whole, query_weight, preferred_element_type=jnp.float32).astype(jnp.bfloat16)
    keys = jnp.dot(whole, key_weight, preferred_element_type=jnp.float32).astype(jnp.bfloat16)
    values = jnp.dot(whole, value_weight, preferred_element_type=jnp.float32).astype(jnp.bfloat16)
    rates = jax.nn.softplus(jnp.dot(whole, rate_weight, preferred_element_type=jnp.float32))
    device = lax.axis_index("tok")
    tok_count = lax.axis_size("tok")
    view_span = min(8, tok_count // 4)
    rates = rates * (device < 3 * tok_count // 4).astype(jnp.float32)
    query_heads = queries.reshape(tok_rows, head_count, head_width)
    key_heads = keys.reshape(tok_rows, head_count, head_width)
    value_heads = values.reshape(tok_rows, head_count, head_width)
    master = jnp.stack((fast_gate, fast_up, fast_down), 1)
    lowered = master.astype(jnp.bfloat16)
    terms = fast_terms(normalize(key_heads), value_heads, rates, lowered)
    view_float = view_ids.astype(jnp.bfloat16)
    payload = (keys, values, view_float)
    before_pieces = []
    after_pieces = []
    for offset in range(1, view_span + 1):
        before_pieces.append(passed_along((payload[0], payload[1], payload[2]), "tok", offset))
        after_pieces.append(passed_along((payload[0], payload[1], payload[2]), "tok", -offset))
    total = lax.psum(terms, "tok")
    fresh = (master - step_size[:, None, None, None] * orthogonalize(total)).astype(jnp.bfloat16)
    own_views = view_float.astype(jnp.float32)
    key_blocks = []
    value_blocks = []
    view_blocks = []
    for offset in range(view_span, 0, -1):
        piece = before_pieces[offset - 1]
        key_blocks.append(piece[0])
        value_blocks.append(piece[1])
        view_blocks.append(jnp.where(device >= offset, piece[2].astype(jnp.float32), -1.0))
    key_blocks.append(keys)
    value_blocks.append(values)
    view_blocks.append(own_views)
    for offset in range(1, view_span + 1):
        piece = after_pieces[offset - 1]
        key_blocks.append(piece[0])
        value_blocks.append(piece[1])
        view_blocks.append(
            jnp.where(device + offset < tok_count, piece[2].astype(jnp.float32), -1.0)
        )
    near_rows = (2 * view_span + 1) * tok_rows
    near_keys = jnp.moveaxis(
        jnp.concatenate(key_blocks, 0).reshape(near_rows, head_count, head_width), 1, 0
    )
    near_values = jnp.moveaxis(
        jnp.concatenate(value_blocks, 0).reshape(near_rows, head_count, head_width), 1, 0
    )
    near_views = jnp.concatenate(view_blocks, 0)
    block_rows = min(tok_rows, 512)
    block_count = tok_rows // block_rows
    query_major = jnp.moveaxis(query_heads, 1, 0)

    def attend_block(block_index):

        def one_head(operands):
            return attend_head(operands[0], operands[1], operands[2], own_views, near_views)

        return lax.map(one_head, (query_major, near_keys, near_values))

    attended_major = lax.map(attend_block, jnp.arange(block_count, dtype=jnp.int32))
    attended = jnp.moveaxis(attended_major, 1, 2).reshape(tok_rows, head_count, head_width)
    applied = apply_fast(normalize(query_heads), fresh)
    mixed = (attended + applied).astype(jnp.bfloat16).reshape(tok_rows, head_count * head_width)
    partial_value = jnp.dot(mixed, out_weight, preferred_element_type=jnp.float32)
    return lax.psum_scatter(partial_value, "head", scatter_dimension=1, tiled=True).astype(
        jnp.bfloat16
    )


def solution(mesh):
    placed = (
        P("tok", "head"),
        P("tok"),
        P(None, "head"),
        P(None, "head"),
        P(None, "head"),
        P("head", None),
        P(None, "head"),
        P("head", None, None),
        P("head", None, None),
        P("head", None, None),
        P("head"),
    )
    return jax.shard_map(
        body, mesh=mesh, in_specs=placed, out_specs=P("tok", "head"), check_vma=False
    )
```

profile of v0, /device:TPU:1, one launch (start us, length us, event | category | flops | bytes accessed | tf_op | source)
XLA Modules:
  0.0 1371.5 jit_solution(8348761470947285355)
XLA Ops:
  6.6 5.1 all_gather.3
  13.7 9.6 collective-permute-start.16
  26.9 6.0 collective-permute-start.18
  37.9 4.2 collective-permute-start
  51.8 7.4 collective-permute-start.1
  59.9 4.2 collective-permute-start.2
  64.9 7.9 collective-permute-start.3
  73.6 6.4 collective-permute-start.4
  80.8 7.7 collective-permute-start.5
  92.7 5.6 collective-permute-start.7
  106.1 4.0 collective-permute-done.9
  111.4 7.1 collective-permute-done.10
  119.8 8.2 collective-permute-done.11
  129.3 6.2 collective-permute-done.12
  136.8 9.4 collective-permute-done.13
  147.4 8.4 collective-permute-done.14
  157.2 10.4 collective-permute-done.15
  167.6 4.0 collective-permute-start.20
  171.6 6.9 collective-permute-start.21
  193.9 11.6 collective-permute-start.32
  207.8 10.4 collective-permute-start.33
  220.2 12.5 collective-permute-start.34
  234.6 15.9 %collective-permute-start.35 = (bf16[128,384]{1,0:T(8,128)(2,1)}, bf16[128,384]{1,0:T(8,128)(2,1)S(1)}, u32[]{:S(2)}, u32[]{:S(2)}) collective-permute-start(bf16[128,384]{1,0:T(8,128)(2,1)} %convolution_convert_fusion), channel_id=1, source_target_pairs={{0,10},{2,12},{4,14},{6,16},{8,18},{10,20},{12,22},{14,24},{16,26}... | collective-permute-start | bytes 294920 | tf_op jit(solution)/shard_map/ppermute | solution.py:19
  252.4 9.8 collective-permute-start.36
  265.1 9.5 collective-permute-start.37
  276.6 5.6 collective-permute-start.38
  299.4 5.5 collective-permute-done.28
  306.2 10.4 collective-permute-done.29
  329.1 9.3 collective-permute-done.44
  353.7 5.3 while.17
  359.0 952.9 %all-reduce.2.cloned.1.call-done = f32[2,3,192,384]{3,2,0,1:T(8,128)} async-done(((f32[2,3,192,384]{3,2,0,1:T(8,128)}), f32[2,3,192,384]{3,2,0,1:T(8,128)}) %all-reduce.2.cloned.1.call-update) | async-done | bytes 1769488 | tf_op jit(solution)/shard_map/psum | solution.py:114
  1346.9 15.8 %reduce-scatter.2.cloned.1.call-done = f32[128,384]{1,0:T(8,128)} async-done(((f32[128,768]{1,0:T(8,128)}), f32[128,384]{1,0:T(8,128)}) %reduce-scatter.2.cloned.1.call-update) | async-done | bytes 196624 | tf_op jit(solution)/shard_map/reduce_scatter | solution.py:159
  (207 shorter events, 158.3 us)
Async XLA Ops:
  6.5 1305.4 %all-reduce.2.cloned.1.call-start = ((), (), s32[]{:S(2)}) async-start(), calls=%async_computation.1 | async-start | bytes 3538944 | tf_op jit(solution)/shard_map/psum | solution.py:114
  13.7 157.9 %collective-permute-start.16 = (bf16[128,384]{1,0:T(8,128)(2,1)}, bf16[128,384]{1,0:T(8,128)(2,1)}, u32[]{:S(2)}, u32[]{:S(2)}) collective-permute-start(bf16[128,384]{1,0:T(8,128)(2,1)} %convolution_convert_fusion.1), channel_id=1, source_target_pairs={{0,16},{2,18},{4,20},{6,22},{8,24},{10,26},{12,28},{14,30},{16,32}... | collective-permute-start | bytes 294920 | tf_op jit(solution)/shard_map/ppermute | solution.py:19
  23.3 156.1 %collective-permute-start.17 = (bf16[128,384]{1,0:T(8,128)(2,1)}, bf16[128,384]{1,0:T(8,128)(2,1)}, u32[]{:S(2)}, u32[]{:S(2)}) collective-permute-start(bf16[128,384]{1,0:T(8,128)(2,1)} %convolution_convert_fusion.1), channel_id=1, source_target_pairs={{0,14},{2,16},{4,18},{6,20},{8,22},{10,24},{12,26},{14,28},{16,30}... | collective-permute-start | bytes 294920 | tf_op jit(solution)/shard_map/ppermute | solution.py:19
  26.9 156.8 %collective-permute-start.18 = (bf16[128,384]{1,0:T(8,128)(2,1)}, bf16[128,384]{1,0:T(8,128)(2,1)}, u32[]{:S(2)}, u32[]{:S(2)}) collective-permute-start(bf16[128,384]{1,0:T(8,128)(2,1)} %convolution_convert_fusion.1), channel_id=1, source_target_pairs={{0,12},{2,14},{4,16},{6,18},{8,20},{10,22},{12,24},{14,26},{16,28}... | collective-permute-start | bytes 294920 | tf_op jit(solution)/shard_map/ppermute | solution.py:19
  32.9 153.6 %collective-permute-start.19 = (bf16[128,384]{1,0:T(8,128)(2,1)}, bf16[128,384]{1,0:T(8,128)(2,1)}, u32[]{:S(2)}, u32[]{:S(2)}) collective-permute-start(bf16[128,384]{1,0:T(8,128)(2,1)} %convolution_convert_fusion.1), channel_id=1, source_target_pairs={{0,10},{2,12},{4,14},{6,16},{8,18},{10,20},{12,22},{14,24},{16,26}... | collective-permute-start | bytes 294920 | tf_op jit(solution)/shard_map/ppermute | solution.py:19
  37.9 13.9 %collective-permute-start = (bf16[128]{0:T(256)(128)(2,1)}, bf16[128]{0:T(256)(128)(2,1)}, u32[]{:S(2)}, u32[]{:S(2)}) collective-permute-start(bf16[128]{0:T(256)(128)(2,1)} %get-tuple-element.87), channel_id=1, source_target_pairs={{0,16},{2,18},{4,20},{6,22},{8,24},{10,26},{12,28},{14,30},{16,32}... | collective-permute-start | bytes 776 | tf_op jit(solution)/shard_map/ppermute | solution.py:19
  49.8 1312.9 %reduce-scatter.2.cloned.1.call-start = ((), (), s32[]{:S(2)}) async-start(), calls=%async_computation.2 | async-start | bytes 589824 | tf_op jit(solution)/shard_map/reduce_scatter | solution.py:159
  135.5 10.7 collective-permute-start.13
  155.9 11.7 collective-permute-start.15
  167.6 22.3 %collective-permute-start.20 = (bf16[128,384]{1,0:T(8,128)(2,1)}, bf16[128,384]{1,0:T(8,128)(2,1)S(1)}, u32[]{:S(2)}, u32[]{:S(2)}) collective-permute-start(bf16[128,384]{1,0:T(8,128)(2,1)} %convolution_convert_fusion.1), channel_id=1, source_target_pairs={{0,8},{2,10},{4,12},{6,14},{8,16},{10,18},{12,20},{14,22},{16,24},... | collective-permute-start | bytes 294920 | tf_op jit(solution)/shard_map/ppermute | solution.py:19
  171.6 19.6 %collective-permute-start.21 = (bf16[128,384]{1,0:T(8,128)(2,1)}, bf16[128,384]{1,0:T(8,128)(2,1)S(1)}, u32[]{:S(2)}, u32[]{:S(2)}) collective-permute-start(bf16[128,384]{1,0:T(8,128)(2,1)} %convolution_convert_fusion.1), channel_id=1, source_target_pairs={{0,6},{2,8},{4,10},{6,12},{8,14},{10,16},{12,18},{14,20},{16,22},{... | collective-permute-start | bytes 294920 | tf_op jit(solution)/shard_map/ppermute | solution.py:19
  179.4 13.1 collective-permute-start.22
  186.6 106.9 %collective-permute-start.24 = (bf16[128,384]{1,0:T(8,128)(2,1)}, bf16[128,384]{1,0:T(8,128)(2,1)S(1)}, u32[]{:S(2)}, u32[]{:S(2)}) collective-permute-start(bf16[128,384]{1,0:T(8,128)(2,1)} %convolution_convert_fusion.1), channel_id=1, source_target_pairs={{2,0},{4,2},{6,4},{8,6},{10,8},{12,10},{14,12},{16,14},{18,16},{20... | collective-permute-start | bytes 294920 | tf_op jit(solution)/shard_map/ppermute | solution.py:19
  189.9 104.9 %collective-permute-start.25 = (bf16[128,384]{1,0:T(8,128)(2,1)}, bf16[128,384]{1,0:T(8,128)(2,1)S(1)}, u32[]{:S(2)}, u32[]{:S(2)}) collective-permute-start(bf16[128,384]{1,0:T(8,128)(2,1)} %convolution_convert_fusion.1), channel_id=1, source_target_pairs={{4,0},{6,2},{8,4},{10,6},{12,8},{14,10},{16,12},{18,14},{20,16},{2... | collective-permute-start | bytes 294920 | tf_op jit(solution)/shard_map/ppermute | solution.py:19
  191.2 104.9 %collective-permute-start.26 = (bf16[128,384]{1,0:T(8,128)(2,1)}, bf16[128,384]{1,0:T(8,128)(2,1)S(1)}, u32[]{:S(2)}, u32[]{:S(2)}) collective-permute-start(bf16[128,384]{1,0:T(8,128)(2,1)} %convolution_convert_fusion.1), channel_id=1, source_target_pairs={{6,0},{8,2},{10,4},{12,6},{14,8},{16,10},{18,12},{20,14},{22,16},{... | collective-permute-start | bytes 294920 | tf_op jit(solution)/shard_map/ppermute | solution.py:19
  192.6 104.9 %collective-permute-start.27 = (bf16[128,384]{1,0:T(8,128)(2,1)}, bf16[128,384]{1,0:T(8,128)(2,1)S(1)}, u32[]{:S(2)}, u32[]{:S(2)}) collective-permute-start(bf16[128,384]{1,0:T(8,128)(2,1)} %convolution_convert_fusion.1), channel_id=1, source_target_pairs={{8,0},{10,2},{12,4},{14,6},{16,8},{18,10},{20,12},{22,14},{24,16},... | collective-permute-start | bytes 294920 | tf_op jit(solution)/shard_map/ppermute | solution.py:19
  193.9 13.9 %collective-permute-start.32 = (bf16[128,384]{1,0:T(8,128)(2,1)}, bf16[128,384]{1,0:T(8,128)(2,1)S(1)}, u32[]{:S(2)}, u32[]{:S(2)}) collective-permute-start(bf16[128,384]{1,0:T(8,128)(2,1)} %convolution_convert_fusion), channel_id=1, source_target_pairs={{0,16},{2,18},{4,20},{6,22},{8,24},{10,26},{12,28},{14,30},{16,32}... | collective-permute-start | bytes 294920 | tf_op jit(solution)/shard_map/ppermute | solution.py:19
  207.8 12.4 collective-permute-start.33
  220.2 14.4 %collective-permute-start.34 = (bf16[128,384]{1,0:T(8,128)(2,1)}, bf16[128,384]{1,0:T(8,128)(2,1)S(1)}, u32[]{:S(2)}, u32[]{:S(2)}) collective-permute-start(bf16[128,384]{1,0:T(8,128)(2,1)} %convolution_convert_fusion), channel_id=1, source_target_pairs={{0,12},{2,14},{4,16},{6,18},{8,20},{10,22},{12,24},{14,26},{16,28}... | collective-permute-start | bytes 294920 | tf_op jit(solution)/shard_map/ppermute | solution.py:19
  234.6 17.8 %collective-permute-start.35 = (bf16[128,384]{1,0:T(8,128)(2,1)}, bf16[128,384]{1,0:T(8,128)(2,1)S(1)}, u32[]{:S(2)}, u32[]{:S(2)}) collective-permute-start(bf16[128,384]{1,0:T(8,128)(2,1)} %convolution_convert_fusion), channel_id=1, source_target_pairs={{0,10},{2,12},{4,14},{6,16},{8,18},{10,20},{12,22},{14,24},{16,26}... | collective-permute-start | bytes 294920 | tf_op jit(solution)/shard_map/ppermute | solution.py:19
  252.4 12.7 collective-permute-start.36
  265.1 11.5 collective-permute-start.37
  290.0 14.9 %collective-permute-start.28 = (bf16[128,384]{1,0:T(8,128)(2,1)}, bf16[128,384]{1,0:T(8,128)(2,1)S(1)}, u32[]{:S(2)}, u32[]{:S(2)}) collective-permute-start(bf16[128,384]{1,0:T(8,128)(2,1)} %convolution_convert_fusion.1), channel_id=1, source_target_pairs={{10,0},{12,2},{14,4},{16,6},{18,8},{20,10},{22,12},{24,14},{26,16}... | collective-permute-start | bytes 294920 | tf_op jit(solution)/shard_map/ppermute | solution.py:19
  293.5 23.2 %collective-permute-start.29 = (bf16[128,384]{1,0:T(8,128)(2,1)}, bf16[128,384]{1,0:T(8,128)(2,1)S(1)}, u32[]{:S(2)}, u32[]{:S(2)}) collective-permute-start(bf16[128,384]{1,0:T(8,128)(2,1)} %convolution_convert_fusion.1), channel_id=1, source_target_pairs={{12,0},{14,2},{16,4},{18,6},{20,8},{22,10},{24,12},{26,14},{28,16}... | collective-permute-start | bytes 294920 | tf_op jit(solution)/shard_map/ppermute | solution.py:19
  294.8 23.2 %collective-permute-start.30 = (bf16[128,384]{1,0:T(8,128)(2,1)}, bf16[128,384]{1,0:T(8,128)(2,1)S(1)}, u32[]{:S(2)}, u32[]{:S(2)}) collective-permute-start(bf16[128,384]{1,0:T(8,128)(2,1)} %convolution_convert_fusion.1), channel_id=1, source_target_pairs={{14,0},{16,2},{18,4},{20,6},{22,8},{24,10},{26,12},{28,14},{30,16}... | collective-permute-start | bytes 294920 | tf_op jit(solution)/shard_map/ppermute | solution.py:19
  296.1 23.2 %collective-permute-start.31 = (bf16[128,384]{1,0:T(8,128)(2,1)}, bf16[128,384]{1,0:T(8,128)(2,1)S(1)}, u32[]{:S(2)}, u32[]{:S(2)}) collective-permute-start(bf16[128,384]{1,0:T(8,128)(2,1)} %convolution_convert_fusion.1), channel_id=1, source_target_pairs={{16,0},{18,2},{20,4},{22,6},{24,8},{26,10},{28,12},{30,14},{32,16}... | collective-permute-start | bytes 294920 | tf_op jit(solution)/shard_map/ppermute | solution.py:19
  297.5 23.2 %collective-permute-start.40 = (bf16[128,384]{1,0:T(8,128)(2,1)}, bf16[128,384]{1,0:T(8,128)(2,1)S(1)}, u32[]{:S(2)}, u32[]{:S(2)}) collective-permute-start(bf16[128,384]{1,0:T(8,128)(2,1)} %convolution_convert_fusion), channel_id=1, source_target_pairs={{2,0},{4,2},{6,4},{8,6},{10,8},{12,10},{14,12},{16,14},{18,16},{20... | collective-permute-start | bytes 294920 | tf_op jit(solution)/shard_map/ppermute | solution.py:19
  304.9 17.7 %collective-permute-start.41 = (bf16[128,384]{1,0:T(8,128)(2,1)}, bf16[128,384]{1,0:T(8,128)(2,1)S(1)}, u32[]{:S(2)}, u32[]{:S(2)}) collective-permute-start(bf16[128,384]{1,0:T(8,128)(2,1)} %convolution_convert_fusion), channel_id=1, source_target_pairs={{4,0},{6,2},{8,4},{10,6},{12,8},{14,10},{16,12},{18,14},{20,16},{2... | collective-permute-start | bytes 294920 | tf_op jit(solution)/shard_map/ppermute | solution.py:19
  319.3 19.0 %collective-permute-start.44 = (bf16[128,384]{1,0:T(8,128)(2,1)}, bf16[128,384]{1,0:T(8,128)(2,1)S(1)}, u32[]{:S(2)}, u32[]{:S(2)}) collective-permute-start(bf16[128,384]{1,0:T(8,128)(2,1)} %convolution_convert_fusion), channel_id=1, source_target_pairs={{10,0},{12,2},{14,4},{16,6},{18,8},{20,10},{22,12},{24,14},{26,16}... | collective-permute-start | bytes 294920 | tf_op jit(solution)/shard_map/ppermute | solution.py:19
  320.7 24.6 %collective-permute-start.45 = (bf16[128,384]{1,0:T(8,128)(2,1)}, bf16[128,384]{1,0:T(8,128)(2,1)}, u32[]{:S(2)}, u32[]{:S(2)}) collective-permute-start(bf16[128,384]{1,0:T(8,128)(2,1)} %convolution_convert_fusion), channel_id=1, source_target_pairs={{12,0},{14,2},{16,4},{18,6},{20,8},{22,10},{24,12},{26,14},{28,16}... | collective-permute-start | bytes 294920 | tf_op jit(solution)/shard_map/ppermute | solution.py:19
  322.6 24.2 %collective-permute-start.46 = (bf16[128,384]{1,0:T(8,128)(2,1)}, bf16[128,384]{1,0:T(8,128)(2,1)}, u32[]{:S(2)}, u32[]{:S(2)}) collective-permute-start(bf16[128,384]{1,0:T(8,128)(2,1)} %convolution_convert_fusion), channel_id=1, source_target_pairs={{14,0},{16,2},{18,4},{20,6},{22,8},{24,10},{26,12},{28,14},{30,16}... | collective-permute-start | bytes 294920 | tf_op jit(solution)/shard_map/ppermute | solution.py:19
  325.4 23.0 %collective-permute-start.47 = (bf16[128,384]{1,0:T(8,128)(2,1)}, bf16[128,384]{1,0:T(8,128)(2,1)}, u32[]{:S(2)}, u32[]{:S(2)}) collective-permute-start(bf16[128,384]{1,0:T(8,128)(2,1)} %convolution_convert_fusion), channel_id=1, source_target_pairs={{16,0},{18,2},{20,4},{22,6},{24,8},{26,10},{28,12},{30,14},{32,16}... | collective-permute-start | bytes 294920 | tf_op jit(solution)/shard_map/ppermute | solution.py:19
  (34 other events, 1671.6 us)
Sparse Core Ops, SparseCore 0:
  49.9 1261.9 all-reduce.1
  1347.0 15.6 reduce-scatter.1
where the time goes:
time: 1380 us; the launch traced here: 1370 us
  waiting for transfers between devices  1070 us (78%)
  starting transfers between devices  196 us (14%)
  matrix products  41.8 us (3%)
  local copies, waits for them, and re-layouts  30.5 us (2%)
  between operations  15 us (1%)
    psum x1, waiting for transfers between devices, body(): total = lax.psum(terms, 'tok')  953 us
    ppermute x48, starting transfers between devices, passed_along(): lax.ppermute(value, axis, [(source, source + steps) for source in range(l...  196 us
    ppermute x48, waiting for transfers between devices, passed_along(): lax.ppermute(value, axis, [(source, source + steps) for source in range(l...  106 us
  transfers between devices with their start and end apart: 50, of which 31 were waited for; matrix products, arithmetic and copies ran while one was open for 3% of the time, Pallas kernels for 0%

commit v1 on v0

v1 whole, which is shorter than its diff:
```python
import jax
import jax.numpy as jnp
from jax import lax
from jax.experimental import pallas as pl
from jax.experimental.pallas import tpu as pltpu
from jax.sharding import Mesh, PartitionSpec as P

NS_STEPS = 5
newton_a = 3.4445
newton_b = -4.775
newton_c = 2.0315
epsilon = 1e-06
masked_score = -1e30

TOK = ("xh", "y", "z", "core")
CHIPS = ("xh", "y", "z")
REACH = 4
DH = 192
FH = 384
f32 = jnp.float32
bf16 = jnp.bfloat16


def normalize(values):
    widened = values.astype(f32)
    scale = lax.rsqrt(jnp.mean(widened * widened, axis=-1, keepdims=True) + epsilon)
    return (widened * scale).astype(bf16)


def halves(x):
    high = x.astype(bf16)
    return high, (x - high.astype(f32)).astype(bf16)


def nt(a, b):
    return lax.dot_general(a, b, (((1,), (1,)), ((), ())), preferred_element_type=f32)


def nn(a, b):
    return lax.dot_general(a, b, (((1,), (0,)), ((), ())), preferred_element_type=f32)


def tn(a, b):
    return lax.dot_general(a, b, (((0,), (0,)), ((), ())), preferred_element_type=f32)


def fresh_kernel(total_ref, master_ref, step_ref, fresh_ref):
    step = step_ref[0, 0]
    currents = []
    for m in range(3):
        matrix = total_ref[m]
        length = jnp.sqrt(jnp.sum(matrix * matrix))
        currents.append(matrix / (length + epsilon))
    for _ in range(NS_STEPS):
        squares = []
        for x in currents:
            h, l = halves(x)
            squares.append((h, l, nt(h, h) + (nt(h, l) + nt(l, h))))
        mixers = []
        for h, l, a in squares:
            ah, al = halves(a)
            aa = nn(ah, ah) + (nn(ah, al) + nn(al, ah))
            mixers.append((h, l, newton_b * a + newton_c * aa))
        nexts = []
        for x, (h, l, b) in zip(currents, mixers):
            bh, bl = halves(b)
            nexts.append(newton_a * x + (nn(bh, h) + (nn(bh, l) + nn(bl, h))))
        currents = nexts
    for m in range(3):
        fresh_ref[m] = (master_ref[m] - step * currents[m]).astype(bf16)


def make_fresh(total, master, step):
    return pl.pallas_call(
        fresh_kernel,
        out_shape=jax.ShapeDtypeStruct((3, DH, FH), bf16),
        in_specs=[
            pl.BlockSpec(memory_space=pltpu.VMEM),
            pl.BlockSpec(memory_space=pltpu.VMEM),
            pl.BlockSpec(memory_space=pltpu.SMEM),
        ],
        out_specs=pl.BlockSpec(memory_space=pltpu.VMEM),
        name="fresh",
    )(total, master, step)


def hop(x, steps):
    return lax.ppermute(
        x, CHIPS, [(i, i + steps) for i in range(64) if 0 <= i + steps < 64]
    )


def body(
    tokens,
    view_ids,
    query_weight,
    key_weight,
    value_weight,
    out_weight,
    rate_weight,
    fast_gate,
    fast_up,
    fast_down,
    step_size,
):
    core = lax.axis_index("core")
    xl = lax.axis_index("xl")
    chip = (lax.axis_index("xh") * 4 + lax.axis_index("y")) * 8 + lax.axis_index("z")
    whole = lax.all_gather(tokens, ("xl", "core"), axis=0, tiled=True)
    features = jnp.concatenate((whole[:256], whole[256:]), 1)
    views = lax.all_gather(view_ids, "core", axis=0, tiled=True)

    def own_columns(w):
        return jnp.where(core == 0, w[:, :DH], w[:, DH:])

    def own(w):
        return lax.dynamic_index_in_dim(w, core, 0, keepdims=False)

    query = nn(features, own_columns(query_weight)).astype(bf16)
    key = nn(features, own_columns(key_weight)).astype(bf16)
    value = nn(features, own_columns(value_weight)).astype(bf16)
    rates = jax.nn.softplus(nn(features, rate_weight))
    rates = jnp.where(core == 0, rates[:, :1], rates[:, 1:])
    rates = rates * (chip < 48).astype(f32)

    tag = (views + 1).astype(bf16)
    tag_rows = jnp.zeros((16, 2 * DH), bf16).at[0, :256].set(tag)
    packed = jnp.concatenate((jnp.concatenate((key, value), 1), tag_rows), 0)
    pieces = [packed]
    ahead = behind = packed
    for _ in range(REACH):
        ahead, behind = hop(ahead, 1), hop(behind, -1)
        pieces += [ahead, behind]

    master = jnp.stack((own(fast_gate), own(fast_up), own(fast_down)), 0)
    lowered = master.astype(bf16)
    keys_n = normalize(key)
    gate = nn(keys_n, lowered[0])
    upward = nn(keys_n, lowered[1])
    logistic = jax.nn.sigmoid(gate)
    active = gate * logistic
    product = (active * upward).astype(bf16)
    error = (-rates * value.astype(f32)).astype(bf16)
    back = nn(error, lowered[2])
    grad_g = (back * upward * logistic * (1.0 + gate * (1.0 - logistic))).astype(bf16)
    grad_u = (back * active).astype(bf16)
    terms = jnp.concatenate((tn(keys_n, grad_g), tn(keys_n, grad_u), tn(error, product)), 0)

    sent = terms.reshape(8, 72, FH).astype(bf16)
    got = lax.all_to_all(sent, ("xh", "y"), 0, 0, tiled=True)
    part = jnp.sum(got.astype(f32), 0).astype(bf16)
    got = lax.all_to_all(jnp.broadcast_to(part[None], (8, 72, FH)), "z", 0, 0, tiled=True)
    part = jnp.sum(got.astype(f32), 0).astype(bf16)
    got = lax.all_to_all(
        jnp.broadcast_to(part[None], (8, 72, FH)), ("xh", "y"), 0, 0, tiled=True
    )
    total = got.astype(f32).reshape(3, DH, FH)
    fresh = make_fresh(total, master, own(step_size).reshape(1, 1))

    near = jnp.concatenate([p[:256] for p in pieces], 0)
    near_views = jnp.concatenate([p[256, :256] for p in pieces], 0)
    scores = nt(query, near[:, :DH]) * DH**-0.5
    scores = jnp.where(tag[:, None] == near_views[None, :], scores, masked_score)
    weights = jnp.exp(scores - jnp.max(scores, axis=-1, keepdims=True))
    weights = (weights / jnp.sum(weights, axis=-1, keepdims=True)).astype(bf16)
    attended = nn(weights, near[:, DH:])

    queries_n = normalize(query)
    gate = nn(queries_n, fresh[0])
    upward = nn(queries_n, fresh[1])
    applied = nt((jax.nn.silu(gate) * upward).astype(bf16), fresh[2])
    mixed = (attended + applied).astype(bf16)

    mine = lax.dynamic_slice_in_dim(out_weight, xl * FH, FH, 1)
    theirs = lax.dynamic_slice_in_dim(out_weight, (1 - xl) * FH, FH, 1)
    other = lax.ppermute(theirs, "xl", [(0, 1), (1, 0)])
    upper = jnp.where(xl == 0, mine, other)
    lower = jnp.where(xl == 0, other, mine)
    out_columns = jnp.concatenate((upper, lower), 0)

    spread = lax.all_gather(mixed, ("xl", "core"), axis=0)
    spread = lax.dynamic_slice_in_dim(spread, core * 128, 128, 1)
    side = jnp.concatenate([spread[h] for h in range(4)], 1)
    return nn(side, out_columns).astype(bf16)


def solution(mesh):
    fine = Mesh(mesh.devices.reshape(2, 4, 8, 2, 2), ("xh", "y", "z", "core", "xl"))
    placed = (
        P(TOK, "xl"),
        P(TOK),
        P(None, "xl"),
        P(None, "xl"),
        P(None, "xl"),
        P("xl", None),
        P(None, "xl"),
        P("xl", None, None),
        P("xl", None, None),
        P("xl", None, None),
        P("xl"),
    )
    return jax.shard_map(
        body, mesh=fine, in_specs=placed, out_specs=P(TOK, "xl"), check_vma=False
    )
```

time: 1380 us -> 138 us (0.10)
  waiting for transfers between devices: 1070 us -> 18.7 us
  starting transfers between devices: 196 us -> 49 us
  matrix products: 41.8 us -> 13.9 us
  blocking collectives: 5.1 us -> 22 us
  between operations: 15 us -> 0.51 us
  local copies, waits for them, and re-layouts: 30.5 us -> 16.7 us
    psum x1 -> x0, waiting for transfers between devices: 953 us -> none  [body(): total = lax.psum(terms, 'tok')]
    ppermute x48 -> x9, starting transfers between devices: 196 us -> 18.7 us  [the longest x8 17.8 us: hop(): lax.ppermute(x, CHIPS, [(i, i + steps) for i in range(64) if 0 <= i + ste...]
    ppermute x48 -> x9, waiting for transfers between devices: 106 us -> 12.8 us  [the longest x8 12.8 us: hop(): lax.ppermute(x, CHIPS, [(i, i + steps) for i in range(64) if 0 <= i + ste...]
    all_to_all x0 -> x3, starting transfers between devices: none -> 30.3 us  [the longest x1 10.9 us: body(): lax.all_to_all(jnp.broadcast_to(part[None], (8, 72, FH)), ('xh', 'y'), 0,...]
    dot_general x32 -> x15, matrix products: 41.8 us -> 13.9 us  [the longest x10 9.01 us: nn(): lax.dot_general(a, b, (((1,), (0,)), ((), ())), preferred_element_type=f32)]
    all_gather x1 -> x3, blocking collectives: 5.1 us -> 22 us  [the longest x1 10.7 us: body(): spread = lax.all_gather(mixed, ('xl', 'core'), axis=0)]
    reduce_scatter x1 -> x0, waiting for transfers between devices: 15.8 us -> none  [body(): lax.psum_scatter(partial_value, 'head', scatter_dimension=1, tiled=True)]
  transfers between devices with their start and end apart: 50 -> 12, of which waited for: 31 -> 4; matrix products, arithmetic and copies ran while one was open for 3% -> 18% of each run, Pallas kernels for 0% -> 0%
where the time goes in v1:
time: 138 us; the launch traced here: 137 us
  starting transfers between devices  49 us (36%)
  blocking collectives  22 us (16%)
  waiting for transfers between devices  18.7 us (14%)
  local copies, waits for them, and re-layouts  16.7 us (12%)
  matrix products  13.9 us (10%)
  Pallas kernels  9.55 us (7%)
  other arithmetic  7.02 us (5%)
    ppermute x8, starting transfers between devices, hop(): lax.ppermute(x, CHIPS, [(i, i + steps) for i in range(64) if 0 <= i + ste...  17.8 us
    ppermute x8, waiting for transfers between devices, hop(): lax.ppermute(x, CHIPS, [(i, i + steps) for i in range(64) if 0 <= i + ste...  12.8 us
    all_to_all x1, starting transfers between devices, body(): lax.all_to_all(jnp.broadcast_to(part[None], (8, 72, FH)), ('xh', 'y'), 0,...  10.9 us
    all_to_all x1, starting transfers between devices, body(): got = lax.all_to_all(sent, ('xh', 'y'), 0, 0, tiled=True)  10.9 us
    all_gather x1, blocking collectives, body(): spread = lax.all_gather(mixed, ('xl', 'core'), axis=0)  10.7 us
    pallas_call x1, Pallas kernels, make_fresh(): pl.pallas_call(fresh_kernel, out_shape=jax.ShapeDtypeStruct((3, DH, FH),...  9.55 us
    all_gather x1, blocking collectives, body(): whole = lax.all_gather(tokens, ('xl', 'core'), axis=0, tiled=True)  9.5 us
    unnamed x51, local copies, waits for them, and re-layouts  9.35 us
  transfers between devices with their start and end apart: 12, of which 4 were waited for; matrix products, arithmetic and copies ran while one was open for 18% of the time, Pallas kernels for 0%

profile of v1, /device:TPU:1, one launch (start us, length us, event | category | flops | bytes accessed | tf_op | source)
XLA Modules:
  0.0 137.3 jit_solution(10782715200827526675)
XLA Ops:
  0.0 9.5 %all_gather.13 = bf16[512,384]{1,0:T(8,128)(2,1)S(1)} all-gather(bf16[128,384]{1,0:T(8,128)(2,1)} %param.13), channel_id=1, replica_groups=mesh['xh'=2,'y'=4,'z'=8,'core'=2,'xl'=2] {'xl','core'}, dimensions={0}, use_global_device_ids=true | all-gather | bytes 491520 | tf_op jit(solution)/shard_map/all_gather | solution.py:109
  9.6 1.7 %fusion.36 = (f32[256]{0:T(256)S(1)}, bf16[256,192]{0,1:T(8,128)(2,1)S(1)}) fusion(bf16[768,384]{1,0:T(8,128)(2,1)} %param.16, pred[]{:T(512)S(6)} %eq.11, bf16[256,384]{1,0:T(8,128)(2,1)S(1)} %get-tuple-element.24, bf16[256,384]{1,0:T(8,128)(2,1)S(1)} %get-tuple-element.23), kind=kOutput, calls=%fused_computation.62 | convolution fusion | flops 76627712 | bytes 1278977 | tf_op jit(solution)/shard_map/dot_general | solution.py:40
  12.0 1.8 %all-gather.1 = s32[2,1,128]{2,1,0:T(1,128)S(1)} all-gather(s32[1,1,128]{2,1,0:T(1,128)S(1)} %bitcast.55), channel_id=1, replica_groups=mesh['xh'=2,'y'=4,'z'=8,'core'=2,'xl'=2] {'core'}, dimensions={0}, use_global_device_ids=true | all-gather | bytes 1536 | tf_op jit(solution)/shard_map/all_gather | solution.py:111
  14.7 2.9 %collective-permute-start = (bf16[272,384]{0,1:T(8,128)(2,1)}, bf16[272,384]{0,1:T(8,128)(2,1)}, u32[]{:S(2)}, u32[]{:S(2)}) collective-permute-start(bf16[272,384]{0,1:T(8,128)(2,1)} %fusion.33), channel_id=1, source_target_pairs={{0,4},{4,8},{8,12},{12,16},{16,20},{20,24},{24,28},{28,32},{32,36}... | collective-permute-start | bytes 626696 | tf_op jit(solution)/shard_map/ppermute | solution.py:88
  17.6 1.3 collective-permute-start.1
  24.0 10.9 %all-to-all-start = ((bf16[8,72,384]{2,1,0:T(8,128)(2,1)}), bf16[8,72,384]{2,1,0:T(8,128)(2,1)S(1)}, u32[]{:S(2)}, u32[]{:S(2)}) async-start(bf16[8,72,384]{2,1,0:T(8,128)(2,1)} %bitcast.6), calls=%async_computation | async-start | bytes 884736 | tf_op jit(solution)/shard_map/all_to_all | solution.py:150
  35.5 1.6 %fusion.34 = (f32[256]{0:T(256)S(1)}, bf16[256,192]{0,1:T(8,128)(2,1)S(1)}) fusion(bf16[768,384]{1,0:T(8,128)(2,1)} %param.15, pred[]{:T(512)S(6)} %eq.11, bf16[256,384]{1,0:T(8,128)(2,1)S(1)} %copy-done.9, bf16[256,384]{1,0:T(8,128)(2,1)S(1)} %copy-done.6), kind=kOutput, calls=%fused_computation.60 | convolution fusion | flops 76627712 | bytes 1278977 | tf_op jit(solution)/shard_map/dot_general | solution.py:40
  37.3 1.0 pad_maximum_fusion.master_ref
  39.0 0.9 slice_reduce_fusion.7
  40.2 0.9 slice_reduce_fusion.6
  41.4 1.3 collective-permute-start.2
  42.7 1.3 collective-permute-start.3
  44.0 1.6 %slice_dynamic-update-slice_fusion.7 = bf16[2304,384]{0,1:T(8,128)(2,1)} fusion(bf16[2304,384]{0,1:T(8,128)(2,1)} %maximum_dynamic-update-slice_fusion, bf16[272,384]{0,1:T(8,128)(2,1)} %collective-permute-done), kind=kLoop, calls=%fused_computation.71 | loop fusion | bytes 393216
  45.7 1.7 %slice_dynamic-update-slice_fusion.6 = bf16[2304,384]{0,1:T(8,128)(2,1)} fusion(bf16[2304,384]{0,1:T(8,128)(2,1)} %slice_dynamic-update-slice_fusion.7, bf16[272,384]{0,1:T(8,128)(2,1)} %collective-permute-done.1), kind=kLoop, calls=%fused_computation.70 | loop fusion | bytes 393216
  47.4 1.9 %broadcast_select_fusion.1 = (bf16[384,384]{1,0:T(8,128)(2,1)}, bf16[384,384]{1,0:T(8,128)(2,1)}) fusion(bf16[384,384]{1,0:T(8,128)(2,1)} %collective-permute-done.8, pred[]{:T(512)S(6)} %eq.27, bf16[384,768]{1,0:T(8,128)(2,1)S(1)} %copy-done.1, s32[]{:T(128)S(6)} %select_n.72), kind=kLoop, calls=%fused_computation.55 | loop fusion | flops 294912 | bytes 1179653 | tf_op jit(solution)/shard_map/jit(_where)/select_n | solution.py:177
  50.2 8.5 %all-to-all-start.1 = ((bf16[8,72,384]{2,1,0:T(8,128)(2,1)}), bf16[8,72,384]{2,1,0:T(8,128)(2,1)S(1)}, u32[]{:S(2)}, u32[]{:S(2)}) async-start(bf16[8,72,384]{2,1,0:T(8,128)(2,1)} %broadcast_in_dim.8), calls=%async_computation.1 | async-start | bytes 884736 | tf_op jit(solution)/shard_map/all_to_all | solution.py:152
  59.4 3.4 %collective-permute-start.4 = (bf16[272,384]{0,1:T(8,128)(2,1)S(1)}, bf16[272,384]{0,1:T(8,128)(2,1)S(1)}, u32[]{:S(2)}, u32[]{:S(2)}) collective-permute-start(bf16[272,384]{0,1:T(8,128)(2,1)S(1)} %collective-permute-done.2), channel_id=1, source_target_pairs={{0,4},{4,8},{8,12},{12,16},{16,20},{20,24},{24,28},{28,32},{32,36}... | collective-permute-start | bytes 626696 | tf_op jit(solution)/shard_map/ppermute | solution.py:88
  62.8 1.3 collective-permute-start.5
  65.5 7.1 %collective-permute-done.4 = bf16[272,384]{0,1:T(8,128)(2,1)S(1)} collective-permute-done((bf16[272,384]{0,1:T(8,128)(2,1)S(1)}, bf16[272,384]{0,1:T(8,128)(2,1)S(1)}, u32[]{:S(2)}, u32[]{:S(2)}) %collective-permute-start.4) | collective-permute-done | bytes 208928 | tf_op jit(solution)/shard_map/ppermute | solution.py:88
  72.5 5.1 %collective-permute-start.6 = (bf16[272,384]{0,1:T(8,128)(2,1)S(1)}, bf16[272,384]{0,1:T(8,128)(2,1)S(1)}, u32[]{:S(2)}, u32[]{:S(2)}) collective-permute-start(bf16[272,384]{0,1:T(8,128)(2,1)S(1)} %collective-permute-done.4), channel_id=1, source_target_pairs={{0,4},{4,8},{8,12},{12,16},{16,20},{20,24},{24,28},{28,32},{32,36}... | collective-permute-start | bytes 626696 | tf_op jit(solution)/shard_map/ppermute | solution.py:88
  77.6 1.3 collective-permute-start.7
  82.2 5.0 %collective-permute-done.7 = bf16[272,384]{0,1:T(8,128)(2,1)S(1)} collective-permute-done((bf16[272,384]{0,1:T(8,128)(2,1)S(1)}, bf16[272,384]{0,1:T(8,128)(2,1)S(1)}, u32[]{:S(2)}, u32[]{:S(2)}) %collective-permute-start.7) | collective-permute-done | bytes 208928 | tf_op jit(solution)/shard_map/ppermute | solution.py:88
  89.6 10.9 %all-to-all-start.2 = ((bf16[8,72,384]{2,1,0:T(8,128)(2,1)}), bf16[8,72,384]{2,1,0:T(8,128)(2,1)S(1)}, u32[]{:S(2)}, u32[]{:S(2)}) async-start(bf16[8,72,384]{2,1,0:T(8,128)(2,1)} %broadcast_in_dim.9), calls=%async_computation.2 | async-start | bytes 884736 | tf_op jit(solution)/shard_map/all_to_all | solution.py:154
  100.6 1.8 %fusion = (f32[256]{0:T(256)S(1)}, f32[256,2304]{1,0:T(8,128)S(1)}) fusion(bf16[2304]{0:T(1024)(128)(2,1)S(1)} %constant_dynamic-update-slice_fusion, bf16[256]{0:T(256)(128)(2,1)S(1)} %bitcast.52, bf16[256,192]{0,1:T(8,128)(2,1)S(1)} %get-tuple-element.28, bf16[2304,384]{0,1:T(8,128)(2,1)} %slice_dynamic-update-slice_fusion), kind=kOutput, calls=%fused_computation.4 | convolution fusion | flops 228851456 | bytes 3348480 | tf_op jit(solution)/shard_map/dot_general | solution.py:36
  103.0 5.9 %all-to-all-done.2 = bf16[8,72,384]{2,1,0:T(8,128)(2,1)S(1)} async-done(((bf16[8,72,384]{2,1,0:T(8,128)(2,1)}), bf16[8,72,384]{2,1,0:T(8,128)(2,1)S(1)}, u32[]{:S(2)}, u32[]{:S(2)}) %all-to-all-start.2) | async-done | bytes 442400 | tf_op jit(solution)/shard_map/all_to_all | solution.py:154
  108.9 1.0 convert.15.total_ref
  109.9 9.6 %fresh.1 = bf16[3,192,384]{2,1,0:T(8,128)(2,1)} custom-call(f32[3,192,384]{2,1,0:T(8,128)} %convert.15.total_ref, f32[3,192,384]{2,1,0:T(8,128)} %pad_maximum_fusion.master_ref, f32[1,1]{1,0:T(1,128)} %bitcast.8.step_ref), custom_call_target="tpu_custom_call" | custom-call | tf_op jit(solution)/shard_map/fresh/pallas_call | solution.py:74
  119.5 1.2 fusion.46
  120.6 2.1 %fusion.4 = f32[256,192]{0,1:T(8,128)} fusion(f32[256,384]{1,0:T(8,128)S(1)} %fusion.46, bf16[3,192,384]{2,1,0:T(8,128)(2,1)} %fresh.1, bf16[256,192]{0,1:T(8,128)(2,1)S(1)} %get-tuple-element.28, f32[256]{0:T(256)S(1)} %add_rsqrt_fusion.1), kind=kOutput, calls=%fused_computation.12 | convolution fusion | flops 76234752 | bytes 984064 | tf_op jit(solution)/shard_map/dot_general | solution.py:36
  122.7 2.0 %fusion.6 = bf16[256,192]{0,1:T(8,128)(2,1)S(1)} fusion(f32[256,192]{0,1:T(8,128)} %fusion.4, f32[256,2304]{1,0:T(8,128)S(1)} %get-tuple-element.30, f32[256]{0:T(256)S(1)} %fusion.1, f32[256]{0:T(256)S(1)} %get-tuple-element.29, bf16[2304,384]{0,1:T(8,128)(2,1)} %slice_dynamic-update-slice_fusion, ...), kind=kOutput, calls=%fused_computation.18 | convolution fusion | flops 229539840 | bytes 3546112 | tf_op jit(solution)/shard_map/dot_general | solution.py:40
  124.8 10.7 %all-gather = bf16[1024,192]{0,1:T(8,128)(2,1)S(1)} all-gather(bf16[256,192]{0,1:T(8,128)(2,1)S(1)} %fusion.6), channel_id=2, replica_groups=mesh['xh'=2,'y'=4,'z'=8,'core'=2,'xl'=2] {'xl','core'}, dimensions={0}, use_global_device_ids=true | all-gather | bytes 491520 | tf_op jit(solution)/shard_map/all_gather | solution.py:181
  136.4 1.0 convolution_convert_fusion.3
  (98 shorter events, 18.8 us)
Async XLA Ops:
  0.0 20.5 %copy-start = (f32[2,192,384]{2,1,0:T(8,128)S(1)}, f32[2,192,384]{2,1,0:T(8,128)}, u32[]{:S(2)}) copy-start(f32[2,192,384]{2,1,0:T(8,128)} %param.20) | copy-start | bytes 1769476
  9.6 2.4 %copy-start.4 = (bf16[256,384]{1,0:T(8,128)(2,1)}, bf16[256,384]{1,0:T(8,128)(2,1)S(1)}, u32[]{:S(2)}) copy-start(bf16[256,384]{1,0:T(8,128)(2,1)S(1)} %get-tuple-element.23) | copy-start | bytes 589828
  9.6 2.4 %copy-start.7 = (bf16[256,384]{1,0:T(8,128)(2,1)}, bf16[256,384]{1,0:T(8,128)(2,1)S(1)}, u32[]{:S(2)}) copy-start(bf16[256,384]{1,0:T(8,128)(2,1)S(1)} %get-tuple-element.24) | copy-start | bytes 589828
  9.6 1.8 %copy-start.12 = (bf16[768,384]{1,0:T(8,128)(2,1)S(1)}, bf16[768,384]{1,0:T(8,128)(2,1)}, u32[]{:S(2)}) copy-start(bf16[768,384]{1,0:T(8,128)(2,1)} %param.17) | copy-start | bytes 1769476
  9.6 2.4 %copy-start.14 = (s32[128]{0:T(128)S(1)}, s32[128]{0:T(128)}, u32[]{:S(2)}) copy-start(s32[128]{0:T(128)} %param.14) | copy-start | bytes 1540
  9.6 9.3 %copy-start.1 = (bf16[384,768]{1,0:T(8,128)(2,1)S(1)}, bf16[384,768]{1,0:T(8,128)(2,1)}, u32[]{:S(2)}) copy-start(bf16[384,768]{1,0:T(8,128)(2,1)} %param.18) | copy-start | bytes 1769476
  11.4 9.2 %copy-start.10 = (f32[2,192,384]{2,1,0:T(8,128)S(1)}, f32[2,192,384]{2,1,0:T(8,128)}, u32[]{:S(2)}) copy-start(f32[2,192,384]{2,1,0:T(8,128)} %param.22) | copy-start | bytes 1769476
  11.4 9.2 %copy-start.11 = (f32[2,192,384]{2,1,0:T(8,128)S(1)}, f32[2,192,384]{2,1,0:T(8,128)}, u32[]{:S(2)}) copy-start(f32[2,192,384]{2,1,0:T(8,128)} %param.21) | copy-start | bytes 1769476
  14.7 24.3 %collective-permute-start = (bf16[272,384]{0,1:T(8,128)(2,1)}, bf16[272,384]{0,1:T(8,128)(2,1)}, u32[]{:S(2)}, u32[]{:S(2)}) collective-permute-start(bf16[272,384]{0,1:T(8,128)(2,1)} %fusion.33), channel_id=1, source_target_pairs={{0,4},{4,8},{8,12},{12,16},{16,20},{20,24},{24,28},{28,32},{32,36}... | collective-permute-start | bytes 626696 | tf_op jit(solution)/shard_map/ppermute | solution.py:88
  17.6 22.7 %collective-permute-start.1 = (bf16[272,384]{0,1:T(8,128)(2,1)}, bf16[272,384]{0,1:T(8,128)(2,1)}, u32[]{:S(2)}, u32[]{:S(2)}) collective-permute-start(bf16[272,384]{0,1:T(8,128)(2,1)} %fusion.33), channel_id=1, source_target_pairs={{4,0},{8,4},{12,8},{16,12},{20,16},{24,20},{28,24},{32,28},{36,32}... | collective-permute-start | bytes 626696 | tf_op jit(solution)/shard_map/ppermute | solution.py:88
  19.6 27.7 %collective-permute-start.8 = (bf16[384,384]{1,0:T(8,128)(2,1)}, bf16[384,384]{1,0:T(8,128)(2,1)}, u32[]{:S(2)}, u32[]{:S(2)}) collective-permute-start(bf16[384,384]{1,0:T(8,128)(2,1)} %constant_dynamic-slice_fusion.3), channel_id=1, source_target_pairs={{0,1},{1,0},{2,3},{3,2},{4,5},{5,4},{6,7},{7,6},{8,9},{9,8},{10,11... | collective-permute-start | bytes 884744 | tf_op jit(solution)/shard_map/ppermute | solution.py:176
  20.6 0.9 copy-start.5
  20.6 1.0 copy-start.8
  20.6 1.0 copy-start.13
  22.8 12.1 %copy-start.15 = (f32[2]{0:T(128)S(1)}, f32[2]{0:T(128)}, u32[]{:S(2)}) copy-start(f32[2]{0:T(128)} %param.23) | copy-start | bytes 28
  23.1 12.3 %copy-start.6 = (bf16[256,384]{1,0:T(8,128)(2,1)S(1)}, bf16[256,384]{1,0:T(8,128)(2,1)}, u32[]{:S(2)}) copy-start(bf16[256,384]{1,0:T(8,128)(2,1)} %copy-done.4) | copy-start | bytes 589828
  23.1 12.3 %copy-start.9 = (bf16[256,384]{1,0:T(8,128)(2,1)S(1)}, bf16[256,384]{1,0:T(8,128)(2,1)}, u32[]{:S(2)}) copy-start(bf16[256,384]{1,0:T(8,128)(2,1)} %copy-done.7) | copy-start | bytes 589828
  24.0 25.3 %all-to-all-start = ((bf16[8,72,384]{2,1,0:T(8,128)(2,1)}), bf16[8,72,384]{2,1,0:T(8,128)(2,1)S(1)}, u32[]{:S(2)}, u32[]{:S(2)}) async-start(bf16[8,72,384]{2,1,0:T(8,128)(2,1)} %bitcast.6), calls=%async_computation | async-start | bytes 884736 | tf_op jit(solution)/shard_map/all_to_all | solution.py:150
  41.4 17.2 %collective-permute-start.2 = (bf16[272,384]{0,1:T(8,128)(2,1)}, bf16[272,384]{0,1:T(8,128)(2,1)S(1)}, u32[]{:S(2)}, u32[]{:S(2)}) collective-permute-start(bf16[272,384]{0,1:T(8,128)(2,1)} %collective-permute-done), channel_id=1, source_target_pairs={{0,4},{4,8},{8,12},{12,16},{16,20},{20,24},{24,28},{28,32},{32,36}... | collective-permute-start | bytes 626696 | tf_op jit(solution)/shard_map/ppermute | solution.py:88
  42.7 16.3 %collective-permute-start.3 = (bf16[272,384]{0,1:T(8,128)(2,1)}, bf16[272,384]{0,1:T(8,128)(2,1)S(1)}, u32[]{:S(2)}, u32[]{:S(2)}) collective-permute-start(bf16[272,384]{0,1:T(8,128)(2,1)} %collective-permute-done.1), channel_id=1, source_target_pairs={{4,0},{8,4},{12,8},{16,12},{20,16},{24,20},{28,24},{32,28},{36,32}... | collective-permute-start | bytes 626696 | tf_op jit(solution)/shard_map/ppermute | solution.py:88
  50.2 38.6 %all-to-all-start.1 = ((bf16[8,72,384]{2,1,0:T(8,128)(2,1)}), bf16[8,72,384]{2,1,0:T(8,128)(2,1)S(1)}, u32[]{:S(2)}, u32[]{:S(2)}) async-start(bf16[8,72,384]{2,1,0:T(8,128)(2,1)} %broadcast_in_dim.8), calls=%async_computation.1 | async-start | bytes 884736 | tf_op jit(solution)/shard_map/all_to_all | solution.py:152
  59.4 13.2 %collective-permute-start.4 = (bf16[272,384]{0,1:T(8,128)(2,1)S(1)}, bf16[272,384]{0,1:T(8,128)(2,1)S(1)}, u32[]{:S(2)}, u32[]{:S(2)}) collective-permute-start(bf16[272,384]{0,1:T(8,128)(2,1)S(1)} %collective-permute-done.2), channel_id=1, source_target_pairs={{0,4},{4,8},{8,12},{12,16},{16,20},{20,24},{24,28},{28,32},{32,36}... | collective-permute-start | bytes 626696 | tf_op jit(solution)/shard_map/ppermute | solution.py:88
  62.8 14.9 %collective-permute-start.5 = (bf16[272,384]{0,1:T(8,128)(2,1)S(1)}, bf16[272,384]{0,1:T(8,128)(2,1)S(1)}, u32[]{:S(2)}, u32[]{:S(2)}) collective-permute-start(bf16[272,384]{0,1:T(8,128)(2,1)S(1)} %collective-permute-done.3), channel_id=1, source_target_pairs={{4,0},{8,4},{12,8},{16,12},{20,16},{24,20},{28,24},{32,28},{36,32}... | collective-permute-start | bytes 626696 | tf_op jit(solution)/shard_map/ppermute | solution.py:88
  72.5 9.3 %collective-permute-start.6 = (bf16[272,384]{0,1:T(8,128)(2,1)S(1)}, bf16[272,384]{0,1:T(8,128)(2,1)S(1)}, u32[]{:S(2)}, u32[]{:S(2)}) collective-permute-start(bf16[272,384]{0,1:T(8,128)(2,1)S(1)} %collective-permute-done.4), channel_id=1, source_target_pairs={{0,4},{4,8},{8,12},{12,16},{16,20},{20,24},{24,28},{28,32},{32,36}... | collective-permute-start | bytes 626696 | tf_op jit(solution)/shard_map/ppermute | solution.py:88
  77.6 9.5 %collective-permute-start.7 = (bf16[272,384]{0,1:T(8,128)(2,1)S(1)}, bf16[272,384]{0,1:T(8,128)(2,1)S(1)}, u32[]{:S(2)}, u32[]{:S(2)}) collective-permute-start(bf16[272,384]{0,1:T(8,128)(2,1)S(1)} %collective-permute-done.5), channel_id=1, source_target_pairs={{4,0},{8,4},{12,8},{16,12},{20,16},{24,20},{28,24},{32,28},{36,32}... | collective-permute-start | bytes 626696 | tf_op jit(solution)/shard_map/ppermute | solution.py:88
  89.6 19.3 %all-to-all-start.2 = ((bf16[8,72,384]{2,1,0:T(8,128)(2,1)}), bf16[8,72,384]{2,1,0:T(8,128)(2,1)S(1)}, u32[]{:S(2)}, u32[]{:S(2)}) async-start(bf16[8,72,384]{2,1,0:T(8,128)(2,1)} %broadcast_in_dim.9), calls=%async_computation.2 | async-start | bytes 884736 | tf_op jit(solution)/shard_map/all_to_all | solution.py:154
  124.7 11.6 %copy-start.2 = (bf16[384,384]{1,0:T(8,128)(2,1)S(1)}, bf16[384,384]{1,0:T(8,128)(2,1)}, u32[]{:S(2)}) copy-start(bf16[384,384]{1,0:T(8,128)(2,1)} %get-tuple-element.17) | copy-start | bytes 884740
  124.8 11.6 %copy-start.3 = (bf16[384,384]{1,0:T(8,128)(2,1)S(1)}, bf16[384,384]{1,0:T(8,128)(2,1)}, u32[]{:S(2)}) copy-start(bf16[384,384]{1,0:T(8,128)(2,1)} %get-tuple-element.18) | copy-start | bytes 884740

commit v2 on v1

v2 whole, which is shorter than its diff:
```python
import jax
import jax.numpy as jnp
from jax import lax
from jax.experimental import pallas as pl
from jax.experimental.pallas import tpu as pltpu
from jax.sharding import Mesh, PartitionSpec as P


NS_STEPS = 5
newton_a = 3.4445
newton_b = -4.775
newton_c = 2.0315
epsilon = 1e-06
masked_score = -1e30

TOK = ("xh", "y", "z", "core")
CHIPS = ("xh", "y", "z")
REACH = 4
DH = 192
FH = 384
TOK_DEV = 128
ROWS = 2 * TOK_DEV
PACKED = ROWS + 16
GATHERED = TOK_DEV + 16
TAGS = 32
f32 = jnp.float32
bf16 = jnp.bfloat16
VMEM = pl.BlockSpec(memory_space=pltpu.VMEM)
SMEM = pl.BlockSpec(memory_space=pltpu.SMEM)


def normalize(values):
    widened = values.astype(f32)
    scale = lax.rsqrt(jnp.mean(widened * widened, axis=-1, keepdims=True) + epsilon)
    return (widened * scale).astype(bf16)


def halves(x):
    high = x.astype(bf16)
    return high, (x - high.astype(f32)).astype(bf16)


def nt(a, b):
    return lax.dot_general(a, b, (((1,), (1,)), ((), ())), preferred_element_type=f32)


def nn(a, b):
    return lax.dot_general(a, b, (((1,), (0,)), ((), ())), preferred_element_type=f32)


def tn(a, b):
    return lax.dot_general(a, b, (((0,), (0,)), ((), ())), preferred_element_type=f32)


def project_kernel(whole, wq, wk, wv, wr, query_ref, packed_ref, rates_ref):
    core = lax.axis_index("core")
    chip = (lax.axis_index("xh") * 4 + lax.axis_index("y")) * 8 + lax.axis_index("z")
    left = jnp.concatenate(
        (whole[:TOK_DEV], whole[GATHERED : GATHERED + TOK_DEV]), 0
    )
    base = 2 * GATHERED
    right = jnp.concatenate(
        (whole[base : base + TOK_DEV], whole[base + GATHERED : base + GATHERED + TOK_DEV]), 0
    )

    def both(w):
        return nn(left, w[:FH]) + nn(right, w[FH:])

    def own(w):
        product = both(w)
        return jnp.where(core == 0, product[:, :DH], product[:, DH:]).astype(bf16)

    query_ref[...] = own(wq)
    packed_ref[:ROWS] = jnp.concatenate((own(wk), own(wv)), 1)
    tags = jnp.concatenate(
        (whole[TOK_DEV:GATHERED, :TOK_DEV], whole[GATHERED + TOK_DEV : base, :TOK_DEV]), 1
    )
    packed_ref[ROWS:] = jnp.concatenate((tags, jnp.zeros((16, FH - ROWS), bf16)), 1)
    both_rates = jax.nn.softplus(nt(left, wr[:, :FH]) + nt(right, wr[:, FH:]))
    rates = jnp.where(core == 0, both_rates[:, :1], both_rates[:, 1:])
    rates_ref[...] = rates * jnp.where(chip < 48, 1.0, 0.0)


def gradient_kernel(packed, rates, gate_ref, up_ref, down_ref, sent_ref):
    core = lax.axis_index("core")
    keys_n = normalize(packed[:ROWS, :DH])
    value = packed[:ROWS, DH:].astype(f32)
    gate = nn(keys_n, gate_ref[core].astype(bf16))
    upward = nn(keys_n, up_ref[core].astype(bf16))
    logistic = jax.nn.sigmoid(gate)
    active = gate * logistic
    product = (active * upward).astype(bf16)
    error = (-rates[...] * value).astype(bf16)
    back = nn(error, down_ref[core].astype(bf16))
    grad_g = (back * upward * logistic * (1.0 + gate * (1.0 - logistic))).astype(bf16)
    grad_u = (back * active).astype(bf16)
    sent_ref[:DH] = tn(keys_n, grad_g).astype(bf16)
    sent_ref[DH : 2 * DH] = tn(keys_n, grad_u).astype(bf16)
    sent_ref[2 * DH :] = tn(error, product).astype(bf16)


def add_kernel(got, sent_ref):
    part = got[0].astype(f32)
    for i in range(1, 8):
        part = part + got[i].astype(f32)
    part = part.astype(bf16)
    for i in range(8):
        sent_ref[i] = part


def attend_kernel(query_ref, *refs):
    pieces, attended_ref, scores_ref = refs[:-2], refs[-2], refs[-1]
    query = query_ref[...]
    numbers = lax.broadcasted_iota(jnp.int32, (TAGS, ROWS), 0).astype(f32)

    def marks(piece):
        return jnp.where(numbers == piece[ROWS : ROWS + 1, :ROWS].astype(f32), 1.0, 0.0).astype(bf16)

    own_marks = marks(pieces[0])
    own_marks = jnp.where(numbers > 0.5, own_marks, jnp.zeros_like(own_marks))
    peak = None
    for p, piece in enumerate(pieces):
        scores = nt(query, piece[:ROWS, :DH]) * DH**-0.5
        scores = jnp.where(tn(own_marks, marks(piece)) > 0.5, scores, masked_score)
        scores_ref[:, p * ROWS : (p + 1) * ROWS] = scores
        high = jnp.max(scores, axis=-1, keepdims=True)
        peak = high if peak is None else jnp.maximum(peak, high)
    mass = None
    for p in range(len(pieces)):
        weights = jnp.exp(scores_ref[:, p * ROWS : (p + 1) * ROWS] - peak)
        scores_ref[:, p * ROWS : (p + 1) * ROWS] = weights
        one = jnp.sum(weights, axis=-1, keepdims=True)
        mass = one if mass is None else mass + one
    inverse = 1.0 / mass
    total = None
    for p, piece in enumerate(pieces):
        weights = (scores_ref[:, p * ROWS : (p + 1) * ROWS] * inverse).astype(bf16)
        one = nn(weights, piece[:ROWS, DH:])
        total = one if total is None else total + one
    attended_ref[...] = total


def fresh_kernel(total_ref, gate_ref, up_ref, down_ref, step_ref, query_ref, attended_ref, mixed_ref):
    core = lax.axis_index("core")
    step = step_ref[core]
    currents = []
    for m in range(3):
        matrix = total_ref[m * DH : (m + 1) * DH].astype(f32)
        length = jnp.sqrt(jnp.sum(matrix * matrix))
        currents.append(matrix / (length + epsilon))
    for _ in range(NS_STEPS):
        squares = []
        for x in currents:
            h, l = halves(x)
            squares.append((h, l, nt(h, h) + (nt(h, l) + nt(l, h))))
        mixers = []
        for h, l, a in squares:
            ah, al = halves(a)
            aa = nn(ah, ah) + (nn(ah, al) + nn(al, ah))
            mixers.append((h, l, newton_b * a + newton_c * aa))
        nexts = []
        for x, (h, l, b) in zip(currents, mixers):
            bh, bl = halves(b)
            nexts.append(newton_a * x + (nn(bh, h) + (nn(bh, l) + nn(bl, h))))
        currents = nexts
    fresh = [
        (master[core] - step * ortho).astype(bf16)
        for master, ortho in zip((gate_ref, up_ref, down_ref), currents)
    ]
    queries_n = normalize(query_ref[...])
    gate = nn(queries_n, fresh[0])
    upward = nn(queries_n, fresh[1])
    product = (gate * jax.nn.sigmoid(gate) * upward).astype(bf16)
    mixed_ref[...] = (attended_ref[...] + nt(product, fresh[2])).astype(bf16)


def out_kernel(spread, weight, other, out_ref):
    core = lax.axis_index("core")
    xl = lax.axis_index("xl")
    rows = pl.ds(pl.multiple_of(core * TOK_DEV, TOK_DEV), TOK_DEV)
    columns = pl.ds(pl.multiple_of(xl * FH, FH), FH)
    total = nn(spread[2 * xl, rows], weight[:DH, columns])
    total += nn(spread[2 * xl + 1, rows], weight[DH:, columns])
    total += nn(spread[2 - 2 * xl, rows], other[:DH])
    total += nn(spread[3 - 2 * xl, rows], other[DH:])
    out_ref[...] = total.astype(bf16)


def call(kernel, shapes, args, specs=None, scratch=(), flops=0, bytes_accessed=0, room=12):
    several = isinstance(shapes, (list, tuple))
    return pl.pallas_call(
        kernel,
        out_shape=shapes,
        in_specs=specs or [VMEM] * len(args),
        out_specs=[VMEM] * len(shapes) if several else VMEM,
        scratch_shapes=list(scratch),
        cost_estimate=pl.CostEstimate(
            flops=flops, bytes_accessed=bytes_accessed, transcendentals=0
        ),
        compiler_params=pltpu.CompilerParams(vmem_limit_bytes=room << 20),
    )(*args)


def shape(dims, dtype):
    return jax.ShapeDtypeStruct(dims, dtype)


def hop(x, steps):
    return lax.ppermute(
        x, CHIPS, [(i, i + steps) for i in range(64) if 0 <= i + steps < 64]
    )


def layer(
    tokens,
    view_ids,
    query_weight,
    key_weight,
    value_weight,
    out_weight,
    rate_weight,
    fast_gate,
    fast_up,
    fast_down,
    step_size,
):
    xl = lax.axis_index("xl")
    tag = jnp.pad((view_ids + 1).astype(bf16)[None], ((0, 15), (0, FH - TOK_DEV)))
    whole = lax.all_gather(
        jnp.concatenate((tokens, tag), 0), ("xl", "core"), axis=0, tiled=True
    )
    query, packed, rates = call(
        project_kernel,
        [shape((ROWS, DH), bf16), shape((PACKED, FH), bf16), shape((ROWS, 1), f32)],
        (whole, query_weight, key_weight, value_weight, rate_weight.T),
        flops=2 * 256 * 768 * 1152,
        bytes_accessed=3 << 20,
    )
    pieces = [packed]
    ahead = behind = packed
    for _ in range(REACH):
        ahead = hop(ahead, 1)
        behind = hop(behind, -1)
        pieces += [ahead, behind]

    sent = call(
        gradient_kernel,
        shape((3 * DH, FH), bf16),
        (packed, rates, fast_gate, fast_up, fast_down),
        flops=2 * 256 * 192 * 384 * 6,
        bytes_accessed=3 << 20,
    ).reshape(8, 72, FH)

    def add(got):
        return call(add_kernel, shape((8, 72, FH), bf16), (got,), bytes_accessed=1 << 20)

    got = lax.all_to_all(sent, ("xh", "y"), 0, 0, tiled=True)
    sent = add(got)
    got = lax.all_to_all(sent, "z", 0, 0, tiled=True)
    sent = add(got)
    total = lax.all_to_all(sent, ("xh", "y"), 0, 0, tiled=True)
    total = total.reshape(3 * DH, FH)

    attended = call(
        attend_kernel,
        shape((ROWS, DH), f32),
        (query, *pieces),
        scratch=[pltpu.VMEM((ROWS, len(pieces) * ROWS), f32)],
        flops=4 * 256 * 2304 * 256,
        bytes_accessed=3 << 20,
    )
    mixed = call(
        fresh_kernel,
        shape((ROWS, DH), bf16),
        (total, fast_gate, fast_up, fast_down, step_size, query, attended),
        specs=[VMEM] * 4 + [SMEM] + [VMEM] * 2,
        flops=10**10,
        bytes_accessed=3 << 20,
    )

    theirs = lax.dynamic_slice_in_dim(out_weight, (1 - xl) * FH, FH, 1)
    other = lax.ppermute(theirs, "xl", [(0, 1), (1, 0)])
    spread = lax.all_gather(mixed, ("xl", "core"), axis=0)
    return call(
        out_kernel,
        shape((TOK_DEV, FH), bf16),
        (spread, out_weight, other),
        flops=2 * 128 * 768 * 384,
        bytes_accessed=2 << 20,
    )


def solution(mesh):
    fine = Mesh(mesh.devices.reshape(2, 4, 8, 2, 2), ("xh", "y", "z", "core", "xl"))
    placed = (
        P(TOK, "xl"),
        P(TOK),
        P(None, "xl"),
        P(None, "xl"),
        P(None, "xl"),
        P("xl", None),
        P(None, "xl"),
        P("xl", None, None),
        P("xl", None, None),
        P("xl", None, None),
        P("xl"),
    )
    return jax.shard_map(
        layer, mesh=fine, in_specs=placed, out_specs=P(TOK, "xl"), check_vma=False
    )
```

time: 138 us -> 126 us (0.913)
  the two profiles are of different devices: /device:TPU:1 before, /device:TPU:5 now
where the time goes in v2:
time: 126 us
  starting transfers between devices  57.5 us (46%)
  blocking collectives  33.1 us (26%)
  Pallas kernels  15.7 us (12%)
  waiting for transfers between devices  10.9 us (9%)
  local copies, waits for them, and re-layouts  6.78 us (5%)
  other arithmetic  1.62 us (1%)
    ppermute x8, starting transfers between devices, hop(): lax.ppermute(x, CHIPS, [(i, i + steps) for i in range(64) if 0 <= i + ste...  44.1 us
    pallas_call x7, Pallas kernels, call(): pl.pallas_call(kernel, out_shape=shapes, in_specs=specs or [VMEM] * len(a...  15.7 us
    all_to_all x1, blocking collectives, layer(): got = lax.all_to_all(sent, ('xh', 'y'), 0, 0, tiled=True)  14.1 us
    all_gather x1, blocking collectives, layer(): spread = lax.all_gather(mixed, ('xl', 'core'), axis=0)  12 us
    ppermute x8, waiting for transfers between devices, hop(): lax.ppermute(x, CHIPS, [(i, i + steps) for i in range(64) if 0 <= i + ste...  10.8 us
    all_to_all x1, starting transfers between devices, layer(): got = lax.all_to_all(sent, 'z', 0, 0, tiled=True)  8.18 us
    all_gather x1, blocking collectives, layer(): lax.all_gather(jnp.concatenate((tokens, tag), 0), ('xl', 'core'), axis=0,...  6.94 us
    unnamed x36, local copies, waits for them, and re-layouts  6.04 us
  transfers between devices with their start and end apart: 11, of which 3 were waited for; matrix products, arithmetic and copies ran while one was open for 1% of the time, Pallas kernels for 10%

profile of v2, /device:TPU:5, one launch (start us, length us, event | category | flops | bytes accessed | tf_op | source)
XLA Modules:
  0.0 125.7 jit_solution(5218754052808003209)
XLA Ops:
  0.0 0.7 convert_bitcast_fusion
  0.7 0.9 fusion.1
  1.6 6.9 %all_gather.9.whole = bf16[576,384]{1,0:T(8,128)(2,1)S(1)} all-gather(bf16[144,384]{1,0:T(8,128)(2,1)S(1)} %fusion.1), channel_id=1, replica_groups=mesh['xh'=2,'y'=4,'z'=8,'core'=2,'xl'=2] {'xl','core'}, dimensions={0}, use_global_device_ids=true | all-gather | bytes 552960 | tf_op jit(solution)/shard_map/all_gather | solution.py:229
  8.6 1.1 copy-done.2
  9.7 1.1 copy-done.3
  10.7 1.1 shard_map.109
  12.5 0.8 shard_map.110
  13.3 14.1 %all_to_all.15.got = bf16[8,72,384]{2,1,0:T(8,128)(2,1)S(1)} all-to-all(bf16[8,72,384]{2,1,0:T(8,128)(2,1)S(1)} %bitcast.7), channel_id=1, replica_groups=mesh['xh'=2,'y'=4,'z'=8,'core'=2,'xl'=2] {'xh','y'}, dimensions={0} | all-to-all | bytes 884736 | tf_op jit(solution)/shard_map/all_to_all | solution.py:257
  27.5 0.8 shard_map.111
  28.3 8.2 %all-to-all-start.1 = ((bf16[8,72,384]{2,1,0:T(8,128)(2,1)}), bf16[8,72,384]{2,1,0:T(8,128)(2,1)S(1)}, u32[]{:S(2)}, u32[]{:S(2)}) async-start(bf16[8,72,384]{2,1,0:T(8,128)(2,1)} %shard_map.111), calls=%async_computation.1 | async-start | bytes 884736 | tf_op jit(solution)/shard_map/all_to_all | solution.py:259
  36.5 3.4 %collective-permute-start = (bf16[272,384]{1,0:T(8,128)(2,1)S(1)}, bf16[272,384]{1,0:T(8,128)(2,1)S(1)}, u32[]{:S(2)}, u32[]{:S(2)}) collective-permute-start(bf16[272,384]{1,0:T(8,128)(2,1)S(1)} %get-tuple-element.8.packed.refs_0_), channel_id=1, source_target_pairs={{0,4},{4,8},{8,12},{12,16},{16,20},{20,24},{24,28},{28,32},{32,36}... | collective-permute-start | bytes 626696 | tf_op jit(solution)/shard_map/ppermute | solution.py:209
  39.9 7.6 %collective-permute-start.1 = (bf16[272,384]{1,0:T(8,128)(2,1)S(1)}, bf16[272,384]{1,0:T(8,128)(2,1)S(1)}, u32[]{:S(2)}, u32[]{:S(2)}) collective-permute-start(bf16[272,384]{1,0:T(8,128)(2,1)S(1)} %get-tuple-element.8.packed.refs_0_), channel_id=1, source_target_pairs={{4,0},{8,4},{12,8},{16,12},{20,16},{24,20},{28,24},{32,28},{36,32}... | collective-permute-start | bytes 626696 | tf_op jit(solution)/shard_map/ppermute | solution.py:209
  47.5 8.2 %collective-permute-done.refs_1_ = bf16[272,384]{1,0:T(8,128)(2,1)S(1)} collective-permute-done((bf16[272,384]{1,0:T(8,128)(2,1)S(1)}, bf16[272,384]{1,0:T(8,128)(2,1)S(1)}, u32[]{:S(2)}, u32[]{:S(2)}) %collective-permute-start) | collective-permute-done | bytes 208928 | tf_op jit(solution)/shard_map/ppermute | solution.py:209
  55.7 1.9 %collective-permute-start.2 = (bf16[272,384]{1,0:T(8,128)(2,1)S(1)}, bf16[272,384]{1,0:T(8,128)(2,1)S(1)}, u32[]{:S(2)}, u32[]{:S(2)}) collective-permute-start(bf16[272,384]{1,0:T(8,128)(2,1)S(1)} %collective-permute-done.refs_1_), channel_id=1, source_target_pairs={{0,4},{4,8},{8,12},{12,16},{16,20},{20,24},{24,28},{28,32},{32,36}... | collective-permute-start | bytes 626696 | tf_op jit(solution)/shard_map/ppermute | solution.py:209
  57.6 9.1 %collective-permute-start.3 = (bf16[272,384]{1,0:T(8,128)(2,1)S(1)}, bf16[272,384]{1,0:T(8,128)(2,1)}, u32[]{:S(2)}, u32[]{:S(2)}) collective-permute-start(bf16[272,384]{1,0:T(8,128)(2,1)S(1)} %collective-permute-done.1.refs_2_), channel_id=1, source_target_pairs={{4,0},{8,4},{12,8},{16,12},{20,16},{24,20},{28,24},{32,28},{36,32}... | collective-permute-start | bytes 626696 | tf_op jit(solution)/shard_map/ppermute | solution.py:209
  66.7 1.2 collective-permute-done.2.refs_3_
  68.0 1.9 %collective-permute-start.4 = (bf16[272,384]{1,0:T(8,128)(2,1)S(1)}, bf16[272,384]{1,0:T(8,128)(2,1)}, u32[]{:S(2)}, u32[]{:S(2)}) collective-permute-start(bf16[272,384]{1,0:T(8,128)(2,1)S(1)} %collective-permute-done.2.refs_3_), channel_id=1, source_target_pairs={{0,4},{4,8},{8,12},{12,16},{16,20},{20,24},{24,28},{28,32},{32,36}... | collective-permute-start | bytes 626696 | tf_op jit(solution)/shard_map/ppermute | solution.py:209
  69.9 9.2 %collective-permute-start.5 = (bf16[272,384]{1,0:T(8,128)(2,1)}, bf16[272,384]{1,0:T(8,128)(2,1)}, u32[]{:S(2)}, u32[]{:S(2)}) collective-permute-start(bf16[272,384]{1,0:T(8,128)(2,1)} %collective-permute-done.3.refs_4_), channel_id=1, source_target_pairs={{4,0},{8,4},{12,8},{16,12},{20,16},{24,20},{28,24},{32,28},{36,32}... | collective-permute-start | bytes 626696 | tf_op jit(solution)/shard_map/ppermute | solution.py:209
  79.1 0.8 shard_map.112
  79.9 4.4 %all-to-all-start.2 = ((bf16[8,72,384]{2,1,0:T(8,128)(2,1)}), bf16[8,72,384]{2,1,0:T(8,128)(2,1)S(1)}, u32[]{:S(2)}, u32[]{:S(2)}) async-start(bf16[8,72,384]{2,1,0:T(8,128)(2,1)} %shard_map.112), calls=%async_computation.2 | async-start | bytes 884736 | tf_op jit(solution)/shard_map/all_to_all | solution.py:261
  84.3 1.9 %collective-permute-start.6 = (bf16[272,384]{1,0:T(8,128)(2,1)}, bf16[272,384]{1,0:T(8,128)(2,1)}, u32[]{:S(2)}, u32[]{:S(2)}) collective-permute-start(bf16[272,384]{1,0:T(8,128)(2,1)} %collective-permute-done.4.refs_5_), channel_id=1, source_target_pairs={{0,4},{4,8},{8,12},{12,16},{16,20},{20,24},{24,28},{28,32},{32,36}... | collective-permute-start | bytes 626696 | tf_op jit(solution)/shard_map/ppermute | solution.py:209
  86.2 9.1 %collective-permute-start.7 = (bf16[272,384]{1,0:T(8,128)(2,1)}, bf16[272,384]{1,0:T(8,128)(2,1)}, u32[]{:S(2)}, u32[]{:S(2)}) collective-permute-start(bf16[272,384]{1,0:T(8,128)(2,1)} %collective-permute-done.5.refs_6_), channel_id=1, source_target_pairs={{4,0},{8,4},{12,8},{16,12},{20,16},{24,20},{28,24},{32,28},{36,32}... | collective-permute-start | bytes 626696 | tf_op jit(solution)/shard_map/ppermute | solution.py:209
  95.4 0.7 constant_dynamic-slice_fusion
  96.1 0.8 collective-permute-start.8
  97.0 1.4 %collective-permute-done.7.refs_8_ = bf16[272,384]{1,0:T(8,128)(2,1)} collective-permute-done((bf16[272,384]{1,0:T(8,128)(2,1)}, bf16[272,384]{1,0:T(8,128)(2,1)}, u32[]{:S(2)}, u32[]{:S(2)}) %collective-permute-start.7) | collective-permute-done | bytes 208928 | tf_op jit(solution)/shard_map/ppermute | solution.py:209
  98.4 3.6 %shard_map.113.attended_ref = f32[256,192]{1,0:T(8,128)S(1)} custom-call(bf16[256,192]{1,0:T(8,128)(2,1)S(1)} %copy-done.14, bf16[272,384]{1,0:T(8,128)(2,1)S(1)} %get-tuple-element.8.packed.refs_0_, bf16[272,384]{1,0:T(8,128)(2,1)S(1)} %collective-permute-done.refs_1_, bf16[272,384]{1,0:T(8,128)(2,1)S(1)} %copy-done.10, bf16[272,384]{1,0:T(8,128)(2,1)S(1)} %copy-done.12, ...), custom_call_target="tpu_custom_call" | custom-call | flops 603979776 | bytes 3145728 | tf_op jit(solution)/shard_map/pallas_call | solution.py:191
  102.0 0.7 copy-done.7
  103.3 0.9 copy-done.8
  104.3 0.9 copy-done.15
  105.2 7.6 %shard_map.114 = bf16[256,192]{1,0:T(8,128)(2,1)S(1)} custom-call(bf16[576,384]{1,0:T(8,128)(2,1)S(1)} %bitcast.8, f32[2,192,384]{2,1,0:T(8,128)S(1)} %copy-done.4, f32[2,192,384]{2,1,0:T(8,128)S(1)} %copy-done.5, f32[2,192,384]{2,1,0:T(8,128)S(1)} %copy-done.6, f32[2]{0:T(128)S(1)} %copy-done.17, bf16[256,192]{1,0:T(8,128)(2,1)S(1)} %copy-done.15, ...), custom_call_target="tpu_custom_call" | custom-call | flops 10000000000 | bytes 3145728 | tf_op jit(solution)/shard_map/pallas_call | solution.py:191
  112.8 12.0 %all-gather = bf16[1024,192]{1,0:T(8,128)(2,1)S(1)} all-gather(bf16[256,192]{1,0:T(8,128)(2,1)S(1)} %shard_map.114), channel_id=2, replica_groups=mesh['xh'=2,'y'=4,'z'=8,'core'=2,'xl'=2] {'xl','core'}, dimensions={0}, use_global_device_ids=true | all-gather | bytes 491520 | tf_op jit(solution)/shard_map/all_gather | solution.py:283
  124.7 0.9 shard_map.115
  (39 shorter events, 1.4 us)
Async XLA Ops:
  0.0 8.6 %copy-start.1 = (bf16[768,384]{1,0:T(8,128)(2,1)S(1)}, bf16[768,384]{1,0:T(8,128)(2,1)}, u32[]{:S(2)}) copy-start(bf16[768,384]{1,0:T(8,128)(2,1)} %wq.1) | copy-start | bytes 1769476
  1.6 7.0 %copy-start.16 = (bf16[768,2]{0,1:T(2,128)(2,1)S(1)}, bf16[768,2]{0,1:T(2,128)(2,1)}, u32[]{:S(2)}) copy-start(bf16[768,2]{0,1:T(2,128)(2,1)} %param.17) | copy-start | bytes 9220
  8.6 1.1 copy-start.2
  9.7 1.1 copy-start.3
  10.7 1.8 %copy-start.4 = (f32[2,192,384]{2,1,0:T(8,128)S(1)}, f32[2,192,384]{2,1,0:T(8,128)}, u32[]{:S(2)}) copy-start(f32[2,192,384]{2,1,0:T(8,128)} %gate_ref.3) | copy-start | bytes 1769476
  10.7 1.8 %copy-start.5 = (f32[2,192,384]{2,1,0:T(8,128)S(1)}, f32[2,192,384]{2,1,0:T(8,128)}, u32[]{:S(2)}) copy-start(f32[2,192,384]{2,1,0:T(8,128)} %up_ref.3) | copy-start | bytes 1769476
  10.7 1.8 %copy-start.6 = (f32[2,192,384]{2,1,0:T(8,128)S(1)}, f32[2,192,384]{2,1,0:T(8,128)}, u32[]{:S(2)}) copy-start(f32[2,192,384]{2,1,0:T(8,128)} %down_ref.3) | copy-start | bytes 1769476
  11.9 0.7 copy-start.13
  28.3 50.8 %all-to-all-start.1 = ((bf16[8,72,384]{2,1,0:T(8,128)(2,1)}), bf16[8,72,384]{2,1,0:T(8,128)(2,1)S(1)}, u32[]{:S(2)}, u32[]{:S(2)}) async-start(bf16[8,72,384]{2,1,0:T(8,128)(2,1)} %shard_map.111), calls=%async_computation.1 | async-start | bytes 884736 | tf_op jit(solution)/shard_map/all_to_all | solution.py:259
  36.5 19.2 %collective-permute-start = (bf16[272,384]{1,0:T(8,128)(2,1)S(1)}, bf16[272,384]{1,0:T(8,128)(2,1)S(1)}, u32[]{:S(2)}, u32[]{:S(2)}) collective-permute-start(bf16[272,384]{1,0:T(8,128)(2,1)S(1)} %get-tuple-element.8.packed.refs_0_), channel_id=1, source_target_pairs={{0,4},{4,8},{8,12},{12,16},{16,20},{20,24},{24,28},{28,32},{32,36}... | collective-permute-start | bytes 626696 | tf_op jit(solution)/shard_map/ppermute | solution.py:209
  39.9 17.8 %collective-permute-start.1 = (bf16[272,384]{1,0:T(8,128)(2,1)S(1)}, bf16[272,384]{1,0:T(8,128)(2,1)S(1)}, u32[]{:S(2)}, u32[]{:S(2)}) collective-permute-start(bf16[272,384]{1,0:T(8,128)(2,1)S(1)} %get-tuple-element.8.packed.refs_0_), channel_id=1, source_target_pairs={{4,0},{8,4},{12,8},{16,12},{20,16},{24,20},{28,24},{32,28},{36,32}... | collective-permute-start | bytes 626696 | tf_op jit(solution)/shard_map/ppermute | solution.py:209
  55.7 12.3 %collective-permute-start.2 = (bf16[272,384]{1,0:T(8,128)(2,1)S(1)}, bf16[272,384]{1,0:T(8,128)(2,1)S(1)}, u32[]{:S(2)}, u32[]{:S(2)}) collective-permute-start(bf16[272,384]{1,0:T(8,128)(2,1)S(1)} %collective-permute-done.refs_1_), channel_id=1, source_target_pairs={{0,4},{4,8},{8,12},{12,16},{16,20},{20,24},{24,28},{28,32},{32,36}... | collective-permute-start | bytes 626696 | tf_op jit(solution)/shard_map/ppermute | solution.py:209
  57.6 22.3 %copy-start.9 = (bf16[272,384]{1,0:T(8,128)(2,1)}, bf16[272,384]{1,0:T(8,128)(2,1)S(1)}, u32[]{:S(2)}) copy-start(bf16[272,384]{1,0:T(8,128)(2,1)S(1)} %collective-permute-done.1.refs_2_) | copy-start | bytes 626692
  57.6 12.2 %collective-permute-start.3 = (bf16[272,384]{1,0:T(8,128)(2,1)S(1)}, bf16[272,384]{1,0:T(8,128)(2,1)}, u32[]{:S(2)}, u32[]{:S(2)}) collective-permute-start(bf16[272,384]{1,0:T(8,128)(2,1)S(1)} %collective-permute-done.1.refs_2_), channel_id=1, source_target_pairs={{4,0},{8,4},{12,8},{16,12},{20,16},{24,20},{28,24},{32,28},{36,32}... | collective-permute-start | bytes 626696 | tf_op jit(solution)/shard_map/ppermute | solution.py:209
  68.0 12.0 %copy-start.11 = (bf16[272,384]{1,0:T(8,128)(2,1)}, bf16[272,384]{1,0:T(8,128)(2,1)S(1)}, u32[]{:S(2)}) copy-start(bf16[272,384]{1,0:T(8,128)(2,1)S(1)} %collective-permute-done.2.refs_3_) | copy-start | bytes 626692
  68.0 16.4 %collective-permute-start.4 = (bf16[272,384]{1,0:T(8,128)(2,1)S(1)}, bf16[272,384]{1,0:T(8,128)(2,1)}, u32[]{:S(2)}, u32[]{:S(2)}) collective-permute-start(bf16[272,384]{1,0:T(8,128)(2,1)S(1)} %collective-permute-done.2.refs_3_), channel_id=1, source_target_pairs={{0,4},{4,8},{8,12},{12,16},{16,20},{20,24},{24,28},{28,32},{32,36}... | collective-permute-start | bytes 626696 | tf_op jit(solution)/shard_map/ppermute | solution.py:209
  69.9 16.4 %collective-permute-start.5 = (bf16[272,384]{1,0:T(8,128)(2,1)}, bf16[272,384]{1,0:T(8,128)(2,1)}, u32[]{:S(2)}, u32[]{:S(2)}) collective-permute-start(bf16[272,384]{1,0:T(8,128)(2,1)} %collective-permute-done.3.refs_4_), channel_id=1, source_target_pairs={{4,0},{8,4},{12,8},{16,12},{20,16},{24,20},{28,24},{32,28},{36,32}... | collective-permute-start | bytes 626696 | tf_op jit(solution)/shard_map/ppermute | solution.py:209
  79.9 15.4 %copy-start = (bf16[384,768]{1,0:T(8,128)(2,1)S(1)}, bf16[384,768]{1,0:T(8,128)(2,1)}, u32[]{:S(2)}) copy-start(bf16[384,768]{1,0:T(8,128)(2,1)} %weight.1) | copy-start | bytes 1769476
  79.9 22.8 %all-to-all-start.2 = ((bf16[8,72,384]{2,1,0:T(8,128)(2,1)}), bf16[8,72,384]{2,1,0:T(8,128)(2,1)S(1)}, u32[]{:S(2)}, u32[]{:S(2)}) async-start(bf16[8,72,384]{2,1,0:T(8,128)(2,1)} %shard_map.112), calls=%async_computation.2 | async-start | bytes 884736 | tf_op jit(solution)/shard_map/all_to_all | solution.py:261
  84.3 12.7 %collective-permute-start.6 = (bf16[272,384]{1,0:T(8,128)(2,1)}, bf16[272,384]{1,0:T(8,128)(2,1)}, u32[]{:S(2)}, u32[]{:S(2)}) collective-permute-start(bf16[272,384]{1,0:T(8,128)(2,1)} %collective-permute-done.4.refs_5_), channel_id=1, source_target_pairs={{0,4},{4,8},{8,12},{12,16},{16,20},{20,24},{24,28},{28,32},{32,36}... | collective-permute-start | bytes 626696 | tf_op jit(solution)/shard_map/ppermute | solution.py:209
  86.2 12.1 %collective-permute-start.7 = (bf16[272,384]{1,0:T(8,128)(2,1)}, bf16[272,384]{1,0:T(8,128)(2,1)}, u32[]{:S(2)}, u32[]{:S(2)}) collective-permute-start(bf16[272,384]{1,0:T(8,128)(2,1)} %collective-permute-done.5.refs_6_), channel_id=1, source_target_pairs={{4,0},{8,4},{12,8},{16,12},{20,16},{24,20},{28,24},{32,28},{36,32}... | collective-permute-start | bytes 626696 | tf_op jit(solution)/shard_map/ppermute | solution.py:209
  95.4 3.0 %copy-start.10 = (bf16[272,384]{1,0:T(8,128)(2,1)S(1)}, bf16[272,384]{1,0:T(8,128)(2,1)}, u32[]{:S(2)}) copy-start(bf16[272,384]{1,0:T(8,128)(2,1)} %copy-done.9) | copy-start | bytes 626692
  95.4 3.0 %copy-start.12 = (bf16[272,384]{1,0:T(8,128)(2,1)S(1)}, bf16[272,384]{1,0:T(8,128)(2,1)}, u32[]{:S(2)}) copy-start(bf16[272,384]{1,0:T(8,128)(2,1)} %copy-done.11) | copy-start | bytes 626692
  95.4 3.0 %copy-start.14 = (bf16[256,192]{1,0:T(8,128)(2,1)S(1)}, bf16[256,192]{1,0:T(8,128)(2,1)}, u32[]{:S(2)}) copy-start(bf16[256,192]{1,0:T(8,128)(2,1)} %copy-done.13) | copy-start | bytes 294916
  96.1 28.6 %collective-permute-start.8 = (bf16[384,384]{1,0:T(8,128)(2,1)}, bf16[384,384]{1,0:T(8,128)(2,1)S(1)}, u32[]{:S(2)}, u32[]{:S(2)}) collective-permute-start(bf16[384,384]{1,0:T(8,128)(2,1)} %constant_dynamic-slice_fusion), channel_id=1, source_target_pairs={{0,1},{1,0},{2,3},{3,2},{4,5},{5,4},{6,7},{7,6},{8,9},{9,8},{10,11... | collective-permute-start | bytes 884744 | tf_op jit(solution)/shard_map/ppermute | solution.py:282
  102.0 0.7 copy-start.7
  102.7 0.7 copy-start.17
  103.3 0.9 copy-start.8
  104.3 0.9 copy-start.15

commit v3 on v2

--- a/solution.py
+++ b/solution.py
@@ -14,7 +14,6 @@
 masked_score = -1e30
 
 TOK = ("xh", "y", "z", "core")
-CHIPS = ("xh", "y", "z")
 REACH = 4
 DH = 192
 FH = 384
@@ -25,6 +24,8 @@
 TAGS = 32
 f32 = jnp.float32
 bf16 = jnp.bfloat16
+ANY = pl.BlockSpec(memory_space=pl.ANY)
+HBM = pl.BlockSpec(memory_space=pltpu.HBM)
 VMEM = pl.BlockSpec(memory_space=pltpu.VMEM)
 SMEM = pl.BlockSpec(memory_space=pltpu.SMEM)
 
@@ -52,7 +53,28 @@
     return lax.dot_general(a, b, (((0,), (0,)), ((), ())), preferred_element_type=f32)
 
 
-def project_kernel(whole, wq, wk, wv, wr, query_ref, packed_ref, rates_ref):
+def copies(sem, *pairs):
+    started = [
+        pltpu.make_async_copy(source, target, sem.at[i]) for i, (source, target) in enumerate(pairs)
+    ]
+    for copy in started:
+        copy.start()
+    return started
+
+
+def tag_kernel(tokens, views_hbm, tagged_ref, views, sem):
+    fetches = copies(sem, (views_hbm, views), (tokens, tagged_ref.at[pl.ds(0, TOK_DEV)]))
+    fetches[0].wait()
+    row = (views[...] + 1).astype(f32).astype(bf16)
+    row = jnp.concatenate((row, jnp.zeros((1, FH - TOK_DEV), bf16)), 1)
+    tagged_ref[TOK_DEV:] = jnp.broadcast_to(row, (16, FH))
+    fetches[1].wait()
+
+
+def project_kernel(
+    whole, wq_hbm, wk_hbm, wv_hbm, wr, query_hbm, packed_ref, rates_ref, wq, wk, wv, query_ref, sem
+):
+    fetches = copies(sem, (wq_hbm, wq), (wk_hbm, wk), (wv_hbm, wv))
     core = lax.axis_index("core")
     chip = (lax.axis_index("xh") * 4 + lax.axis_index("y")) * 8 + lax.axis_index("z")
     left = jnp.concatenate(
@@ -62,29 +84,38 @@
     right = jnp.concatenate(
         (whole[base : base + TOK_DEV], whole[base + GATHERED : base + GATHERED + TOK_DEV]), 0
     )
-
-    def both(w):
-        return nn(left, w[:FH]) + nn(right, w[FH:])
-
-    def own(w):
-        product = both(w)
-        return jnp.where(core == 0, product[:, :DH], product[:, DH:]).astype(bf16)
-
-    query_ref[...] = own(wq)
-    packed_ref[:ROWS] = jnp.concatenate((own(wk), own(wv)), 1)
-    tags = jnp.concatenate(
-        (whole[TOK_DEV:GATHERED, :TOK_DEV], whole[GATHERED + TOK_DEV : base, :TOK_DEV]), 1
-    )
-    packed_ref[ROWS:] = jnp.concatenate((tags, jnp.zeros((16, FH - ROWS), bf16)), 1)
     both_rates = jax.nn.softplus(nt(left, wr[:, :FH]) + nt(right, wr[:, FH:]))
     rates = jnp.where(core == 0, both_rates[:, :1], both_rates[:, 1:])
     rates_ref[...] = rates * jnp.where(chip < 48, 1.0, 0.0)
+    tags = jnp.concatenate(
+        (whole[TOK_DEV:GATHERED, :TOK_DEV], whole[GATHERED + TOK_DEV : base, :TOK_DEV]), 1
+    )
+    tags = jnp.concatenate((tags, jnp.zeros((16, FH - ROWS), bf16)), 1)
+
+    def both(w):
+        return nn(left, w[:FH]) + nn(right, w[FH:])
+
+    fetches[0].wait()
+    query = both(wq)
+    query_ref[...] = jnp.where(core == 0, query[:, :DH], query[:, DH:]).astype(bf16)
+    store = pltpu.make_async_copy(query_ref, query_hbm, sem.at[3])
+    store.start()
+    fetches[1].wait()
+    key = both(wk).astype(bf16)
+    fetches[2].wait()
+    value = both(wv).astype(bf16)
+    for h in range(2):
+        part = slice(h * DH, (h + 1) * DH)
+        packed_ref[h, :ROWS] = jnp.concatenate((key[:, part], value[:, part]), 1)
+        packed_ref[h, ROWS:] = tags
+    store.wait()
 
 
 def gradient_kernel(packed, rates, gate_ref, up_ref, down_ref, sent_ref):
     core = lax.axis_index("core")
-    keys_n = normalize(packed[:ROWS, :DH])
-    value = packed[:ROWS, DH:].astype(f32)
+    mine = packed[core]
+    keys_n = normalize(mine[:ROWS, :DH])
+    value = mine[:ROWS, DH:].astype(f32)
     gate = nn(keys_n, gate_ref[core].astype(bf16))
     upward = nn(keys_n, up_ref[core].astype(bf16))
     logistic = jax.nn.sigmoid(gate)
@@ -99,6 +130,13 @@
     sent_ref[2 * DH :] = tn(error, product).astype(bf16)
 
 
+def pick_kernel(*refs):
+    pieces, picked_ref = refs[:-1], refs[-1]
+    core = lax.axis_index("core")
+    for i, piece in enumerate(pieces):
+        picked_ref[i] = piece[1 - core]
+
+
 def add_kernel(got, sent_ref):
     part = got[0].astype(f32)
     for i in range(1, 8):
@@ -108,10 +146,14 @@
         sent_ref[i] = part
 
 
-def attend_kernel(query_ref, *refs):
-    pieces, attended_ref, scores_ref = refs[:-2], refs[-2], refs[-1]
+def attend_kernel(query_ref, own, *refs):
+    relayed, swapped = refs[:REACH], refs[REACH]
+    attended_hbm, scores_ref, attended_ref, sem = refs[REACH + 1 :]
+    core = lax.axis_index("core")
     query = query_ref[...]
     numbers = lax.broadcasted_iota(jnp.int32, (TAGS, ROWS), 0).astype(f32)
+    pieces = [ref.at[core] for ref in (own, *relayed)]
+    pieces += [swapped.at[i] for i in range(REACH)]
 
     def marks(piece):
         return jnp.where(numbers == piece[ROWS : ROWS + 1, :ROWS].astype(f32), 1.0, 0.0).astype(bf16)
@@ -138,11 +180,25 @@
         one = nn(weights, piece[:ROWS, DH:])
         total = one if total is None else total + one
     attended_ref[...] = total
-
-
-def fresh_kernel(total_ref, gate_ref, up_ref, down_ref, step_ref, query_ref, attended_ref, mixed_ref):
-    core = lax.axis_index("core")
-    step = step_ref[core]
+    store = pltpu.make_async_copy(attended_ref, attended_hbm, sem.at[0])
+    store.start()
+    store.wait()
+
+
+def fresh_kernel(
+    total_ref, gate_hbm, up_hbm, down_hbm, step_hbm, query_hbm, attended_hbm,
+    mixed_ref, masters, step_ref, query_ref, attended_ref, sem,
+):
+    core = lax.axis_index("core")
+    fetches = copies(
+        sem,
+        (gate_hbm.at[core], masters.at[0]),
+        (up_hbm.at[core], masters.at[1]),
+        (down_hbm.at[core], masters.at[2]),
+        (step_hbm, step_ref),
+        (query_hbm, query_ref),
+        (attended_hbm, attended_ref),
+    )
     currents = []
     for m in range(3):
         matrix = total_ref[m * DH : (m + 1) * DH].astype(f32)
@@ -152,21 +208,24 @@
         squares = []
         for x in currents:
             h, l = halves(x)
-            squares.append((h, l, nt(h, h) + (nt(h, l) + nt(l, h))))
+            cross = nt(h, l)
+            squares.append((h, l, nt(h, h) + (cross + cross.T)))
         mixers = []
         for h, l, a in squares:
             ah, al = halves(a)
-            aa = nn(ah, ah) + (nn(ah, al) + nn(al, ah))
+            cross = nt(ah, al)
+            aa = nt(ah, ah) + (cross + cross.T)
             mixers.append((h, l, newton_b * a + newton_c * aa))
         nexts = []
         for x, (h, l, b) in zip(currents, mixers):
             bh, bl = halves(b)
-            nexts.append(newton_a * x + (nn(bh, h) + (nn(bh, l) + nn(bl, h))))
+            wide = nn(bh, jnp.concatenate((h, l), 1))
+            nexts.append(newton_a * x + (wide[:, :FH] + (wide[:, FH:] + nn(bl, h))))
         currents = nexts
-    fresh = [
-        (master[core] - step * ortho).astype(bf16)
-        for master, ortho in zip((gate_ref, up_ref, down_ref), currents)
-    ]
+    for fetch in fetches:
+        fetch.wait()
+    step = step_ref[core]
+    fresh = [(masters[m] - step * currents[m]).astype(bf16) for m in range(3)]
     queries_n = normalize(query_ref[...])
     gate = nn(queries_n, fresh[0])
     upward = nn(queries_n, fresh[1])
@@ -186,13 +245,17 @@
     out_ref[...] = total.astype(bf16)
 
 
-def call(kernel, shapes, args, specs=None, scratch=(), flops=0, bytes_accessed=0, room=12):
+def call(kernel, shapes, args, specs=None, outs=None, scratch=(), flops=0, bytes_accessed=0, room=12):
     several = isinstance(shapes, (list, tuple))
+    args = [
+        pltpu.with_memory_space_constraint(arg, pltpu.HBM) if spec is HBM else arg
+        for arg, spec in zip(args, specs or [VMEM] * len(args))
+    ]
     return pl.pallas_call(
         kernel,
         out_shape=shapes,
         in_specs=specs or [VMEM] * len(args),
-        out_specs=[VMEM] * len(shapes) if several else VMEM,
+        out_specs=outs or ([VMEM] * len(shapes) if several else VMEM),
         scratch_shapes=list(scratch),
         cost_estimate=pl.CostEstimate(
             flops=flops, bytes_accessed=bytes_accessed, transcendentals=0
@@ -205,10 +268,9 @@
     return jax.ShapeDtypeStruct(dims, dtype)
 
 
-def hop(x, steps):
-    return lax.ppermute(
-        x, CHIPS, [(i, i + steps) for i in range(64) if 0 <= i + steps < 64]
-    )
+def hop(x):
+    pairs = [(2 * c, 2 * c + 2) for c in range(63)] + [(2 * c + 3, 2 * c + 1) for c in range(63)]
+    return lax.ppermute(x, TOK, pairs)
 
 
 def layer(
@@ -225,23 +287,31 @@
     step_size,
 ):
     xl = lax.axis_index("xl")
-    tag = jnp.pad((view_ids + 1).astype(bf16)[None], ((0, 15), (0, FH - TOK_DEV)))
-    whole = lax.all_gather(
-        jnp.concatenate((tokens, tag), 0), ("xl", "core"), axis=0, tiled=True
-    )
+    tagged = call(
+        tag_kernel,
+        shape((GATHERED, FH), bf16),
+        (tokens, view_ids.reshape(1, TOK_DEV)),
+        specs=[HBM, HBM],
+        scratch=[pltpu.VMEM((1, TOK_DEV), jnp.int32), pltpu.SemaphoreType.DMA((2,))],
+        bytes_accessed=1 << 18,
+    )
+    whole = lax.all_gather(tagged, ("xl", "core"), axis=0, tiled=True)
     query, packed, rates = call(
         project_kernel,
-        [shape((ROWS, DH), bf16), shape((PACKED, FH), bf16), shape((ROWS, 1), f32)],
+        [shape((ROWS, DH), bf16), shape((2, PACKED, FH), bf16), shape((ROWS, 1), f32)],
         (whole, query_weight, key_weight, value_weight, rate_weight.T),
+        specs=[VMEM, HBM, HBM, HBM, VMEM],
+        outs=[ANY, VMEM, VMEM],
+        scratch=[pltpu.VMEM((768, FH), bf16)] * 3
+        + [pltpu.VMEM((ROWS, DH), bf16), pltpu.SemaphoreType.DMA((4,))],
         flops=2 * 256 * 768 * 1152,
         bytes_accessed=3 << 20,
     )
-    pieces = [packed]
-    ahead = behind = packed
+    relayed = []
+    moving = packed
     for _ in range(REACH):
-        ahead = hop(ahead, 1)
-        behind = hop(behind, -1)
-        pieces += [ahead, behind]
+        moving = hop(moving)
+        relayed.append(moving)
 
     sent = call(
         gradient_kernel,
@@ -261,11 +331,18 @@
     total = lax.all_to_all(sent, ("xh", "y"), 0, 0, tiled=True)
     total = total.reshape(3 * DH, FH)
 
+    picked = call(pick_kernel, shape((REACH, PACKED, FH), bf16), relayed, bytes_accessed=2 << 20)
+    swapped = lax.ppermute(picked, "core", [(0, 1), (1, 0)])
     attended = call(
         attend_kernel,
-        shape((ROWS, DH), f32),
-        (query, *pieces),
-        scratch=[pltpu.VMEM((ROWS, len(pieces) * ROWS), f32)],
+        pltpu.HBM((ROWS, DH), f32),
+        (query, packed, *relayed, swapped),
+        outs=HBM,
+        scratch=[
+            pltpu.VMEM((ROWS, (2 * REACH + 1) * ROWS), f32),
+            pltpu.VMEM((ROWS, DH), f32),
+            pltpu.SemaphoreType.DMA((1,)),
+        ],
         flops=4 * 256 * 2304 * 256,
         bytes_accessed=3 << 20,
     )
@@ -273,7 +350,14 @@
         fresh_kernel,
         shape((ROWS, DH), bf16),
         (total, fast_gate, fast_up, fast_down, step_size, query, attended),
-        specs=[VMEM] * 4 + [SMEM] + [VMEM] * 2,
+        specs=[VMEM] + [HBM] * 4 + [ANY, HBM],
+        scratch=[
+            pltpu.VMEM((3, DH, FH), f32),
+            pltpu.SMEM((2,), f32),
+            pltpu.VMEM((ROWS, DH), bf16),
+            pltpu.VMEM((ROWS, DH), f32),
+            pltpu.SemaphoreType.DMA((6,)),
+        ],
         flops=10**10,
         bytes_accessed=3 << 20,
     )
@@ -305,6 +389,4 @@
         P("xl", None, None),
         P("xl"),
     )
-    return jax.shard_map(
-        layer, mesh=fine, in_specs=placed, out_specs=P(TOK, "xl"), check_vma=False
-    )
+    return jax.shard_map(layer, mesh=fine, in_specs=placed, out_specs=P(TOK, "xl"), check_vma=False)

time: 126 us -> 117 us (0.929)
  the two profiles are of different devices: /device:TPU:5 before, /device:TPU:1 now
where the time goes in v3:
time: 117 us; the launch traced here: 116 us
  waiting for transfers between devices  40.3 us (34%)
  starting transfers between devices  37.6 us (32%)
  Pallas kernels  19.6 us (17%)
  blocking collectives  17.7 us (15%)
    all_to_all x1, starting transfers between devices, layer(): got = lax.all_to_all(sent, ('xh', 'y'), 0, 0, tiled=True)  22.8 us
    pallas_call x9, Pallas kernels, call(): pl.pallas_call(kernel, out_shape=shapes, in_specs=specs or [VMEM] * len(a...  19.6 us
    ppermute x4, waiting for transfers between devices, hop(): return lax.ppermute(x, TOK, pairs)  15 us
    all_to_all x1, waiting for transfers between devices, layer(): got = lax.all_to_all(sent, 'z', 0, 0, tiled=True)  14.3 us
    all_gather x1, blocking collectives, layer(): whole = lax.all_gather(tagged, ('xl', 'core'), axis=0, tiled=True)  9.31 us
    all_gather x1, blocking collectives, layer(): spread = lax.all_gather(mixed, ('xl', 'core'), axis=0)  8.42 us
    all_to_all x1, waiting for transfers between devices, layer(): got = lax.all_to_all(sent, ('xh', 'y'), 0, 0, tiled=True)  7.15 us
    ppermute x4, starting transfers between devices, hop(): return lax.ppermute(x, TOK, pairs)  5.15 us
  transfers between devices with their start and end apart: 9, of which 5 were waited for; matrix products, arithmetic and copies ran while one was open for 1% of the time, Pallas kernels for 13%

profile of v3, /device:TPU:1, one launch (start us, length us, event | category | flops | bytes accessed | tf_op | source)
XLA Modules:
  0.0 116.1 jit_solution(12733639413370624048)
XLA Ops:
  0.0 0.9 shard_map.109
  0.9 0.0 copy-start.4
  0.9 9.3 %all_gather.9.whole = bf16[576,384]{1,0:T(8,128)(2,1)S(1)} all-gather(bf16[144,384]{1,0:T(8,128)(2,1)S(1)} %shard_map.109), channel_id=1, replica_groups=mesh['xh'=2,'y'=4,'z'=8,'core'=2,'xl'=2] {'xl','core'}, dimensions={0}, use_global_device_ids=true | all-gather | bytes 552960 | tf_op jit(solution)/shard_map/all_gather | solution.py:298
  10.3 0.0 copy-done.4
  10.3 2.9 %shard_map.110 = (bf16[256,192]{1,0:T(8,128)(2,1)S(1)}, bf16[2,272,384]{2,1,0:T(8,128)(2,1)S(1)}, f32[256,1]{1,0:T(8,128)S(1)}) custom-call(bf16[576,384]{1,0:T(8,128)(2,1)S(1)} %all_gather.9.whole, bf16[768,384]{1,0:T(8,128)(2,1)} %wq_hbm.1, bf16[768,384]{1,0:T(8,128)(2,1)} %wk_hbm.1, bf16[768,384]{1,0:T(8,128)(2,1)} %wv_hbm.1, bf16[2,768]{1,0:T(2,128)(2,1)S(1)} %bitcast.7), custom_call_target="tpu_custom_call" | custom-call | flops 452984832 | bytes 3145728 | tf_op jit(solution)/shard_map/pallas_call | solution.py:254
  13.1 1.3 %collective-permute-start = (bf16[2,272,384]{2,1,0:T(8,128)(2,1)S(1)}, bf16[2,272,384]{2,1,0:T(8,128)(2,1)S(1)}, u32[]{:S(2)}, u32[]{:S(2)}) collective-permute-start(bf16[2,272,384]{2,1,0:T(8,128)(2,1)S(1)} %get-tuple-element.8.packed.own), channel_id=1, source_target_pairs={{0,4},{4,8},{8,12},{12,16},{16,20},{20,24},{24,28},{28,32},{32,36}... | collective-permute-start | bytes 1253384 | tf_op jit(solution)/shard_map/ppermute | solution.py:273
  14.4 7.5 %collective-permute-done.refs_0_ = bf16[2,272,384]{2,1,0:T(8,128)(2,1)S(1)} collective-permute-done((bf16[2,272,384]{2,1,0:T(8,128)(2,1)S(1)}, bf16[2,272,384]{2,1,0:T(8,128)(2,1)S(1)}, u32[]{:S(2)}, u32[]{:S(2)}) %collective-permute-start) | collective-permute-done | bytes 417824 | tf_op jit(solution)/shard_map/ppermute | solution.py:273
  21.9 1.3 %collective-permute-start.1 = (bf16[2,272,384]{2,1,0:T(8,128)(2,1)S(1)}, bf16[2,272,384]{2,1,0:T(8,128)(2,1)S(1)}, u32[]{:S(2)}, u32[]{:S(2)}) collective-permute-start(bf16[2,272,384]{2,1,0:T(8,128)(2,1)S(1)} %collective-permute-done.refs_0_), channel_id=1, source_target_pairs={{0,4},{4,8},{8,12},{12,16},{16,20},{20,24},{24,28},{28,32},{32,36}... | collective-permute-start | bytes 1253384 | tf_op jit(solution)/shard_map/ppermute | solution.py:273
  23.2 7.5 %collective-permute-done.1.refs_1_ = bf16[2,272,384]{2,1,0:T(8,128)(2,1)S(1)} collective-permute-done((bf16[2,272,384]{2,1,0:T(8,128)(2,1)S(1)}, bf16[2,272,384]{2,1,0:T(8,128)(2,1)S(1)}, u32[]{:S(2)}, u32[]{:S(2)}) %collective-permute-start.1) | collective-permute-done | bytes 417824 | tf_op jit(solution)/shard_map/ppermute | solution.py:273
  30.7 1.3 %collective-permute-start.2 = (bf16[2,272,384]{2,1,0:T(8,128)(2,1)S(1)}, bf16[2,272,384]{2,1,0:T(8,128)(2,1)S(1)}, u32[]{:S(2)}, u32[]{:S(2)}) collective-permute-start(bf16[2,272,384]{2,1,0:T(8,128)(2,1)S(1)} %collective-permute-done.1.refs_1_), channel_id=1, source_target_pairs={{0,4},{4,8},{8,12},{12,16},{16,20},{20,24},{24,28},{28,32},{32,36}... | collective-permute-start | bytes 1253384 | tf_op jit(solution)/shard_map/ppermute | solution.py:273
  32.0 1.6 %shard_map.111 = bf16[576,384]{1,0:T(8,128)(2,1)} custom-call(bf16[2,272,384]{2,1,0:T(8,128)(2,1)S(1)} %get-tuple-element.8.packed.own, f32[256,1]{1,0:T(8,128)S(1)} %get-tuple-element.9.rates, f32[2,192,384]{2,1,0:T(8,128)S(1)} %copy-done.1, f32[2,192,384]{2,1,0:T(8,128)S(1)} %copy-done.2, f32[2,192,384]{2,1,0:T(8,128)S(1)} %copy-done.3), custom_call_target="tpu_custom_call" | custom-call | flops 226492416 | bytes 3145728 | tf_op jit(solution)/shard_map/pallas_call | solution.py:254
  33.6 22.8 %all-to-all-start = ((bf16[8,72,384]{2,1,0:T(8,128)(2,1)}), bf16[8,72,384]{2,1,0:T(8,128)(2,1)S(1)}, u32[]{:S(2)}, u32[]{:S(2)}) async-start(bf16[8,72,384]{2,1,0:T(8,128)(2,1)} %bitcast.2), calls=%async_computation | async-start | bytes 884736 | tf_op jit(solution)/shard_map/all_to_all | solution.py:327
  56.4 0.0 collective-permute-done.2.refs_2_
  56.4 1.3 %collective-permute-start.3 = (bf16[2,272,384]{2,1,0:T(8,128)(2,1)S(1)}, bf16[2,272,384]{2,1,0:T(8,128)(2,1)S(1)}, u32[]{:S(2)}, u32[]{:S(2)}) collective-permute-start(bf16[2,272,384]{2,1,0:T(8,128)(2,1)S(1)} %collective-permute-done.2.refs_2_), channel_id=1, source_target_pairs={{0,4},{4,8},{8,12},{12,16},{16,20},{20,24},{24,28},{28,32},{32,36}... | collective-permute-start | bytes 1253384 | tf_op jit(solution)/shard_map/ppermute | solution.py:273
  57.7 7.1 %all-to-all-done.got = bf16[8,72,384]{2,1,0:T(8,128)(2,1)S(1)} async-done(((bf16[8,72,384]{2,1,0:T(8,128)(2,1)}), bf16[8,72,384]{2,1,0:T(8,128)(2,1)S(1)}, u32[]{:S(2)}, u32[]{:S(2)}) %all-to-all-start) | async-done | bytes 442400 | tf_op jit(solution)/shard_map/all_to_all | solution.py:327
  64.9 0.9 shard_map.112
  65.7 3.8 %all-to-all-start.1 = ((bf16[8,72,384]{2,1,0:T(8,128)(2,1)}), bf16[8,72,384]{2,1,0:T(8,128)(2,1)S(1)}, u32[]{:S(2)}, u32[]{:S(2)}) async-start(bf16[8,72,384]{2,1,0:T(8,128)(2,1)} %shard_map.112), calls=%async_computation.1 | async-start | bytes 884736 | tf_op jit(solution)/shard_map/all_to_all | solution.py:329
  69.5 0.0 collective-permute-done.3.refs_3_
  69.5 1.0 shard_map.114
  70.6 0.8 collective-permute-start.4
  71.4 14.3 %all-to-all-done.1.got = bf16[8,72,384]{2,1,0:T(8,128)(2,1)S(1)} async-done(((bf16[8,72,384]{2,1,0:T(8,128)(2,1)}), bf16[8,72,384]{2,1,0:T(8,128)(2,1)S(1)}, u32[]{:S(2)}, u32[]{:S(2)}) %all-to-all-start.1) | async-done | bytes 442400 | tf_op jit(solution)/shard_map/all_to_all | solution.py:329
  85.7 0.9 shard_map.113
  86.6 4.1 %all-to-all-start.2 = ((bf16[8,72,384]{2,1,0:T(8,128)(2,1)}), bf16[8,72,384]{2,1,0:T(8,128)(2,1)S(1)}, u32[]{:S(2)}, u32[]{:S(2)}) async-start(bf16[8,72,384]{2,1,0:T(8,128)(2,1)} %shard_map.113), calls=%async_computation.2 | async-start | bytes 884736 | tf_op jit(solution)/shard_map/all_to_all | solution.py:331
  90.7 0.7 constant_dynamic-slice_fusion
  91.4 0.9 collective-permute-start.5
  92.4 0.0 collective-permute-done.4.refs_4_
  92.4 4.1 %shard_map.115.attended_hbm = f32[256,192]{1,0:T(8,128)} custom-call(bf16[256,192]{1,0:T(8,128)(2,1)S(1)} %get-tuple-element.10.query_ref.query_hbm, bf16[2,272,384]{2,1,0:T(8,128)(2,1)S(1)} %get-tuple-element.8.packed.own, bf16[2,272,384]{2,1,0:T(8,128)(2,1)S(1)} %collective-permute-done.refs_0_, bf16[2,272,384]{2,1,0:T(8,128)(2,1)S(1)} %collective-permute-done.1.refs_1_, ...), custom_call_target="tpu_custom_call" | custom-call | flops 603979776 | bytes 3145728 | tf_op jit(solution)/shard_map/pallas_call | solution.py:254
  96.5 3.8 %all-to-all-done.2 = bf16[8,72,384]{2,1,0:T(8,128)(2,1)S(1)} async-done(((bf16[8,72,384]{2,1,0:T(8,128)(2,1)}), bf16[8,72,384]{2,1,0:T(8,128)(2,1)S(1)}, u32[]{:S(2)}, u32[]{:S(2)}) %all-to-all-start.2) | async-done | bytes 442400 | tf_op jit(solution)/shard_map/all_to_all | solution.py:331
  100.3 6.4 %shard_map.116 = bf16[256,192]{1,0:T(8,128)(2,1)S(1)} custom-call(bf16[576,384]{1,0:T(8,128)(2,1)S(1)} %bitcast.6, f32[2,192,384]{2,1,0:T(8,128)} %gate_hbm.1, f32[2,192,384]{2,1,0:T(8,128)} %up_hbm.1, f32[2,192,384]{2,1,0:T(8,128)} %down_hbm.1, f32[2]{0:T(128)} %step_hbm.1, bf16[256,192]{1,0:T(8,128)(2,1)S(1)} %get-tuple-element.10.query_ref.query_hbm, ...), custom_call_target="tpu_custom_call" | custom-call | flops 10000000000 | bytes 3145728 | tf_op jit(solution)/shard_map/pallas_call | solution.py:254
  106.7 8.4 %all-gather = bf16[1024,192]{1,0:T(8,128)(2,1)S(1)} all-gather(bf16[256,192]{1,0:T(8,128)(2,1)S(1)} %shard_map.116), channel_id=2, replica_groups=mesh['xh'=2,'y'=4,'z'=8,'core'=2,'xl'=2] {'xl','core'}, dimensions={0}, use_global_device_ids=true | all-gather | bytes 491520 | tf_op jit(solution)/shard_map/all_gather | solution.py:367
  115.2 0.0 collective-permute-done.5.other
  115.2 1.0 shard_map.117
  (8 shorter events, 0.0 us)
Async XLA Ops:
  0.9 9.3 %copy-start.4 = (bf16[768,2]{0,1:T(2,128)(2,1)S(1)}, bf16[768,2]{0,1:T(2,128)(2,1)}, u32[]{:S(2)}) copy-start(bf16[768,2]{0,1:T(2,128)(2,1)} %param.17) | copy-start | bytes 9220
  10.3 21.7 %copy-start.1 = (f32[2,192,384]{2,1,0:T(8,128)S(1)}, f32[2,192,384]{2,1,0:T(8,128)}, u32[]{:S(2)}) copy-start(f32[2,192,384]{2,1,0:T(8,128)} %gate_hbm.1) | copy-start | bytes 1769476
  10.3 21.7 %copy-start.2 = (f32[2,192,384]{2,1,0:T(8,128)S(1)}, f32[2,192,384]{2,1,0:T(8,128)}, u32[]{:S(2)}) copy-start(f32[2,192,384]{2,1,0:T(8,128)} %up_hbm.1) | copy-start | bytes 1769476
  10.3 21.7 %copy-start.3 = (f32[2,192,384]{2,1,0:T(8,128)S(1)}, f32[2,192,384]{2,1,0:T(8,128)}, u32[]{:S(2)}) copy-start(f32[2,192,384]{2,1,0:T(8,128)} %down_hbm.1) | copy-start | bytes 1769476
  13.1 8.8 %collective-permute-start = (bf16[2,272,384]{2,1,0:T(8,128)(2,1)S(1)}, bf16[2,272,384]{2,1,0:T(8,128)(2,1)S(1)}, u32[]{:S(2)}, u32[]{:S(2)}) collective-permute-start(bf16[2,272,384]{2,1,0:T(8,128)(2,1)S(1)} %get-tuple-element.8.packed.own), channel_id=1, source_target_pairs={{0,4},{4,8},{8,12},{12,16},{16,20},{20,24},{24,28},{28,32},{32,36}... | collective-permute-start | bytes 1253384 | tf_op jit(solution)/shard_map/ppermute | solution.py:273
  21.9 8.8 %collective-permute-start.1 = (bf16[2,272,384]{2,1,0:T(8,128)(2,1)S(1)}, bf16[2,272,384]{2,1,0:T(8,128)(2,1)S(1)}, u32[]{:S(2)}, u32[]{:S(2)}) collective-permute-start(bf16[2,272,384]{2,1,0:T(8,128)(2,1)S(1)} %collective-permute-done.refs_0_), channel_id=1, source_target_pairs={{0,4},{4,8},{8,12},{12,16},{16,20},{20,24},{24,28},{28,32},{32,36}... | collective-permute-start | bytes 1253384 | tf_op jit(solution)/shard_map/ppermute | solution.py:273
  30.7 25.7 %collective-permute-start.2 = (bf16[2,272,384]{2,1,0:T(8,128)(2,1)S(1)}, bf16[2,272,384]{2,1,0:T(8,128)(2,1)S(1)}, u32[]{:S(2)}, u32[]{:S(2)}) collective-permute-start(bf16[2,272,384]{2,1,0:T(8,128)(2,1)S(1)} %collective-permute-done.1.refs_1_), channel_id=1, source_target_pairs={{0,4},{4,8},{8,12},{12,16},{16,20},{20,24},{24,28},{28,32},{32,36}... | collective-permute-start | bytes 1253384 | tf_op jit(solution)/shard_map/ppermute | solution.py:273
  33.6 31.3 %all-to-all-start = ((bf16[8,72,384]{2,1,0:T(8,128)(2,1)}), bf16[8,72,384]{2,1,0:T(8,128)(2,1)S(1)}, u32[]{:S(2)}, u32[]{:S(2)}) async-start(bf16[8,72,384]{2,1,0:T(8,128)(2,1)} %bitcast.2), calls=%async_computation | async-start | bytes 884736 | tf_op jit(solution)/shard_map/all_to_all | solution.py:327
  56.4 13.1 %collective-permute-start.3 = (bf16[2,272,384]{2,1,0:T(8,128)(2,1)S(1)}, bf16[2,272,384]{2,1,0:T(8,128)(2,1)S(1)}, u32[]{:S(2)}, u32[]{:S(2)}) collective-permute-start(bf16[2,272,384]{2,1,0:T(8,128)(2,1)S(1)} %collective-permute-done.2.refs_2_), channel_id=1, source_target_pairs={{0,4},{4,8},{8,12},{12,16},{16,20},{20,24},{24,28},{28,32},{32,36}... | collective-permute-start | bytes 1253384 | tf_op jit(solution)/shard_map/ppermute | solution.py:273
  65.7 20.0 %all-to-all-start.1 = ((bf16[8,72,384]{2,1,0:T(8,128)(2,1)}), bf16[8,72,384]{2,1,0:T(8,128)(2,1)S(1)}, u32[]{:S(2)}, u32[]{:S(2)}) async-start(bf16[8,72,384]{2,1,0:T(8,128)(2,1)} %shard_map.112), calls=%async_computation.1 | async-start | bytes 884736 | tf_op jit(solution)/shard_map/all_to_all | solution.py:329
  70.6 21.8 %collective-permute-start.4 = (bf16[4,272,384]{2,1,0:T(8,128)(2,1)}, bf16[4,272,384]{2,1,0:T(8,128)(2,1)}, u32[]{:S(2)}, u32[]{:S(2)}) collective-permute-start(bf16[4,272,384]{2,1,0:T(8,128)(2,1)} %shard_map.114), channel_id=1, source_target_pairs={{0,2},{2,0},{1,3},{3,1},{4,6},{6,4},{5,7},{7,5},{8,10},{10,8},{9,1... | collective-permute-start | bytes 2506760 | tf_op jit(solution)/shard_map/ppermute | solution.py:335
  86.6 4.1 %copy-start = (bf16[384,768]{1,0:T(8,128)(2,1)S(1)}, bf16[384,768]{1,0:T(8,128)(2,1)}, u32[]{:S(2)}) copy-start(bf16[384,768]{1,0:T(8,128)(2,1)} %weight.1) | copy-start | bytes 1769476
  86.6 13.8 %all-to-all-start.2 = ((bf16[8,72,384]{2,1,0:T(8,128)(2,1)}), bf16[8,72,384]{2,1,0:T(8,128)(2,1)S(1)}, u32[]{:S(2)}, u32[]{:S(2)}) async-start(bf16[8,72,384]{2,1,0:T(8,128)(2,1)} %shard_map.113), calls=%async_computation.2 | async-start | bytes 884736 | tf_op jit(solution)/shard_map/all_to_all | solution.py:331
  91.4 23.7 %collective-permute-start.5 = (bf16[384,384]{1,0:T(8,128)(2,1)}, bf16[384,384]{1,0:T(8,128)(2,1)S(1)}, u32[]{:S(2)}, u32[]{:S(2)}) collective-permute-start(bf16[384,384]{1,0:T(8,128)(2,1)} %constant_dynamic-slice_fusion), channel_id=1, source_target_pairs={{0,1},{1,0},{2,3},{3,2},{4,5},{5,4},{6,7},{7,6},{8,9},{9,8},{10,11... | collective-permute-start | bytes 884744 | tf_op jit(solution)/shard_map/ppermute | solution.py:366

commit v4 on v2

--- a/solution.py
+++ b/solution.py
@@ -25,6 +25,8 @@
 TAGS = 32
 f32 = jnp.float32
 bf16 = jnp.bfloat16
+ANY = pl.BlockSpec(memory_space=pl.ANY)
+HBM = pl.BlockSpec(memory_space=pltpu.HBM)
 VMEM = pl.BlockSpec(memory_space=pltpu.VMEM)
 SMEM = pl.BlockSpec(memory_space=pltpu.SMEM)
 
@@ -50,6 +52,32 @@
 
 def tn(a, b):
     return lax.dot_general(a, b, (((0,), (0,)), ((), ())), preferred_element_type=f32)
+
+
+def copies(sem, *pairs):
+    started = [
+        pltpu.make_async_copy(source, target, sem.at[i]) for i, (source, target) in enumerate(pairs)
+    ]
+    for copy in started:
+        copy.start()
+    return started
+
+
+def tag_kernel(tokens, views_hbm, wq_hbm, wk_hbm, wv_hbm, tagged_ref, wq, wk, wv, views, sem):
+    fetches = copies(
+        sem,
+        (views_hbm, views),
+        (tokens, tagged_ref.at[pl.ds(0, TOK_DEV)]),
+        (wq_hbm, wq),
+        (wk_hbm, wk),
+        (wv_hbm, wv),
+    )
+    fetches[0].wait()
+    row = (views[...] + 1).astype(f32).astype(bf16)
+    row = jnp.concatenate((row, jnp.zeros((1, FH - TOK_DEV), bf16)), 1)
+    tagged_ref[TOK_DEV:] = jnp.broadcast_to(row, (16, FH))
+    for fetch in fetches[1:]:
+        fetch.wait()
 
 
 def project_kernel(whole, wq, wk, wv, wr, query_ref, packed_ref, rates_ref):
@@ -62,6 +90,13 @@
     right = jnp.concatenate(
         (whole[base : base + TOK_DEV], whole[base + GATHERED : base + GATHERED + TOK_DEV]), 0
     )
+    both_rates = jax.nn.softplus(nt(left, wr[:, :FH]) + nt(right, wr[:, FH:]))
+    rates = jnp.where(core == 0, both_rates[:, :1], both_rates[:, 1:])
+    rates_ref[...] = rates * jnp.where(chip < 48, 1.0, 0.0)
+    tags = jnp.concatenate(
+        (whole[TOK_DEV:GATHERED, :TOK_DEV], whole[GATHERED + TOK_DEV : base, :TOK_DEV]), 1
+    )
+    tags = jnp.concatenate((tags, jnp.zeros((16, FH - ROWS), bf16)), 1)
 
     def both(w):
         return nn(left, w[:FH]) + nn(right, w[FH:])
@@ -70,15 +105,9 @@
         product = both(w)
         return jnp.where(core == 0, product[:, :DH], product[:, DH:]).astype(bf16)
 
+    packed_ref[:ROWS] = jnp.concatenate((own(wk), own(wv)), 1)
+    packed_ref[ROWS:] = tags
     query_ref[...] = own(wq)
-    packed_ref[:ROWS] = jnp.concatenate((own(wk), own(wv)), 1)
-    tags = jnp.concatenate(
-        (whole[TOK_DEV:GATHERED, :TOK_DEV], whole[GATHERED + TOK_DEV : base, :TOK_DEV]), 1
-    )
-    packed_ref[ROWS:] = jnp.concatenate((tags, jnp.zeros((16, FH - ROWS), bf16)), 1)
-    both_rates = jax.nn.softplus(nt(left, wr[:, :FH]) + nt(right, wr[:, FH:]))
-    rates = jnp.where(core == 0, both_rates[:, :1], both_rates[:, 1:])
-    rates_ref[...] = rates * jnp.where(chip < 48, 1.0, 0.0)
 
 
 def gradient_kernel(packed, rates, gate_ref, up_ref, down_ref, sent_ref):
@@ -108,8 +137,8 @@
         sent_ref[i] = part
 
 
-def attend_kernel(query_ref, *refs):
-    pieces, attended_ref, scores_ref = refs[:-2], refs[-2], refs[-1]
+def blend_kernel(query_ref, fresh, *refs):
+    pieces, mixed_ref, scores_ref = refs[: 2 * REACH + 1], refs[-2], refs[-1]
     query = query_ref[...]
     numbers = lax.broadcasted_iota(jnp.int32, (TAGS, ROWS), 0).astype(f32)
 
@@ -137,12 +166,22 @@
         weights = (scores_ref[:, p * ROWS : (p + 1) * ROWS] * inverse).astype(bf16)
         one = nn(weights, piece[:ROWS, DH:])
         total = one if total is None else total + one
-    attended_ref[...] = total
-
-
-def fresh_kernel(total_ref, gate_ref, up_ref, down_ref, step_ref, query_ref, attended_ref, mixed_ref):
+    queries_n = normalize(query)
+    gate = nn(queries_n, fresh[0])
+    upward = nn(queries_n, fresh[1])
+    product = (gate * jax.nn.sigmoid(gate) * upward).astype(bf16)
+    mixed_ref[...] = (total + nt(product, fresh[2])).astype(bf16)
+
+
+def fresh_kernel(total_ref, gate_hbm, up_hbm, down_hbm, step_hbm, fresh_ref, masters, step_ref, sem):
     core = lax.axis_index("core")
-    step = step_ref[core]
+    fetches = copies(
+        sem,
+        (gate_hbm.at[core], masters.at[0]),
+        (up_hbm.at[core], masters.at[1]),
+        (down_hbm.at[core], masters.at[2]),
+        (step_hbm, step_ref),
+    )
     currents = []
     for m in range(3):
         matrix = total_ref[m * DH : (m + 1) * DH].astype(f32)
@@ -152,26 +191,25 @@
         squares = []
         for x in currents:
             h, l = halves(x)
-            squares.append((h, l, nt(h, h) + (nt(h, l) + nt(l, h))))
+            cross = nt(h, l)
+            squares.append((h, l, nt(h, h) + (cross + cross.T)))
         mixers = []
         for h, l, a in squares:
             ah, al = halves(a)
-            aa = nn(ah, ah) + (nn(ah, al) + nn(al, ah))
+            cross = nt(ah, al)
+            aa = nt(ah, ah) + (cross + cross.T)
             mixers.append((h, l, newton_b * a + newton_c * aa))
         nexts = []
         for x, (h, l, b) in zip(currents, mixers):
             bh, bl = halves(b)
-            nexts.append(newton_a * x + (nn(bh, h) + (nn(bh, l) + nn(bl, h))))
+            wide = nn(bh, jnp.concatenate((h, l), 1))
+            nexts.append(newton_a * x + (wide[:, :FH] + (wide[:, FH:] + nn(bl, h))))
         currents = nexts
-    fresh = [
-        (master[core] - step * ortho).astype(bf16)
-        for master, ortho in zip((gate_ref, up_ref, down_ref), currents)
-    ]
-    queries_n = normalize(query_ref[...])
-    gate = nn(queries_n, fresh[0])
-    upward = nn(queries_n, fresh[1])
-    product = (gate * jax.nn.sigmoid(gate) * upward).astype(bf16)
-    mixed_ref[...] = (attended_ref[...] + nt(product, fresh[2])).astype(bf16)
+    for fetch in fetches:
+        fetch.wait()
+    step = step_ref[core]
+    for m in range(3):
+        fresh_ref[m] = (masters[m] - step * currents[m]).astype(bf16)
 
 
 def out_kernel(spread, weight, other, out_ref):
@@ -186,13 +224,17 @@
     out_ref[...] = total.astype(bf16)
 
 
-def call(kernel, shapes, args, specs=None, scratch=(), flops=0, bytes_accessed=0, room=12):
+def call(kernel, shapes, args, specs=None, outs=None, scratch=(), flops=0, bytes_accessed=0, room=12):
     several = isinstance(shapes, (list, tuple))
+    args = [
+        pltpu.with_memory_space_constraint(arg, pltpu.HBM) if spec is HBM else arg
+        for arg, spec in zip(args, specs or [VMEM] * len(args))
+    ]
     return pl.pallas_call(
         kernel,
         out_shape=shapes,
         in_specs=specs or [VMEM] * len(args),
-        out_specs=[VMEM] * len(shapes) if several else VMEM,
+        out_specs=outs or ([VMEM] * len(shapes) if several else VMEM),
         scratch_shapes=list(scratch),
         cost_estimate=pl.CostEstimate(
             flops=flops, bytes_accessed=bytes_accessed, transcendentals=0
@@ -225,14 +267,19 @@
     step_size,
 ):
     xl = lax.axis_index("xl")
-    tag = jnp.pad((view_ids + 1).astype(bf16)[None], ((0, 15), (0, FH - TOK_DEV)))
-    whole = lax.all_gather(
-        jnp.concatenate((tokens, tag), 0), ("xl", "core"), axis=0, tiled=True
-    )
+    tagged, *weights = call(
+        tag_kernel,
+        [shape((GATHERED, FH), bf16)] + [shape((768, FH), bf16)] * 3,
+        (tokens, view_ids.reshape(1, TOK_DEV), query_weight, key_weight, value_weight),
+        specs=[HBM] * 5,
+        scratch=[pltpu.VMEM((1, TOK_DEV), jnp.int32), pltpu.SemaphoreType.DMA((5,))],
+        bytes_accessed=1 << 18,
+    )
+    whole = lax.all_gather(tagged, ("xl", "core"), axis=0, tiled=True)
     query, packed, rates = call(
         project_kernel,
         [shape((ROWS, DH), bf16), shape((PACKED, FH), bf16), shape((ROWS, 1), f32)],
-        (whole, query_weight, key_weight, value_weight, rate_weight.T),
+        (whole, *weights, rate_weight.T),
         flops=2 * 256 * 768 * 1152,
         bytes_accessed=3 << 20,
     )
@@ -261,20 +308,25 @@
     total = lax.all_to_all(sent, ("xh", "y"), 0, 0, tiled=True)
     total = total.reshape(3 * DH, FH)
 
-    attended = call(
-        attend_kernel,
-        shape((ROWS, DH), f32),
-        (query, *pieces),
+    fresh = call(
+        fresh_kernel,
+        shape((3, DH, FH), bf16),
+        (total, fast_gate, fast_up, fast_down, step_size),
+        specs=[VMEM] + [HBM] * 4,
+        scratch=[
+            pltpu.VMEM((3, DH, FH), f32),
+            pltpu.SMEM((2,), f32),
+            pltpu.SemaphoreType.DMA((4,)),
+        ],
+        flops=10**10,
+        bytes_accessed=3 << 20,
+    )
+    mixed = call(
+        blend_kernel,
+        shape((ROWS, DH), bf16),
+        (query, fresh, *pieces),
         scratch=[pltpu.VMEM((ROWS, len(pieces) * ROWS), f32)],
         flops=4 * 256 * 2304 * 256,
-        bytes_accessed=3 << 20,
-    )
-    mixed = call(
-        fresh_kernel,
-        shape((ROWS, DH), bf16),
-        (total, fast_gate, fast_up, fast_down, step_size, query, attended),
-        specs=[VMEM] * 4 + [SMEM] + [VMEM] * 2,
-        flops=10**10,
         bytes_accessed=3 << 20,
     )
 
@@ -305,6 +357,4 @@
         P("xl", None, None),
         P("xl"),
     )
-    return jax.shard_map(
-        layer, mesh=fine, in_specs=placed, out_specs=P(TOK, "xl"), check_vma=False
-    )
+    return jax.shard_map(layer, mesh=fine, in_specs=placed, out_specs=P(TOK, "xl"), check_vma=False)

time: 126 us -> 115 us (0.913)
  local copies, waits for them, and re-layouts: 6.78 us -> 1.74 us
  waiting for transfers between devices: 10.9 us -> 8.19 us
  other arithmetic: 1.62 us -> 0 us
  Pallas kernels: 15.7 us -> 14.4 us
    unnamed x36 -> x10, local copies, waits for them, and re-layouts: 6.04 us -> 0.99 us
    ppermute x8, waiting for transfers between devices: 10.8 us -> 8.18 us  [hop(): lax.ppermute(x, CHIPS, [(i, i + steps) for i in range(64) if 0 <= i + ste...]
    pallas_call x7 -> x8, Pallas kernels: 15.7 us -> 14.4 us  [call(): pl.pallas_call(kernel, out_shape=shapes, in_specs=specs or [VMEM] * len(a...]
  transfers between devices with their start and end apart: 11 -> 11, of which waited for: 3 -> 1; matrix products, arithmetic and copies ran while one was open for 1% -> 1% of each run, Pallas kernels for 10% -> 8%
where the time goes in v4:
time: 115 us; the launch traced here: 114 us
  starting transfers between devices  57.3 us (50%)
  blocking collectives  32.2 us (28%)
  Pallas kernels  14.4 us (13%)
  waiting for transfers between devices  8.19 us (7%)
  local copies, waits for them, and re-layouts  1.74 us (2%)
    ppermute x8, starting transfers between devices, hop(): lax.ppermute(x, CHIPS, [(i, i + steps) for i in range(64) if 0 <= i + ste...  44 us
    pallas_call x8, Pallas kernels, call(): pl.pallas_call(kernel, out_shape=shapes, in_specs=specs or [VMEM] * len(a...  14.4 us
    all_to_all x1, blocking collectives, layer(): got = lax.all_to_all(sent, ('xh', 'y'), 0, 0, tiled=True)  14.1 us
    all_gather x1, blocking collectives, layer(): spread = lax.all_gather(mixed, ('xl', 'core'), axis=0)  11.1 us
    all_to_all x1, starting transfers between devices, layer(): got = lax.all_to_all(sent, 'z', 0, 0, tiled=True)  8.19 us
    ppermute x8, waiting for transfers between devices, hop(): lax.ppermute(x, CHIPS, [(i, i + steps) for i in range(64) if 0 <= i + ste...  8.18 us
    all_gather x1, blocking collectives, layer(): whole = lax.all_gather(tagged, ('xl', 'core'), axis=0, tiled=True)  6.94 us
    all_to_all x1, starting transfers between devices, layer(): total = lax.all_to_all(sent, ('xh', 'y'), 0, 0, tiled=True)  4.37 us
  transfers between devices with their start and end apart: 11, of which 1 were waited for; matrix products, arithmetic and copies ran while one was open for 1% of the time, Pallas kernels for 8%

profile of v4, /device:TPU:5, one launch (start us, length us, event | category | flops | bytes accessed | tf_op | source)
XLA Modules:
  0.0 114.1 jit_solution(12301748266166082259)
XLA Ops:
  0.0 1.5 %shard_map.109 = (bf16[144,384]{1,0:T(8,128)(2,1)S(1)}, bf16[768,384]{1,0:T(8,128)(2,1)S(1)}, bf16[768,384]{1,0:T(8,128)(2,1)S(1)}, bf16[768,384]{1,0:T(8,128)(2,1)S(1)}) custom-call(bf16[128,384]{1,0:T(8,128)(2,1)} %tokens.1, s32[1,128]{1,0:T(1,128)} %bitcast.9, bf16[768,384]{1,0:T(8,128)(2,1)} %wq_hbm.1, bf16[768,384]{1,0:T(8,128)(2,1)} %wk_hbm.1, ...), custom_call_target="tpu_custom_call" | custom-call | bytes 262144 | tf_op jit(solution)/shard_map/pallas_call | solution.py:233
  1.5 6.9 %all_gather.9.whole = bf16[576,384]{1,0:T(8,128)(2,1)S(1)} all-gather(bf16[144,384]{1,0:T(8,128)(2,1)S(1)} %get-tuple-element.12), channel_id=1, replica_groups=mesh['xh'=2,'y'=4,'z'=8,'core'=2,'xl'=2] {'xl','core'}, dimensions={0}, use_global_device_ids=true | all-gather | bytes 552960 | tf_op jit(solution)/shard_map/all_gather | solution.py:278
  8.5 0.7 copy-done.4
  9.2 1.1 shard_map.110
  10.3 0.1 copy-done.2
  10.4 0.2 copy-done.3
  10.6 0.8 shard_map.111
  11.4 14.1 %all_to_all.15.got = bf16[8,72,384]{2,1,0:T(8,128)(2,1)S(1)} all-to-all(bf16[8,72,384]{2,1,0:T(8,128)(2,1)S(1)} %bitcast.6), channel_id=1, replica_groups=mesh['xh'=2,'y'=4,'z'=8,'core'=2,'xl'=2] {'xh','y'}, dimensions={0} | all-to-all | bytes 884736 | tf_op jit(solution)/shard_map/all_to_all | solution.py:304
  25.6 0.8 shard_map.112
  26.4 8.2 %all-to-all-start.1 = ((bf16[8,72,384]{2,1,0:T(8,128)(2,1)}), bf16[8,72,384]{2,1,0:T(8,128)(2,1)S(1)}, u32[]{:S(2)}, u32[]{:S(2)}) async-start(bf16[8,72,384]{2,1,0:T(8,128)(2,1)} %shard_map.112), calls=%async_computation.1 | async-start | bytes 884736 | tf_op jit(solution)/shard_map/all_to_all | solution.py:306
  34.6 3.4 %collective-permute-start = (bf16[272,384]{1,0:T(8,128)(2,1)S(1)}, bf16[272,384]{1,0:T(8,128)(2,1)S(1)}, u32[]{:S(2)}, u32[]{:S(2)}) collective-permute-start(bf16[272,384]{1,0:T(8,128)(2,1)S(1)} %get-tuple-element.17.packed.refs_0_), channel_id=1, source_target_pairs={{0,4},{4,8},{8,12},{12,16},{16,20},{20,24},{24,28},{28,32},{32,36}... | collective-permute-start | bytes 626696 | tf_op jit(solution)/shard_map/ppermute | solution.py:251
  37.9 7.6 %collective-permute-start.1 = (bf16[272,384]{1,0:T(8,128)(2,1)S(1)}, bf16[272,384]{1,0:T(8,128)(2,1)S(1)}, u32[]{:S(2)}, u32[]{:S(2)}) collective-permute-start(bf16[272,384]{1,0:T(8,128)(2,1)S(1)} %get-tuple-element.17.packed.refs_0_), channel_id=1, source_target_pairs={{4,0},{8,4},{12,8},{16,12},{20,16},{24,20},{28,24},{32,28},{36,32}... | collective-permute-start | bytes 626696 | tf_op jit(solution)/shard_map/ppermute | solution.py:251
  45.6 8.2 %collective-permute-done.refs_1_ = bf16[272,384]{1,0:T(8,128)(2,1)S(1)} collective-permute-done((bf16[272,384]{1,0:T(8,128)(2,1)S(1)}, bf16[272,384]{1,0:T(8,128)(2,1)S(1)}, u32[]{:S(2)}, u32[]{:S(2)}) %collective-permute-start) | collective-permute-done | bytes 208928 | tf_op jit(solution)/shard_map/ppermute | solution.py:251
  53.8 1.9 %collective-permute-start.2 = (bf16[272,384]{1,0:T(8,128)(2,1)S(1)}, bf16[272,384]{1,0:T(8,128)(2,1)S(1)}, u32[]{:S(2)}, u32[]{:S(2)}) collective-permute-start(bf16[272,384]{1,0:T(8,128)(2,1)S(1)} %collective-permute-done.refs_1_), channel_id=1, source_target_pairs={{0,4},{4,8},{8,12},{12,16},{16,20},{20,24},{24,28},{28,32},{32,36}... | collective-permute-start | bytes 626696 | tf_op jit(solution)/shard_map/ppermute | solution.py:251
  55.7 0.0 collective-permute-done.1.refs_2_
  55.7 9.1 %collective-permute-start.3 = (bf16[272,384]{1,0:T(8,128)(2,1)S(1)}, bf16[272,384]{1,0:T(8,128)(2,1)S(1)}, u32[]{:S(2)}, u32[]{:S(2)}) collective-permute-start(bf16[272,384]{1,0:T(8,128)(2,1)S(1)} %collective-permute-done.1.refs_2_), channel_id=1, source_target_pairs={{4,0},{8,4},{12,8},{16,12},{20,16},{24,20},{28,24},{32,28},{36,32}... | collective-permute-start | bytes 626696 | tf_op jit(solution)/shard_map/ppermute | solution.py:251
  64.8 0.8 shard_map.113
  65.6 4.4 %all-to-all-start.2 = ((bf16[8,72,384]{2,1,0:T(8,128)(2,1)}), bf16[8,72,384]{2,1,0:T(8,128)(2,1)S(1)}, u32[]{:S(2)}, u32[]{:S(2)}) async-start(bf16[8,72,384]{2,1,0:T(8,128)(2,1)} %shard_map.113), calls=%async_computation.2 | async-start | bytes 884736 | tf_op jit(solution)/shard_map/all_to_all | solution.py:308
  70.0 0.0 collective-permute-done.2.refs_3_
  70.0 1.9 %collective-permute-start.4 = (bf16[272,384]{1,0:T(8,128)(2,1)S(1)}, bf16[272,384]{1,0:T(8,128)(2,1)S(1)}, u32[]{:S(2)}, u32[]{:S(2)}) collective-permute-start(bf16[272,384]{1,0:T(8,128)(2,1)S(1)} %collective-permute-done.2.refs_3_), channel_id=1, source_target_pairs={{0,4},{4,8},{8,12},{12,16},{16,20},{20,24},{24,28},{28,32},{32,36}... | collective-permute-start | bytes 626696 | tf_op jit(solution)/shard_map/ppermute | solution.py:251
  71.9 9.1 %collective-permute-start.5 = (bf16[272,384]{1,0:T(8,128)(2,1)S(1)}, bf16[272,384]{1,0:T(8,128)(2,1)S(1)}, u32[]{:S(2)}, u32[]{:S(2)}) collective-permute-start(bf16[272,384]{1,0:T(8,128)(2,1)S(1)} %collective-permute-done.3.refs_4_), channel_id=1, source_target_pairs={{4,0},{8,4},{12,8},{16,12},{20,16},{24,20},{28,24},{32,28},{36,32}... | collective-permute-start | bytes 626696 | tf_op jit(solution)/shard_map/ppermute | solution.py:251
  81.0 0.8 constant_dynamic-slice_fusion
  81.8 0.8 collective-permute-start.8
  82.6 1.9 %collective-permute-start.6 = (bf16[272,384]{1,0:T(8,128)(2,1)S(1)}, bf16[272,384]{1,0:T(8,128)(2,1)S(1)}, u32[]{:S(2)}, u32[]{:S(2)}) collective-permute-start(bf16[272,384]{1,0:T(8,128)(2,1)S(1)} %collective-permute-done.4.refs_5_), channel_id=1, source_target_pairs={{0,4},{4,8},{8,12},{12,16},{16,20},{20,24},{24,28},{28,32},{32,36}... | collective-permute-start | bytes 626696 | tf_op jit(solution)/shard_map/ppermute | solution.py:251
  84.5 0.0 collective-permute-done.5.refs_6_
  84.5 9.1 %collective-permute-start.7 = (bf16[272,384]{1,0:T(8,128)(2,1)S(1)}, bf16[272,384]{1,0:T(8,128)(2,1)S(1)}, u32[]{:S(2)}, u32[]{:S(2)}) collective-permute-start(bf16[272,384]{1,0:T(8,128)(2,1)S(1)} %collective-permute-done.5.refs_6_), channel_id=1, source_target_pairs={{4,0},{8,4},{12,8},{16,12},{20,16},{24,20},{28,24},{32,28},{36,32}... | collective-permute-start | bytes 626696 | tf_op jit(solution)/shard_map/ppermute | solution.py:251
  93.6 0.0 all-to-all-done.2
  93.6 5.8 %shard_map.114.fresh = bf16[3,192,384]{2,1,0:T(8,128)(2,1)S(1)} custom-call(bf16[576,384]{1,0:T(8,128)(2,1)S(1)} %bitcast.7, f32[2,192,384]{2,1,0:T(8,128)} %gate_hbm.1, f32[2,192,384]{2,1,0:T(8,128)} %up_hbm.1, f32[2,192,384]{2,1,0:T(8,128)} %down_hbm.1, f32[2]{0:T(128)} %step_hbm.1), custom_call_target="tpu_custom_call" | custom-call | flops 10000000000 | bytes 3145728 | tf_op jit(solution)/shard_map/pallas_call | solution.py:233
  99.5 0.0 collective-permute-done.6.refs_7_
  99.5 2.5 %shard_map.115 = bf16[256,192]{1,0:T(8,128)(2,1)S(1)} custom-call(bf16[256,192]{1,0:T(8,128)(2,1)S(1)} %get-tuple-element.16.query_ref, bf16[3,192,384]{2,1,0:T(8,128)(2,1)S(1)} %shard_map.114.fresh, bf16[272,384]{1,0:T(8,128)(2,1)S(1)} %get-tuple-element.17.packed.refs_0_, bf16[272,384]{1,0:T(8,128)(2,1)S(1)} %collective-permute-done.refs_1_, ...), custom_call_target="tpu_custom_call" | custom-call | flops 603979776 | bytes 3145728 | tf_op jit(solution)/shard_map/pallas_call | solution.py:233
  102.0 11.1 %all-gather = bf16[1024,192]{1,0:T(8,128)(2,1)S(1)} all-gather(bf16[256,192]{1,0:T(8,128)(2,1)S(1)} %shard_map.115), channel_id=2, replica_groups=mesh['xh'=2,'y'=4,'z'=8,'core'=2,'xl'=2] {'xl','core'}, dimensions={0}, use_global_device_ids=true | all-gather | bytes 491520 | tf_op jit(solution)/shard_map/all_gather | solution.py:335
  113.1 0.9 shard_map.116
  (12 shorter events, 0.0 us)
Async XLA Ops:
  8.5 0.7 copy-start.4
  9.2 1.1 copy-start.1
  9.2 1.2 %copy-start.2 = (f32[2,192,384]{2,1,0:T(8,128)S(1)}, f32[2,192,384]{2,1,0:T(8,128)}, u32[]{:S(2)}) copy-start(f32[2,192,384]{2,1,0:T(8,128)} %up_hbm.1) | copy-start | bytes 1769476
  9.2 1.4 %copy-start.3 = (f32[2,192,384]{2,1,0:T(8,128)S(1)}, f32[2,192,384]{2,1,0:T(8,128)}, u32[]{:S(2)}) copy-start(f32[2,192,384]{2,1,0:T(8,128)} %down_hbm.1) | copy-start | bytes 1769476
  26.4 38.4 %all-to-all-start.1 = ((bf16[8,72,384]{2,1,0:T(8,128)(2,1)}), bf16[8,72,384]{2,1,0:T(8,128)(2,1)S(1)}, u32[]{:S(2)}, u32[]{:S(2)}) async-start(bf16[8,72,384]{2,1,0:T(8,128)(2,1)} %shard_map.112), calls=%async_computation.1 | async-start | bytes 884736 | tf_op jit(solution)/shard_map/all_to_all | solution.py:306
  34.6 19.2 %collective-permute-start = (bf16[272,384]{1,0:T(8,128)(2,1)S(1)}, bf16[272,384]{1,0:T(8,128)(2,1)S(1)}, u32[]{:S(2)}, u32[]{:S(2)}) collective-permute-start(bf16[272,384]{1,0:T(8,128)(2,1)S(1)} %get-tuple-element.17.packed.refs_0_), channel_id=1, source_target_pairs={{0,4},{4,8},{8,12},{12,16},{16,20},{20,24},{24,28},{28,32},{32,36}... | collective-permute-start | bytes 626696 | tf_op jit(solution)/shard_map/ppermute | solution.py:251
  37.9 17.7 %collective-permute-start.1 = (bf16[272,384]{1,0:T(8,128)(2,1)S(1)}, bf16[272,384]{1,0:T(8,128)(2,1)S(1)}, u32[]{:S(2)}, u32[]{:S(2)}) collective-permute-start(bf16[272,384]{1,0:T(8,128)(2,1)S(1)} %get-tuple-element.17.packed.refs_0_), channel_id=1, source_target_pairs={{4,0},{8,4},{12,8},{16,12},{20,16},{24,20},{28,24},{32,28},{36,32}... | collective-permute-start | bytes 626696 | tf_op jit(solution)/shard_map/ppermute | solution.py:251
  53.8 16.2 %collective-permute-start.2 = (bf16[272,384]{1,0:T(8,128)(2,1)S(1)}, bf16[272,384]{1,0:T(8,128)(2,1)S(1)}, u32[]{:S(2)}, u32[]{:S(2)}) collective-permute-start(bf16[272,384]{1,0:T(8,128)(2,1)S(1)} %collective-permute-done.refs_1_), channel_id=1, source_target_pairs={{0,4},{4,8},{8,12},{12,16},{16,20},{20,24},{24,28},{28,32},{32,36}... | collective-permute-start | bytes 626696 | tf_op jit(solution)/shard_map/ppermute | solution.py:251
  55.7 16.2 %collective-permute-start.3 = (bf16[272,384]{1,0:T(8,128)(2,1)S(1)}, bf16[272,384]{1,0:T(8,128)(2,1)S(1)}, u32[]{:S(2)}, u32[]{:S(2)}) collective-permute-start(bf16[272,384]{1,0:T(8,128)(2,1)S(1)} %collective-permute-done.1.refs_2_), channel_id=1, source_target_pairs={{4,0},{8,4},{12,8},{16,12},{20,16},{24,20},{28,24},{32,28},{36,32}... | collective-permute-start | bytes 626696 | tf_op jit(solution)/shard_map/ppermute | solution.py:251
  65.6 15.4 %copy-start = (bf16[384,768]{1,0:T(8,128)(2,1)S(1)}, bf16[384,768]{1,0:T(8,128)(2,1)}, u32[]{:S(2)}) copy-start(bf16[384,768]{1,0:T(8,128)(2,1)} %weight.1) | copy-start | bytes 1769476
  65.6 28.0 %all-to-all-start.2 = ((bf16[8,72,384]{2,1,0:T(8,128)(2,1)}), bf16[8,72,384]{2,1,0:T(8,128)(2,1)S(1)}, u32[]{:S(2)}, u32[]{:S(2)}) async-start(bf16[8,72,384]{2,1,0:T(8,128)(2,1)} %shard_map.113), calls=%async_computation.2 | async-start | bytes 884736 | tf_op jit(solution)/shard_map/all_to_all | solution.py:308
  70.0 12.6 %collective-permute-start.4 = (bf16[272,384]{1,0:T(8,128)(2,1)S(1)}, bf16[272,384]{1,0:T(8,128)(2,1)S(1)}, u32[]{:S(2)}, u32[]{:S(2)}) collective-permute-start(bf16[272,384]{1,0:T(8,128)(2,1)S(1)} %collective-permute-done.2.refs_3_), channel_id=1, source_target_pairs={{0,4},{4,8},{8,12},{12,16},{16,20},{20,24},{24,28},{28,32},{32,36}... | collective-permute-start | bytes 626696 | tf_op jit(solution)/shard_map/ppermute | solution.py:251
  71.9 12.6 %collective-permute-start.5 = (bf16[272,384]{1,0:T(8,128)(2,1)S(1)}, bf16[272,384]{1,0:T(8,128)(2,1)S(1)}, u32[]{:S(2)}, u32[]{:S(2)}) collective-permute-start(bf16[272,384]{1,0:T(8,128)(2,1)S(1)} %collective-permute-done.3.refs_4_), channel_id=1, source_target_pairs={{4,0},{8,4},{12,8},{16,12},{20,16},{24,20},{28,24},{32,28},{36,32}... | collective-permute-start | bytes 626696 | tf_op jit(solution)/shard_map/ppermute | solution.py:251
  81.8 31.4 %collective-permute-start.8 = (bf16[384,384]{1,0:T(8,128)(2,1)}, bf16[384,384]{1,0:T(8,128)(2,1)S(1)}, u32[]{:S(2)}, u32[]{:S(2)}) collective-permute-start(bf16[384,384]{1,0:T(8,128)(2,1)} %constant_dynamic-slice_fusion), channel_id=1, source_target_pairs={{0,1},{1,0},{2,3},{3,2},{4,5},{5,4},{6,7},{7,6},{8,9},{9,8},{10,11... | collective-permute-start | bytes 884744 | tf_op jit(solution)/shard_map/ppermute | solution.py:334
  82.6 16.9 %collective-permute-start.6 = (bf16[272,384]{1,0:T(8,128)(2,1)S(1)}, bf16[272,384]{1,0:T(8,128)(2,1)S(1)}, u32[]{:S(2)}, u32[]{:S(2)}) collective-permute-start(bf16[272,384]{1,0:T(8,128)(2,1)S(1)} %collective-permute-done.4.refs_5_), channel_id=1, source_target_pairs={{0,4},{4,8},{8,12},{12,16},{16,20},{20,24},{24,28},{28,32},{32,36}... | collective-permute-start | bytes 626696 | tf_op jit(solution)/shard_map/ppermute | solution.py:251
  84.5 14.9 %collective-permute-start.7 = (bf16[272,384]{1,0:T(8,128)(2,1)S(1)}, bf16[272,384]{1,0:T(8,128)(2,1)S(1)}, u32[]{:S(2)}, u32[]{:S(2)}) collective-permute-start(bf16[272,384]{1,0:T(8,128)(2,1)S(1)} %collective-permute-done.5.refs_6_), channel_id=1, source_target_pairs={{4,0},{8,4},{12,8},{16,12},{20,16},{24,20},{28,24},{32,28},{36,32}... | collective-permute-start | bytes 626696 | tf_op jit(solution)/shard_map/ppermute | solution.py:251

commit v5 on v4

--- a/solution.py
+++ b/solution.py
@@ -63,7 +63,11 @@
     return started
 
 
-def tag_kernel(tokens, views_hbm, wq_hbm, wk_hbm, wv_hbm, tagged_ref, wq, wk, wv, views, sem):
+def tag_kernel(
+    tokens, views_hbm, wq_hbm, wk_hbm, wv_hbm, wr_hbm, wo_hbm,
+    tagged_ref, wq, wk, wv, wr, theirs, views, sem,
+):
+    columns = pl.ds(pl.multiple_of((1 - lax.axis_index("xl")) * FH, FH), FH)
     fetches = copies(
         sem,
         (views_hbm, views),
@@ -71,6 +75,8 @@
         (wq_hbm, wq),
         (wk_hbm, wk),
         (wv_hbm, wv),
+        (wr_hbm, wr),
+        (wo_hbm.at[:, columns], theirs),
     )
     fetches[0].wait()
     row = (views[...] + 1).astype(f32).astype(bf16)
@@ -266,20 +272,29 @@
     fast_down,
     step_size,
 ):
-    xl = lax.axis_index("xl")
-    tagged, *weights = call(
+    tagged, *weights, theirs = call(
         tag_kernel,
-        [shape((GATHERED, FH), bf16)] + [shape((768, FH), bf16)] * 3,
-        (tokens, view_ids.reshape(1, TOK_DEV), query_weight, key_weight, value_weight),
-        specs=[HBM] * 5,
-        scratch=[pltpu.VMEM((1, TOK_DEV), jnp.int32), pltpu.SemaphoreType.DMA((5,))],
+        [shape((GATHERED, FH), bf16)]
+        + [shape((768, FH), bf16)] * 3
+        + [shape((2, 768), bf16), shape((FH, FH), bf16)],
+        (
+            tokens,
+            view_ids.reshape(1, TOK_DEV),
+            query_weight,
+            key_weight,
+            value_weight,
+            rate_weight.T,
+            out_weight,
+        ),
+        specs=[HBM] * 7,
+        scratch=[pltpu.VMEM((1, TOK_DEV), jnp.int32), pltpu.SemaphoreType.DMA((7,))],
         bytes_accessed=1 << 18,
     )
     whole = lax.all_gather(tagged, ("xl", "core"), axis=0, tiled=True)
     query, packed, rates = call(
         project_kernel,
         [shape((ROWS, DH), bf16), shape((PACKED, FH), bf16), shape((ROWS, 1), f32)],
-        (whole, *weights, rate_weight.T),
+        (whole, *weights),
         flops=2 * 256 * 768 * 1152,
         bytes_accessed=3 << 20,
     )
@@ -330,7 +345,6 @@
         bytes_accessed=3 << 20,
     )
 
-    theirs = lax.dynamic_slice_in_dim(out_weight, (1 - xl) * FH, FH, 1)
     other = lax.ppermute(theirs, "xl", [(0, 1), (1, 0)])
     spread = lax.all_gather(mixed, ("xl", "core"), axis=0)
     return call(
@@ -357,4 +371,6 @@
         P("xl", None, None),
         P("xl"),
     )
-    return jax.shard_map(layer, mesh=fine, in_specs=placed, out_specs=P(TOK, "xl"), check_vma=False)
+    return jax.shard_map(
+        layer, mesh=fine, in_specs=placed, out_specs=P(TOK, "xl"), check_vma=False
+    )

time: 115 us -> 114 us (level)
  local copies, waits for them, and re-layouts: 1.74 us -> 0.29 us
  transfers between devices with their start and end apart: 11 -> 11, of which waited for: 1 -> 2; matrix products, arithmetic and copies ran while one was open for 1% -> 0% of each run, Pallas kernels for 8% -> 8%
where the time goes in v5:
time: 114 us
  starting transfers between devices  57.4 us (50%)
  blocking collectives  32.6 us (29%)
  Pallas kernels  14.5 us (13%)
  waiting for transfers between devices  8.58 us (8%)
    ppermute x8, starting transfers between devices, hop(): lax.ppermute(x, CHIPS, [(i, i + steps) for i in range(64) if 0 <= i + ste...  44 us
    pallas_call x8, Pallas kernels, call(): pl.pallas_call(kernel, out_shape=shapes, in_specs=specs or [VMEM] * len(a...  14.5 us
    all_to_all x1, blocking collectives, layer(): got = lax.all_to_all(sent, ('xh', 'y'), 0, 0, tiled=True)  14.1 us
    all_gather x1, blocking collectives, layer(): spread = lax.all_gather(mixed, ('xl', 'core'), axis=0)  11.5 us
    ppermute x8, waiting for transfers between devices, hop(): lax.ppermute(x, CHIPS, [(i, i + steps) for i in range(64) if 0 <= i + ste...  8.57 us
    all_to_all x1, starting transfers between devices, layer(): got = lax.all_to_all(sent, 'z', 0, 0, tiled=True)  8.19 us
    all_gather x1, blocking collectives, layer(): whole = lax.all_gather(tagged, ('xl', 'core'), axis=0, tiled=True)  6.94 us
    all_to_all x1, starting transfers between devices, layer(): total = lax.all_to_all(sent, ('xh', 'y'), 0, 0, tiled=True)  4.24 us
  transfers between devices with their start and end apart: 11, of which 2 were waited for; matrix products, arithmetic and copies ran while one was open for 0% of the time, Pallas kernels for 8%

profile of v5, /device:TPU:5, one launch (start us, length us, event | category | flops | bytes accessed | tf_op | source)
XLA Modules:
  0.0 113.5 jit_solution(16078070153613091596)
XLA Ops:
  0.0 1.6 %shard_map.109 = (bf16[144,384]{1,0:T(8,128)(2,1)S(1)}, bf16[768,384]{1,0:T(8,128)(2,1)S(1)}, bf16[768,384]{1,0:T(8,128)(2,1)S(1)}, bf16[768,384]{1,0:T(8,128)(2...) custom-call(bf16[128,384]{1,0:T(8,128)(2,1)} %tokens.1, s32[1,128]{1,0:T(1,128)} %bitcast.9, ...), custom_call_target="tpu_custom_call" | custom-call | bytes 262144 | tf_op jit(solution)/shard_map/pallas_call | solution.py:239
  1.6 6.9 %all_gather.9.whole = bf16[576,384]{1,0:T(8,128)(2,1)S(1)} all-gather(bf16[144,384]{1,0:T(8,128)(2,1)S(1)} %get-tuple-element.14), channel_id=1, replica_groups=mesh['xh'=2,'y'=4,'z'=8,'core'=2,'xl'=2] {'xl','core'}, dimensions={0}, use_global_device_ids=true | all-gather | bytes 552960 | tf_op jit(solution)/shard_map/all_gather | solution.py:293
  8.6 1.1 shard_map.110
  9.7 0.1 copy-done.2
  9.8 0.2 copy-done.3
  10.0 0.8 shard_map.111
  10.8 14.1 %all_to_all.15.got = bf16[8,72,384]{2,1,0:T(8,128)(2,1)S(1)} all-to-all(bf16[8,72,384]{2,1,0:T(8,128)(2,1)S(1)} %bitcast.6), channel_id=1, replica_groups=mesh['xh'=2,'y'=4,'z'=8,'core'=2,'xl'=2] {'xh','y'}, dimensions={0} | all-to-all | bytes 884736 | tf_op jit(solution)/shard_map/all_to_all | solution.py:319
  25.0 0.8 shard_map.112
  25.8 8.2 %all-to-all-start.1 = ((bf16[8,72,384]{2,1,0:T(8,128)(2,1)}), bf16[8,72,384]{2,1,0:T(8,128)(2,1)S(1)}, u32[]{:S(2)}, u32[]{:S(2)}) async-start(bf16[8,72,384]{2,1,0:T(8,128)(2,1)} %shard_map.112), calls=%async_computation.1 | async-start | bytes 884736 | tf_op jit(solution)/shard_map/all_to_all | solution.py:321
  34.0 3.4 %collective-permute-start = (bf16[272,384]{1,0:T(8,128)(2,1)S(1)}, bf16[272,384]{1,0:T(8,128)(2,1)S(1)}, u32[]{:S(2)}, u32[]{:S(2)}) collective-permute-start(bf16[272,384]{1,0:T(8,128)(2,1)S(1)} %get-tuple-element.20.packed.refs_0_), channel_id=1, source_target_pairs={{0,4},{4,8},{8,12},{12,16},{16,20},{20,24},{24,28},{28,32},{32,36}... | collective-permute-start | bytes 626696 | tf_op jit(solution)/shard_map/ppermute | solution.py:257
  37.4 7.6 %collective-permute-start.1 = (bf16[272,384]{1,0:T(8,128)(2,1)S(1)}, bf16[272,384]{1,0:T(8,128)(2,1)S(1)}, u32[]{:S(2)}, u32[]{:S(2)}) collective-permute-start(bf16[272,384]{1,0:T(8,128)(2,1)S(1)} %get-tuple-element.20.packed.refs_0_), channel_id=1, source_target_pairs={{4,0},{8,4},{12,8},{16,12},{20,16},{24,20},{28,24},{32,28},{36,32}... | collective-permute-start | bytes 626696 | tf_op jit(solution)/shard_map/ppermute | solution.py:257
  45.0 8.2 %collective-permute-done.refs_1_ = bf16[272,384]{1,0:T(8,128)(2,1)S(1)} collective-permute-done((bf16[272,384]{1,0:T(8,128)(2,1)S(1)}, bf16[272,384]{1,0:T(8,128)(2,1)S(1)}, u32[]{:S(2)}, u32[]{:S(2)}) %collective-permute-start) | collective-permute-done | bytes 208928 | tf_op jit(solution)/shard_map/ppermute | solution.py:257
  53.2 1.9 %collective-permute-start.2 = (bf16[272,384]{1,0:T(8,128)(2,1)S(1)}, bf16[272,384]{1,0:T(8,128)(2,1)S(1)}, u32[]{:S(2)}, u32[]{:S(2)}) collective-permute-start(bf16[272,384]{1,0:T(8,128)(2,1)S(1)} %collective-permute-done.refs_1_), channel_id=1, source_target_pairs={{0,4},{4,8},{8,12},{12,16},{16,20},{20,24},{24,28},{28,32},{32,36}... | collective-permute-start | bytes 626696 | tf_op jit(solution)/shard_map/ppermute | solution.py:257
  55.1 0.0 collective-permute-done.1.refs_2_
  55.1 9.1 %collective-permute-start.3 = (bf16[272,384]{1,0:T(8,128)(2,1)S(1)}, bf16[272,384]{1,0:T(8,128)(2,1)S(1)}, u32[]{:S(2)}, u32[]{:S(2)}) collective-permute-start(bf16[272,384]{1,0:T(8,128)(2,1)S(1)} %collective-permute-done.1.refs_2_), channel_id=1, source_target_pairs={{4,0},{8,4},{12,8},{16,12},{20,16},{24,20},{28,24},{32,28},{36,32}... | collective-permute-start | bytes 626696 | tf_op jit(solution)/shard_map/ppermute | solution.py:257
  64.2 0.0 all-to-all-done.1.got
  64.2 0.8 shard_map.113
  65.0 4.2 %all-to-all-start.2 = ((bf16[8,72,384]{2,1,0:T(8,128)(2,1)}), bf16[8,72,384]{2,1,0:T(8,128)(2,1)S(1)}, u32[]{:S(2)}, u32[]{:S(2)}) async-start(bf16[8,72,384]{2,1,0:T(8,128)(2,1)} %shard_map.113), calls=%async_computation.2 | async-start | bytes 884736 | tf_op jit(solution)/shard_map/all_to_all | solution.py:323
  69.3 0.0 collective-permute-done.2.refs_3_
  69.3 1.9 %collective-permute-start.4 = (bf16[272,384]{1,0:T(8,128)(2,1)S(1)}, bf16[272,384]{1,0:T(8,128)(2,1)S(1)}, u32[]{:S(2)}, u32[]{:S(2)}) collective-permute-start(bf16[272,384]{1,0:T(8,128)(2,1)S(1)} %collective-permute-done.2.refs_3_), channel_id=1, source_target_pairs={{0,4},{4,8},{8,12},{12,16},{16,20},{20,24},{24,28},{28,32},{32,36}... | collective-permute-start | bytes 626696 | tf_op jit(solution)/shard_map/ppermute | solution.py:257
  71.2 9.1 %collective-permute-start.5 = (bf16[272,384]{1,0:T(8,128)(2,1)S(1)}, bf16[272,384]{1,0:T(8,128)(2,1)S(1)}, u32[]{:S(2)}, u32[]{:S(2)}) collective-permute-start(bf16[272,384]{1,0:T(8,128)(2,1)S(1)} %collective-permute-done.3.refs_4_), channel_id=1, source_target_pairs={{4,0},{8,4},{12,8},{16,12},{20,16},{24,20},{28,24},{32,28},{36,32}... | collective-permute-start | bytes 626696 | tf_op jit(solution)/shard_map/ppermute | solution.py:257
  80.3 0.9 collective-permute-start.8
  81.3 0.4 collective-permute-done.4.refs_5_
  81.6 1.9 %collective-permute-start.6 = (bf16[272,384]{1,0:T(8,128)(2,1)S(1)}, bf16[272,384]{1,0:T(8,128)(2,1)S(1)}, u32[]{:S(2)}, u32[]{:S(2)}) collective-permute-start(bf16[272,384]{1,0:T(8,128)(2,1)S(1)} %collective-permute-done.4.refs_5_), channel_id=1, source_target_pairs={{0,4},{4,8},{8,12},{12,16},{16,20},{20,24},{24,28},{28,32},{32,36}... | collective-permute-start | bytes 626696 | tf_op jit(solution)/shard_map/ppermute | solution.py:257
  83.6 9.1 %collective-permute-start.7 = (bf16[272,384]{1,0:T(8,128)(2,1)S(1)}, bf16[272,384]{1,0:T(8,128)(2,1)S(1)}, u32[]{:S(2)}, u32[]{:S(2)}) collective-permute-start(bf16[272,384]{1,0:T(8,128)(2,1)S(1)} %collective-permute-done.5.refs_6_), channel_id=1, source_target_pairs={{4,0},{8,4},{12,8},{16,12},{20,16},{24,20},{28,24},{32,28},{36,32}... | collective-permute-start | bytes 626696 | tf_op jit(solution)/shard_map/ppermute | solution.py:257
  92.7 5.8 %shard_map.114.fresh = bf16[3,192,384]{2,1,0:T(8,128)(2,1)S(1)} custom-call(bf16[576,384]{1,0:T(8,128)(2,1)S(1)} %bitcast.7, f32[2,192,384]{2,1,0:T(8,128)} %gate_hbm.1, f32[2,192,384]{2,1,0:T(8,128)} %up_hbm.1, f32[2,192,384]{2,1,0:T(8,128)} %down_hbm.1, f32[2]{0:T(128)} %step_hbm.1), custom_call_target="tpu_custom_call" | custom-call | flops 10000000000 | bytes 3145728 | tf_op jit(solution)/shard_map/pallas_call | solution.py:239
  98.5 0.0 collective-permute-done.6.refs_7_
  98.5 0.0 collective-permute-done.7.refs_8_
  98.5 2.5 %shard_map.115 = bf16[256,192]{1,0:T(8,128)(2,1)S(1)} custom-call(bf16[256,192]{1,0:T(8,128)(2,1)S(1)} %get-tuple-element.19.query_ref, bf16[3,192,384]{2,1,0:T(8,128)(2,1)S(1)} %shard_map.114.fresh, bf16[272,384]{1,0:T(8,128)(2,1)S(1)} %get-tuple-element.20.packed.refs_0_, bf16[272,384]{1,0:T(8,128)(2,1)S(1)} %collective-permute-done.refs_1_, ...), custom_call_target="tpu_custom_call" | custom-call | flops 603979776 | bytes 3145728 | tf_op jit(solution)/shard_map/pallas_call | solution.py:239
  101.1 0.0 copy-start
  101.1 11.5 %all-gather = bf16[1024,192]{1,0:T(8,128)(2,1)S(1)} all-gather(bf16[256,192]{1,0:T(8,128)(2,1)S(1)} %shard_map.115), channel_id=2, replica_groups=mesh['xh'=2,'y'=4,'z'=8,'core'=2,'xl'=2] {'xl','core'}, dimensions={0}, use_global_device_ids=true | all-gather | bytes 491520 | tf_op jit(solution)/shard_map/all_gather | solution.py:349
  112.6 0.9 shard_map.116
  (9 shorter events, 0.0 us)
Async XLA Ops:
  8.6 1.1 copy-start.1
  8.6 1.2 %copy-start.2 = (f32[2,192,384]{2,1,0:T(8,128)S(1)}, f32[2,192,384]{2,1,0:T(8,128)}, u32[]{:S(2)}) copy-start(f32[2,192,384]{2,1,0:T(8,128)} %up_hbm.1) | copy-start | bytes 1769476
  8.6 1.4 %copy-start.3 = (f32[2,192,384]{2,1,0:T(8,128)S(1)}, f32[2,192,384]{2,1,0:T(8,128)}, u32[]{:S(2)}) copy-start(f32[2,192,384]{2,1,0:T(8,128)} %down_hbm.1) | copy-start | bytes 1769476
  25.8 38.4 %all-to-all-start.1 = ((bf16[8,72,384]{2,1,0:T(8,128)(2,1)}), bf16[8,72,384]{2,1,0:T(8,128)(2,1)S(1)}, u32[]{:S(2)}, u32[]{:S(2)}) async-start(bf16[8,72,384]{2,1,0:T(8,128)(2,1)} %shard_map.112), calls=%async_computation.1 | async-start | bytes 884736 | tf_op jit(solution)/shard_map/all_to_all | solution.py:321
  34.0 19.2 %collective-permute-start = (bf16[272,384]{1,0:T(8,128)(2,1)S(1)}, bf16[272,384]{1,0:T(8,128)(2,1)S(1)}, u32[]{:S(2)}, u32[]{:S(2)}) collective-permute-start(bf16[272,384]{1,0:T(8,128)(2,1)S(1)} %get-tuple-element.20.packed.refs_0_), channel_id=1, source_target_pairs={{0,4},{4,8},{8,12},{12,16},{16,20},{20,24},{24,28},{28,32},{32,36}... | collective-permute-start | bytes 626696 | tf_op jit(solution)/shard_map/ppermute | solution.py:257
  37.4 17.7 %collective-permute-start.1 = (bf16[272,384]{1,0:T(8,128)(2,1)S(1)}, bf16[272,384]{1,0:T(8,128)(2,1)S(1)}, u32[]{:S(2)}, u32[]{:S(2)}) collective-permute-start(bf16[272,384]{1,0:T(8,128)(2,1)S(1)} %get-tuple-element.20.packed.refs_0_), channel_id=1, source_target_pairs={{4,0},{8,4},{12,8},{16,12},{20,16},{24,20},{28,24},{32,28},{36,32}... | collective-permute-start | bytes 626696 | tf_op jit(solution)/shard_map/ppermute | solution.py:257
  53.2 16.1 %collective-permute-start.2 = (bf16[272,384]{1,0:T(8,128)(2,1)S(1)}, bf16[272,384]{1,0:T(8,128)(2,1)S(1)}, u32[]{:S(2)}, u32[]{:S(2)}) collective-permute-start(bf16[272,384]{1,0:T(8,128)(2,1)S(1)} %collective-permute-done.refs_1_), channel_id=1, source_target_pairs={{0,4},{4,8},{8,12},{12,16},{16,20},{20,24},{24,28},{28,32},{32,36}... | collective-permute-start | bytes 626696 | tf_op jit(solution)/shard_map/ppermute | solution.py:257
  55.1 16.1 %collective-permute-start.3 = (bf16[272,384]{1,0:T(8,128)(2,1)S(1)}, bf16[272,384]{1,0:T(8,128)(2,1)S(1)}, u32[]{:S(2)}, u32[]{:S(2)}) collective-permute-start(bf16[272,384]{1,0:T(8,128)(2,1)S(1)} %collective-permute-done.1.refs_2_), channel_id=1, source_target_pairs={{4,0},{8,4},{12,8},{16,12},{20,16},{24,20},{28,24},{32,28},{36,32}... | collective-permute-start | bytes 626696 | tf_op jit(solution)/shard_map/ppermute | solution.py:257
  65.0 27.6 %all-to-all-start.2 = ((bf16[8,72,384]{2,1,0:T(8,128)(2,1)}), bf16[8,72,384]{2,1,0:T(8,128)(2,1)S(1)}, u32[]{:S(2)}, u32[]{:S(2)}) async-start(bf16[8,72,384]{2,1,0:T(8,128)(2,1)} %shard_map.113), calls=%async_computation.2 | async-start | bytes 884736 | tf_op jit(solution)/shard_map/all_to_all | solution.py:323
  69.3 12.4 %collective-permute-start.4 = (bf16[272,384]{1,0:T(8,128)(2,1)S(1)}, bf16[272,384]{1,0:T(8,128)(2,1)S(1)}, u32[]{:S(2)}, u32[]{:S(2)}) collective-permute-start(bf16[272,384]{1,0:T(8,128)(2,1)S(1)} %collective-permute-done.2.refs_3_), channel_id=1, source_target_pairs={{0,4},{4,8},{8,12},{12,16},{16,20},{20,24},{24,28},{28,32},{32,36}... | collective-permute-start | bytes 626696 | tf_op jit(solution)/shard_map/ppermute | solution.py:257
  71.2 12.3 %collective-permute-start.5 = (bf16[272,384]{1,0:T(8,128)(2,1)S(1)}, bf16[272,384]{1,0:T(8,128)(2,1)S(1)}, u32[]{:S(2)}, u32[]{:S(2)}) collective-permute-start(bf16[272,384]{1,0:T(8,128)(2,1)S(1)} %collective-permute-done.3.refs_4_), channel_id=1, source_target_pairs={{4,0},{8,4},{12,8},{16,12},{20,16},{24,20},{28,24},{32,28},{36,32}... | collective-permute-start | bytes 626696 | tf_op jit(solution)/shard_map/ppermute | solution.py:257
  80.3 32.3 %collective-permute-start.8 = (bf16[384,384]{1,0:T(8,128)(2,1)S(1)}, bf16[384,384]{1,0:T(8,128)(2,1)S(1)}, u32[]{:S(2)}, u32[]{:S(2)}) collective-permute-start(bf16[384,384]{1,0:T(8,128)(2,1)S(1)} %get-tuple-element.22), channel_id=1, source_target_pairs={{0,1},{1,0},{2,3},{3,2},{4,5},{5,4},{6,7},{7,6},{8,9},{9,8},{10,11... | collective-permute-start | bytes 884744 | tf_op jit(solution)/shard_map/ppermute | solution.py:348
  81.6 16.9 %collective-permute-start.6 = (bf16[272,384]{1,0:T(8,128)(2,1)S(1)}, bf16[272,384]{1,0:T(8,128)(2,1)S(1)}, u32[]{:S(2)}, u32[]{:S(2)}) collective-permute-start(bf16[272,384]{1,0:T(8,128)(2,1)S(1)} %collective-permute-done.4.refs_5_), channel_id=1, source_target_pairs={{0,4},{4,8},{8,12},{12,16},{16,20},{20,24},{24,28},{28,32},{32,36}... | collective-permute-start | bytes 626696 | tf_op jit(solution)/shard_map/ppermute | solution.py:257
  83.6 15.0 %collective-permute-start.7 = (bf16[272,384]{1,0:T(8,128)(2,1)S(1)}, bf16[272,384]{1,0:T(8,128)(2,1)S(1)}, u32[]{:S(2)}, u32[]{:S(2)}) collective-permute-start(bf16[272,384]{1,0:T(8,128)(2,1)S(1)} %collective-permute-done.5.refs_6_), channel_id=1, source_target_pairs={{4,0},{8,4},{12,8},{16,12},{20,16},{24,20},{28,24},{32,28},{36,32}... | collective-permute-start | bytes 626696 | tf_op jit(solution)/shard_map/ppermute | solution.py:257
  101.1 11.5 %copy-start = (bf16[384,768]{1,0:T(8,128)(2,1)S(1)}, bf16[384,768]{1,0:T(8,128)(2,1)}, u32[]{:S(2)}) copy-start(bf16[384,768]{1,0:T(8,128)(2,1)} %weight.1) | copy-start | bytes 1769476

commit v6 on v5

--- a/solution.py
+++ b/solution.py
@@ -23,6 +23,7 @@
 PACKED = ROWS + 16
 GATHERED = TOK_DEV + 16
 TAGS = 32
+WIDE = 256
 f32 = jnp.float32
 bf16 = jnp.bfloat16
 ANY = pl.BlockSpec(memory_space=pl.ANY)
@@ -68,13 +69,14 @@
     tagged_ref, wq, wk, wv, wr, theirs, views, sem,
 ):
     columns = pl.ds(pl.multiple_of((1 - lax.axis_index("xl")) * FH, FH), FH)
+    near = pl.ds(pl.multiple_of(lax.axis_index("core") * TOK_DEV, TOK_DEV), WIDE)
     fetches = copies(
         sem,
         (views_hbm, views),
         (tokens, tagged_ref.at[pl.ds(0, TOK_DEV)]),
-        (wq_hbm, wq),
-        (wk_hbm, wk),
-        (wv_hbm, wv),
+        (wq_hbm.at[:, near], wq),
+        (wk_hbm.at[:, near], wk),
+        (wv_hbm.at[:, near], wv),
         (wr_hbm, wr),
         (wo_hbm.at[:, columns], theirs),
     )
@@ -109,14 +111,14 @@
 
     def own(w):
         product = both(w)
-        return jnp.where(core == 0, product[:, :DH], product[:, DH:]).astype(bf16)
+        return jnp.where(core == 0, product[:, :DH], product[:, WIDE - DH :]).astype(bf16)
 
     packed_ref[:ROWS] = jnp.concatenate((own(wk), own(wv)), 1)
     packed_ref[ROWS:] = tags
     query_ref[...] = own(wq)
 
 
-def gradient_kernel(packed, rates, gate_ref, up_ref, down_ref, sent_ref):
+def gradient_kernel(packed, rates, gate_ref, up_ref, down_ref, sent_hbm, sent_ref, sem):
     core = lax.axis_index("core")
     keys_n = normalize(packed[:ROWS, :DH])
     value = packed[:ROWS, DH:].astype(f32)
@@ -126,21 +128,30 @@
     active = gate * logistic
     product = (active * upward).astype(bf16)
     error = (-rates[...] * value).astype(bf16)
+    stores = []
+
+    def send(i, part):
+        rows = pl.ds(i * DH, DH)
+        sent_ref[rows] = part.astype(bf16)
+        stores.append(pltpu.make_async_copy(sent_ref.at[rows], sent_hbm.at[rows], sem.at[i]))
+        stores[-1].start()
+
+    send(2, tn(error, product))
     back = nn(error, down_ref[core].astype(bf16))
+    send(1, tn(keys_n, (back * active).astype(bf16)))
     grad_g = (back * upward * logistic * (1.0 + gate * (1.0 - logistic))).astype(bf16)
-    grad_u = (back * active).astype(bf16)
-    sent_ref[:DH] = tn(keys_n, grad_g).astype(bf16)
-    sent_ref[DH : 2 * DH] = tn(keys_n, grad_u).astype(bf16)
-    sent_ref[2 * DH :] = tn(error, product).astype(bf16)
-
-
-def add_kernel(got, sent_ref):
+    send(0, tn(keys_n, grad_g))
+    for store in stores:
+        store.wait()
+
+
+def add_kernel(got, sent_hbm, part_ref, sem):
     part = got[0].astype(f32)
     for i in range(1, 8):
         part = part + got[i].astype(f32)
-    part = part.astype(bf16)
-    for i in range(8):
-        sent_ref[i] = part
+    part_ref[...] = part.astype(bf16)
+    for store in copies(sem, *[(part_ref, sent_hbm.at[i]) for i in range(8)]):
+        store.wait()
 
 
 def blend_kernel(query_ref, fresh, *refs):
@@ -275,7 +286,7 @@
     tagged, *weights, theirs = call(
         tag_kernel,
         [shape((GATHERED, FH), bf16)]
-        + [shape((768, FH), bf16)] * 3
+        + [shape((768, WIDE), bf16)] * 3
         + [shape((2, 768), bf16), shape((FH, FH), bf16)],
         (
             tokens,
@@ -307,14 +318,23 @@
 
     sent = call(
         gradient_kernel,
-        shape((3 * DH, FH), bf16),
+        pltpu.HBM((3 * DH, FH), bf16),
         (packed, rates, fast_gate, fast_up, fast_down),
+        outs=HBM,
+        scratch=[pltpu.VMEM((3 * DH, FH), bf16), pltpu.SemaphoreType.DMA((3,))],
         flops=2 * 256 * 192 * 384 * 6,
         bytes_accessed=3 << 20,
     ).reshape(8, 72, FH)
 
     def add(got):
-        return call(add_kernel, shape((8, 72, FH), bf16), (got,), bytes_accessed=1 << 20)
+        return call(
+            add_kernel,
+            pltpu.HBM((8, 72, FH), bf16),
+            (got,),
+            outs=HBM,
+            scratch=[pltpu.VMEM((72, FH), bf16), pltpu.SemaphoreType.DMA((8,))],
+            bytes_accessed=1 << 20,
+        )
 
     got = lax.all_to_all(sent, ("xh", "y"), 0, 0, tiled=True)
     sent = add(got)
@@ -371,6 +391,4 @@
         P("xl", None, None),
         P("xl"),
     )
-    return jax.shard_map(
-        layer, mesh=fine, in_specs=placed, out_specs=P(TOK, "xl"), check_vma=False
-    )
+    return jax.shard_map(layer, mesh=fine, in_specs=placed, out_specs=P(TOK, "xl"), check_vma=False)

time: 114 us -> 115 us (level)
  no operation moved by 1% of the time
where the time goes in v6:
time: 115 us; the launch traced here: 114 us
  starting transfers between devices  57.3 us (50%)
  blocking collectives  32.9 us (29%)
  Pallas kernels  15 us (13%)
  waiting for transfers between devices  8.66 us (8%)
    ppermute x8, starting transfers between devices, hop(): lax.ppermute(x, CHIPS, [(i, i + steps) for i in range(64) if 0 <= i + ste...  44 us
    pallas_call x8, Pallas kernels, call(): pl.pallas_call(kernel, out_shape=shapes, in_specs=specs or [VMEM] * len(a...  15 us
    all_to_all x1, blocking collectives, layer(): got = lax.all_to_all(sent, ('xh', 'y'), 0, 0, tiled=True)  14.4 us
    all_gather x1, blocking collectives, layer(): spread = lax.all_gather(mixed, ('xl', 'core'), axis=0)  11.5 us
    ppermute x8, waiting for transfers between devices, hop(): lax.ppermute(x, CHIPS, [(i, i + steps) for i in range(64) if 0 <= i + ste...  8.65 us
    all_to_all x1, starting transfers between devices, layer(): got = lax.all_to_all(sent, 'z', 0, 0, tiled=True)  8.2 us
    all_gather x1, blocking collectives, layer(): whole = lax.all_gather(tagged, ('xl', 'core'), axis=0, tiled=True)  7.08 us
    all_to_all x1, starting transfers between devices, layer(): total = lax.all_to_all(sent, ('xh', 'y'), 0, 0, tiled=True)  4.26 us
  transfers between devices with their start and end apart: 11, of which 2 were waited for; matrix products, arithmetic and copies ran while one was open for 0% of the time, Pallas kernels for 8%

profile of v6, /device:TPU:5, one launch (start us, length us, event | category | flops | bytes accessed | tf_op | source)
XLA Modules:
  0.0 114.5 jit_solution(9793184621587156443)
XLA Ops:
  0.0 1.5 %shard_map.109 = (bf16[144,384]{1,0:T(8,128)(2,1)S(1)}, bf16[768,256]{1,0:T(8,128)(2,1)S(1)}, bf16[768,256]{1,0:T(8,128)(2,1)S(1)}, bf16[768,256]{1,0:T(8,128)(2...) custom-call(bf16[128,384]{1,0:T(8,128)(2,1)} %tokens.1, s32[1,128]{1,0:T(1,128)} %bitcast.9, ...), custom_call_target="tpu_custom_call" | custom-call | bytes 262144 | tf_op jit(solution)/shard_map/pallas_call | solution.py:250
  1.5 0.0 copy-start.3
  1.5 7.1 %all_gather.9.whole = bf16[576,384]{1,0:T(8,128)(2,1)S(1)} all-gather(bf16[144,384]{1,0:T(8,128)(2,1)S(1)} %get-tuple-element.14), channel_id=1, replica_groups=mesh['xh'=2,'y'=4,'z'=8,'core'=2,'xl'=2] {'xl','core'}, dimensions={0}, use_global_device_ids=true | all-gather | bytes 552960 | tf_op jit(solution)/shard_map/all_gather | solution.py:304
  8.6 0.8 shard_map.110
  9.4 0.2 copy-done.1
  9.6 0.2 copy-done.2
  9.8 1.6 %shard_map.111 = bf16[576,384]{1,0:T(8,128)(2,1)} custom-call(bf16[272,384]{1,0:T(8,128)(2,1)S(1)} %get-tuple-element.20.packed.refs_0_, f32[256,1]{1,0:T(8,128)S(1)} %get-tuple-element.21.rates, f32[2,192,384]{2,1,0:T(8,128)S(1)} %copy-done.1, f32[2,192,384]{2,1,0:T(8,128)S(1)} %copy-done.2, f32[2,192,384]{2,1,0:T(8,128)S(1)} %copy-done.3), custom_call_target="tpu_custom_call" | custom-call | flops 226492416 | bytes 3145728 | tf_op jit(solution)/shard_map/pallas_call | solution.py:250
  11.4 14.4 %all_to_all.15.got = bf16[8,72,384]{2,1,0:T(8,128)(2,1)S(1)} all-to-all(bf16[8,72,384]{2,1,0:T(8,128)(2,1)} %bitcast.7), channel_id=1, replica_groups=mesh['xh'=2,'y'=4,'z'=8,'core'=2,'xl'=2] {'xh','y'}, dimensions={0} | all-to-all | bytes 884736 | tf_op jit(solution)/shard_map/all_to_all | solution.py:339
  25.8 0.9 shard_map.112
  26.7 8.2 %all-to-all-start.1 = ((bf16[8,72,384]{2,1,0:T(8,128)(2,1)}), bf16[8,72,384]{2,1,0:T(8,128)(2,1)S(1)}, u32[]{:S(2)}, u32[]{:S(2)}) async-start(bf16[8,72,384]{2,1,0:T(8,128)(2,1)} %shard_map.112), calls=%async_computation.1 | async-start | bytes 884736 | tf_op jit(solution)/shard_map/all_to_all | solution.py:341
  34.9 3.4 %collective-permute-start = (bf16[272,384]{1,0:T(8,128)(2,1)S(1)}, bf16[272,384]{1,0:T(8,128)(2,1)S(1)}, u32[]{:S(2)}, u32[]{:S(2)}) collective-permute-start(bf16[272,384]{1,0:T(8,128)(2,1)S(1)} %get-tuple-element.20.packed.refs_0_), channel_id=1, source_target_pairs={{0,4},{4,8},{8,12},{12,16},{16,20},{20,24},{24,28},{28,32},{32,36}... | collective-permute-start | bytes 626696 | tf_op jit(solution)/shard_map/ppermute | solution.py:268
  38.2 7.6 %collective-permute-start.1 = (bf16[272,384]{1,0:T(8,128)(2,1)S(1)}, bf16[272,384]{1,0:T(8,128)(2,1)S(1)}, u32[]{:S(2)}, u32[]{:S(2)}) collective-permute-start(bf16[272,384]{1,0:T(8,128)(2,1)S(1)} %get-tuple-element.20.packed.refs_0_), channel_id=1, source_target_pairs={{4,0},{8,4},{12,8},{16,12},{20,16},{24,20},{28,24},{32,28},{36,32}... | collective-permute-start | bytes 626696 | tf_op jit(solution)/shard_map/ppermute | solution.py:268
  45.9 8.2 %collective-permute-done.refs_1_ = bf16[272,384]{1,0:T(8,128)(2,1)S(1)} collective-permute-done((bf16[272,384]{1,0:T(8,128)(2,1)S(1)}, bf16[272,384]{1,0:T(8,128)(2,1)S(1)}, u32[]{:S(2)}, u32[]{:S(2)}) %collective-permute-start) | collective-permute-done | bytes 208928 | tf_op jit(solution)/shard_map/ppermute | solution.py:268
  54.1 1.9 %collective-permute-start.2 = (bf16[272,384]{1,0:T(8,128)(2,1)S(1)}, bf16[272,384]{1,0:T(8,128)(2,1)S(1)}, u32[]{:S(2)}, u32[]{:S(2)}) collective-permute-start(bf16[272,384]{1,0:T(8,128)(2,1)S(1)} %collective-permute-done.refs_1_), channel_id=1, source_target_pairs={{0,4},{4,8},{8,12},{12,16},{16,20},{20,24},{24,28},{28,32},{32,36}... | collective-permute-start | bytes 626696 | tf_op jit(solution)/shard_map/ppermute | solution.py:268
  56.0 0.0 collective-permute-done.1.refs_2_
  56.0 9.1 %collective-permute-start.3 = (bf16[272,384]{1,0:T(8,128)(2,1)S(1)}, bf16[272,384]{1,0:T(8,128)(2,1)S(1)}, u32[]{:S(2)}, u32[]{:S(2)}) collective-permute-start(bf16[272,384]{1,0:T(8,128)(2,1)S(1)} %collective-permute-done.1.refs_2_), channel_id=1, source_target_pairs={{4,0},{8,4},{12,8},{16,12},{20,16},{24,20},{28,24},{32,28},{36,32}... | collective-permute-start | bytes 626696 | tf_op jit(solution)/shard_map/ppermute | solution.py:268
  65.1 0.0 all-to-all-done.1.got
  65.1 0.9 shard_map.113
  66.0 4.3 %all-to-all-start.2 = ((bf16[8,72,384]{2,1,0:T(8,128)(2,1)}), bf16[8,72,384]{2,1,0:T(8,128)(2,1)S(1)}, u32[]{:S(2)}, u32[]{:S(2)}) async-start(bf16[8,72,384]{2,1,0:T(8,128)(2,1)} %shard_map.113), calls=%async_computation.2 | async-start | bytes 884736 | tf_op jit(solution)/shard_map/all_to_all | solution.py:343
  70.3 0.0 collective-permute-done.2.refs_3_
  70.3 1.9 %collective-permute-start.4 = (bf16[272,384]{1,0:T(8,128)(2,1)S(1)}, bf16[272,384]{1,0:T(8,128)(2,1)S(1)}, u32[]{:S(2)}, u32[]{:S(2)}) collective-permute-start(bf16[272,384]{1,0:T(8,128)(2,1)S(1)} %collective-permute-done.2.refs_3_), channel_id=1, source_target_pairs={{0,4},{4,8},{8,12},{12,16},{16,20},{20,24},{24,28},{28,32},{32,36}... | collective-permute-start | bytes 626696 | tf_op jit(solution)/shard_map/ppermute | solution.py:268
  72.2 9.1 %collective-permute-start.5 = (bf16[272,384]{1,0:T(8,128)(2,1)S(1)}, bf16[272,384]{1,0:T(8,128)(2,1)S(1)}, u32[]{:S(2)}, u32[]{:S(2)}) collective-permute-start(bf16[272,384]{1,0:T(8,128)(2,1)S(1)} %collective-permute-done.3.refs_4_), channel_id=1, source_target_pairs={{4,0},{8,4},{12,8},{16,12},{20,16},{24,20},{28,24},{32,28},{36,32}... | collective-permute-start | bytes 626696 | tf_op jit(solution)/shard_map/ppermute | solution.py:268
  81.3 0.9 collective-permute-start.8
  82.2 0.5 collective-permute-done.4.refs_5_
  82.6 1.9 %collective-permute-start.6 = (bf16[272,384]{1,0:T(8,128)(2,1)S(1)}, bf16[272,384]{1,0:T(8,128)(2,1)S(1)}, u32[]{:S(2)}, u32[]{:S(2)}) collective-permute-start(bf16[272,384]{1,0:T(8,128)(2,1)S(1)} %collective-permute-done.4.refs_5_), channel_id=1, source_target_pairs={{0,4},{4,8},{8,12},{12,16},{16,20},{20,24},{24,28},{28,32},{32,36}... | collective-permute-start | bytes 626696 | tf_op jit(solution)/shard_map/ppermute | solution.py:268
  84.5 9.1 %collective-permute-start.7 = (bf16[272,384]{1,0:T(8,128)(2,1)S(1)}, bf16[272,384]{1,0:T(8,128)(2,1)S(1)}, u32[]{:S(2)}, u32[]{:S(2)}) collective-permute-start(bf16[272,384]{1,0:T(8,128)(2,1)S(1)} %collective-permute-done.5.refs_6_), channel_id=1, source_target_pairs={{4,0},{8,4},{12,8},{16,12},{20,16},{24,20},{28,24},{32,28},{36,32}... | collective-permute-start | bytes 626696 | tf_op jit(solution)/shard_map/ppermute | solution.py:268
  93.6 0.0 all-to-all-done.2
  93.6 5.8 %shard_map.114.fresh = bf16[3,192,384]{2,1,0:T(8,128)(2,1)S(1)} custom-call(bf16[576,384]{1,0:T(8,128)(2,1)S(1)} %bitcast.6, f32[2,192,384]{2,1,0:T(8,128)} %gate_hbm.1, f32[2,192,384]{2,1,0:T(8,128)} %up_hbm.1, f32[2,192,384]{2,1,0:T(8,128)} %down_hbm.1, f32[2]{0:T(128)} %step_hbm.1), custom_call_target="tpu_custom_call" | custom-call | flops 10000000000 | bytes 3145728 | tf_op jit(solution)/shard_map/pallas_call | solution.py:250
  99.5 2.5 %shard_map.115 = bf16[256,192]{1,0:T(8,128)(2,1)S(1)} custom-call(bf16[256,192]{1,0:T(8,128)(2,1)S(1)} %get-tuple-element.19.query_ref, bf16[3,192,384]{2,1,0:T(8,128)(2,1)S(1)} %shard_map.114.fresh, bf16[272,384]{1,0:T(8,128)(2,1)S(1)} %get-tuple-element.20.packed.refs_0_, bf16[272,384]{1,0:T(8,128)(2,1)S(1)} %collective-permute-done.refs_1_, ...), custom_call_target="tpu_custom_call" | custom-call | flops 603979776 | bytes 3145728 | tf_op jit(solution)/shard_map/pallas_call | solution.py:250
  102.1 0.0 copy-start
  102.1 11.5 %all-gather = bf16[1024,192]{1,0:T(8,128)(2,1)S(1)} all-gather(bf16[256,192]{1,0:T(8,128)(2,1)S(1)} %shard_map.115), channel_id=2, replica_groups=mesh['xh'=2,'y'=4,'z'=8,'core'=2,'xl'=2] {'xl','core'}, dimensions={0}, use_global_device_ids=true | all-gather | bytes 491520 | tf_op jit(solution)/shard_map/all_gather | solution.py:369
  113.5 0.9 shard_map.116
  (9 shorter events, 0.0 us)
Async XLA Ops:
  1.5 7.9 %copy-start.3 = (f32[2,192,384]{2,1,0:T(8,128)S(1)}, f32[2,192,384]{2,1,0:T(8,128)}, u32[]{:S(2)}) copy-start(f32[2,192,384]{2,1,0:T(8,128)} %down_hbm.1) | copy-start | bytes 1769476
  8.6 1.1 copy-start.1
  8.6 1.2 %copy-start.2 = (f32[2,192,384]{2,1,0:T(8,128)S(1)}, f32[2,192,384]{2,1,0:T(8,128)}, u32[]{:S(2)}) copy-start(f32[2,192,384]{2,1,0:T(8,128)} %up_hbm.1) | copy-start | bytes 1769476
  26.7 38.4 %all-to-all-start.1 = ((bf16[8,72,384]{2,1,0:T(8,128)(2,1)}), bf16[8,72,384]{2,1,0:T(8,128)(2,1)S(1)}, u32[]{:S(2)}, u32[]{:S(2)}) async-start(bf16[8,72,384]{2,1,0:T(8,128)(2,1)} %shard_map.112), calls=%async_computation.1 | async-start | bytes 884736 | tf_op jit(solution)/shard_map/all_to_all | solution.py:341
  34.9 19.2 %collective-permute-start = (bf16[272,384]{1,0:T(8,128)(2,1)S(1)}, bf16[272,384]{1,0:T(8,128)(2,1)S(1)}, u32[]{:S(2)}, u32[]{:S(2)}) collective-permute-start(bf16[272,384]{1,0:T(8,128)(2,1)S(1)} %get-tuple-element.20.packed.refs_0_), channel_id=1, source_target_pairs={{0,4},{4,8},{8,12},{12,16},{16,20},{20,24},{24,28},{28,32},{32,36}... | collective-permute-start | bytes 626696 | tf_op jit(solution)/shard_map/ppermute | solution.py:268
  38.2 17.7 %collective-permute-start.1 = (bf16[272,384]{1,0:T(8,128)(2,1)S(1)}, bf16[272,384]{1,0:T(8,128)(2,1)S(1)}, u32[]{:S(2)}, u32[]{:S(2)}) collective-permute-start(bf16[272,384]{1,0:T(8,128)(2,1)S(1)} %get-tuple-element.20.packed.refs_0_), channel_id=1, source_target_pairs={{4,0},{8,4},{12,8},{16,12},{20,16},{24,20},{28,24},{32,28},{36,32}... | collective-permute-start | bytes 626696 | tf_op jit(solution)/shard_map/ppermute | solution.py:268
  54.1 16.2 %collective-permute-start.2 = (bf16[272,384]{1,0:T(8,128)(2,1)S(1)}, bf16[272,384]{1,0:T(8,128)(2,1)S(1)}, u32[]{:S(2)}, u32[]{:S(2)}) collective-permute-start(bf16[272,384]{1,0:T(8,128)(2,1)S(1)} %collective-permute-done.refs_1_), channel_id=1, source_target_pairs={{0,4},{4,8},{8,12},{12,16},{16,20},{20,24},{24,28},{28,32},{32,36}... | collective-permute-start | bytes 626696 | tf_op jit(solution)/shard_map/ppermute | solution.py:268
  56.0 16.2 %collective-permute-start.3 = (bf16[272,384]{1,0:T(8,128)(2,1)S(1)}, bf16[272,384]{1,0:T(8,128)(2,1)S(1)}, u32[]{:S(2)}, u32[]{:S(2)}) collective-permute-start(bf16[272,384]{1,0:T(8,128)(2,1)S(1)} %collective-permute-done.1.refs_2_), channel_id=1, source_target_pairs={{4,0},{8,4},{12,8},{16,12},{20,16},{24,20},{28,24},{32,28},{36,32}... | collective-permute-start | bytes 626696 | tf_op jit(solution)/shard_map/ppermute | solution.py:268
  66.0 27.6 %all-to-all-start.2 = ((bf16[8,72,384]{2,1,0:T(8,128)(2,1)}), bf16[8,72,384]{2,1,0:T(8,128)(2,1)S(1)}, u32[]{:S(2)}, u32[]{:S(2)}) async-start(bf16[8,72,384]{2,1,0:T(8,128)(2,1)} %shard_map.113), calls=%async_computation.2 | async-start | bytes 884736 | tf_op jit(solution)/shard_map/all_to_all | solution.py:343
  70.3 12.4 %collective-permute-start.4 = (bf16[272,384]{1,0:T(8,128)(2,1)S(1)}, bf16[272,384]{1,0:T(8,128)(2,1)S(1)}, u32[]{:S(2)}, u32[]{:S(2)}) collective-permute-start(bf16[272,384]{1,0:T(8,128)(2,1)S(1)} %collective-permute-done.2.refs_3_), channel_id=1, source_target_pairs={{0,4},{4,8},{8,12},{12,16},{16,20},{20,24},{24,28},{28,32},{32,36}... | collective-permute-start | bytes 626696 | tf_op jit(solution)/shard_map/ppermute | solution.py:268
  72.2 12.3 %collective-permute-start.5 = (bf16[272,384]{1,0:T(8,128)(2,1)S(1)}, bf16[272,384]{1,0:T(8,128)(2,1)S(1)}, u32[]{:S(2)}, u32[]{:S(2)}) collective-permute-start(bf16[272,384]{1,0:T(8,128)(2,1)S(1)} %collective-permute-done.3.refs_4_), channel_id=1, source_target_pairs={{4,0},{8,4},{12,8},{16,12},{20,16},{24,20},{28,24},{32,28},{36,32}... | collective-permute-start | bytes 626696 | tf_op jit(solution)/shard_map/ppermute | solution.py:268
  81.3 32.3 %collective-permute-start.8 = (bf16[384,384]{1,0:T(8,128)(2,1)S(1)}, bf16[384,384]{1,0:T(8,128)(2,1)S(1)}, u32[]{:S(2)}, u32[]{:S(2)}) collective-permute-start(bf16[384,384]{1,0:T(8,128)(2,1)S(1)} %get-tuple-element.22), channel_id=1, source_target_pairs={{0,1},{1,0},{2,3},{3,2},{4,5},{5,4},{6,7},{7,6},{8,9},{9,8},{10,11... | collective-permute-start | bytes 884744 | tf_op jit(solution)/shard_map/ppermute | solution.py:368
  82.6 16.9 %collective-permute-start.6 = (bf16[272,384]{1,0:T(8,128)(2,1)S(1)}, bf16[272,384]{1,0:T(8,128)(2,1)S(1)}, u32[]{:S(2)}, u32[]{:S(2)}) collective-permute-start(bf16[272,384]{1,0:T(8,128)(2,1)S(1)} %collective-permute-done.4.refs_5_), channel_id=1, source_target_pairs={{0,4},{4,8},{8,12},{12,16},{16,20},{20,24},{24,28},{28,32},{32,36}... | collective-permute-start | bytes 626696 | tf_op jit(solution)/shard_map/ppermute | solution.py:268
  84.5 15.0 %collective-permute-start.7 = (bf16[272,384]{1,0:T(8,128)(2,1)S(1)}, bf16[272,384]{1,0:T(8,128)(2,1)S(1)}, u32[]{:S(2)}, u32[]{:S(2)}) collective-permute-start(bf16[272,384]{1,0:T(8,128)(2,1)S(1)} %collective-permute-done.5.refs_6_), channel_id=1, source_target_pairs={{4,0},{8,4},{12,8},{16,12},{20,16},{24,20},{28,24},{32,28},{36,32}... | collective-permute-start | bytes 626696 | tf_op jit(solution)/shard_map/ppermute | solution.py:268
  102.1 11.5 %copy-start = (bf16[384,768]{1,0:T(8,128)(2,1)S(1)}, bf16[384,768]{1,0:T(8,128)(2,1)}, u32[]{:S(2)}) copy-start(bf16[384,768]{1,0:T(8,128)(2,1)} %weight.1) | copy-start | bytes 1769476

commit v7 on v6

--- a/solution.py
+++ b/solution.py
@@ -145,13 +145,13 @@
         store.wait()
 
 
-def add_kernel(got, sent_hbm, part_ref, sem):
+def add_kernel(got, sent_ref):
     part = got[0].astype(f32)
     for i in range(1, 8):
         part = part + got[i].astype(f32)
-    part_ref[...] = part.astype(bf16)
-    for store in copies(sem, *[(part_ref, sent_hbm.at[i]) for i in range(8)]):
-        store.wait()
+    part = part.astype(bf16)
+    for i in range(8):
+        sent_ref[i] = part
 
 
 def blend_kernel(query_ref, fresh, *refs):
@@ -213,8 +213,7 @@
         mixers = []
         for h, l, a in squares:
             ah, al = halves(a)
-            cross = nt(ah, al)
-            aa = nt(ah, ah) + (cross + cross.T)
+            aa = nn(ah, ah) + (nn(ah, al) + nn(al, ah))
             mixers.append((h, l, newton_b * a + newton_c * aa))
         nexts = []
         for x, (h, l, b) in zip(currents, mixers):
@@ -327,14 +326,7 @@
     ).reshape(8, 72, FH)
 
     def add(got):
-        return call(
-            add_kernel,
-            pltpu.HBM((8, 72, FH), bf16),
-            (got,),
-            outs=HBM,
-            scratch=[pltpu.VMEM((72, FH), bf16), pltpu.SemaphoreType.DMA((8,))],
-            bytes_accessed=1 << 20,
-        )
+        return call(add_kernel, shape((8, 72, FH), bf16), (got,), bytes_accessed=1 << 20)
 
     got = lax.all_to_all(sent, ("xh", "y"), 0, 0, tiled=True)
     sent = add(got)

time: 115 us -> 115 us (level)
  no operation moved by 1% of the time
where the time goes in v7:
time: 115 us; the launch traced here: 114 us
  starting transfers between devices  57.3 us (50%)
  blocking collectives  32.9 us (29%)
  Pallas kernels  14.7 us (13%)
  waiting for transfers between devices  8.64 us (8%)
    ppermute x8, starting transfers between devices, hop(): lax.ppermute(x, CHIPS, [(i, i + steps) for i in range(64) if 0 <= i + ste...  44 us
    pallas_call x8, Pallas kernels, call(): pl.pallas_call(kernel, out_shape=shapes, in_specs=specs or [VMEM] * len(a...  14.7 us
    all_to_all x1, blocking collectives, layer(): got = lax.all_to_all(sent, ('xh', 'y'), 0, 0, tiled=True)  14.3 us
    all_gather x1, blocking collectives, layer(): spread = lax.all_gather(mixed, ('xl', 'core'), axis=0)  11.5 us
    ppermute x8, waiting for transfers between devices, hop(): lax.ppermute(x, CHIPS, [(i, i + steps) for i in range(64) if 0 <= i + ste...  8.64 us
    all_to_all x1, starting transfers between devices, layer(): got = lax.all_to_all(sent, 'z', 0, 0, tiled=True)  8.18 us
    all_gather x1, blocking collectives, layer(): whole = lax.all_gather(tagged, ('xl', 'core'), axis=0, tiled=True)  7.08 us
    all_to_all x1, starting transfers between devices, layer(): total = lax.all_to_all(sent, ('xh', 'y'), 0, 0, tiled=True)  4.24 us
  transfers between devices with their start and end apart: 11, of which 2 were waited for; matrix products, arithmetic and copies ran while one was open for 0% of the time, Pallas kernels for 8%

profile of v7, /device:TPU:5, one launch (start us, length us, event | category | flops | bytes accessed | tf_op | source)
XLA Modules:
  0.0 114.2 jit_solution(17167888956056773658)
XLA Ops:
  0.0 1.5 %shard_map.109 = (bf16[144,384]{1,0:T(8,128)(2,1)S(1)}, bf16[768,256]{1,0:T(8,128)(2,1)S(1)}, bf16[768,256]{1,0:T(8,128)(2,1)S(1)}, bf16[768,256]{1,0:T(8,128)(2...) custom-call(bf16[128,384]{1,0:T(8,128)(2,1)} %tokens.1, s32[1,128]{1,0:T(1,128)} %bitcast.9, ...), custom_call_target="tpu_custom_call" | custom-call | bytes 262144 | tf_op jit(solution)/shard_map/pallas_call | solution.py:249
  1.5 0.0 copy-start.3
  1.5 7.1 %all_gather.9.whole = bf16[576,384]{1,0:T(8,128)(2,1)S(1)} all-gather(bf16[144,384]{1,0:T(8,128)(2,1)S(1)} %get-tuple-element.14), channel_id=1, replica_groups=mesh['xh'=2,'y'=4,'z'=8,'core'=2,'xl'=2] {'xl','core'}, dimensions={0}, use_global_device_ids=true | all-gather | bytes 552960 | tf_op jit(solution)/shard_map/all_gather | solution.py:303
  8.6 0.8 shard_map.110
  9.4 0.2 copy-done.1
  9.6 0.2 copy-done.2
  9.8 1.6 %shard_map.111 = bf16[576,384]{1,0:T(8,128)(2,1)} custom-call(bf16[272,384]{1,0:T(8,128)(2,1)S(1)} %get-tuple-element.20.packed.refs_0_, f32[256,1]{1,0:T(8,128)S(1)} %get-tuple-element.21.rates, f32[2,192,384]{2,1,0:T(8,128)S(1)} %copy-done.1, f32[2,192,384]{2,1,0:T(8,128)S(1)} %copy-done.2, f32[2,192,384]{2,1,0:T(8,128)S(1)} %copy-done.3), custom_call_target="tpu_custom_call" | custom-call | flops 226492416 | bytes 3145728 | tf_op jit(solution)/shard_map/pallas_call | solution.py:249
  11.4 14.3 %all_to_all.15.got = bf16[8,72,384]{2,1,0:T(8,128)(2,1)S(1)} all-to-all(bf16[8,72,384]{2,1,0:T(8,128)(2,1)} %bitcast.7), channel_id=1, replica_groups=mesh['xh'=2,'y'=4,'z'=8,'core'=2,'xl'=2] {'xh','y'}, dimensions={0} | all-to-all | bytes 884736 | tf_op jit(solution)/shard_map/all_to_all | solution.py:331
  25.8 0.8 shard_map.112
  26.6 8.2 %all-to-all-start.1 = ((bf16[8,72,384]{2,1,0:T(8,128)(2,1)}), bf16[8,72,384]{2,1,0:T(8,128)(2,1)S(1)}, u32[]{:S(2)}, u32[]{:S(2)}) async-start(bf16[8,72,384]{2,1,0:T(8,128)(2,1)} %shard_map.112), calls=%async_computation.1 | async-start | bytes 884736 | tf_op jit(solution)/shard_map/all_to_all | solution.py:333
  34.8 3.4 %collective-permute-start = (bf16[272,384]{1,0:T(8,128)(2,1)S(1)}, bf16[272,384]{1,0:T(8,128)(2,1)S(1)}, u32[]{:S(2)}, u32[]{:S(2)}) collective-permute-start(bf16[272,384]{1,0:T(8,128)(2,1)S(1)} %get-tuple-element.20.packed.refs_0_), channel_id=1, source_target_pairs={{0,4},{4,8},{8,12},{12,16},{16,20},{20,24},{24,28},{28,32},{32,36}... | collective-permute-start | bytes 626696 | tf_op jit(solution)/shard_map/ppermute | solution.py:267
  38.1 7.6 %collective-permute-start.1 = (bf16[272,384]{1,0:T(8,128)(2,1)S(1)}, bf16[272,384]{1,0:T(8,128)(2,1)S(1)}, u32[]{:S(2)}, u32[]{:S(2)}) collective-permute-start(bf16[272,384]{1,0:T(8,128)(2,1)S(1)} %get-tuple-element.20.packed.refs_0_), channel_id=1, source_target_pairs={{4,0},{8,4},{12,8},{16,12},{20,16},{24,20},{28,24},{32,28},{36,32}... | collective-permute-start | bytes 626696 | tf_op jit(solution)/shard_map/ppermute | solution.py:267
  45.8 8.2 %collective-permute-done.refs_1_ = bf16[272,384]{1,0:T(8,128)(2,1)S(1)} collective-permute-done((bf16[272,384]{1,0:T(8,128)(2,1)S(1)}, bf16[272,384]{1,0:T(8,128)(2,1)S(1)}, u32[]{:S(2)}, u32[]{:S(2)}) %collective-permute-start) | collective-permute-done | bytes 208928 | tf_op jit(solution)/shard_map/ppermute | solution.py:267
  54.0 1.9 %collective-permute-start.2 = (bf16[272,384]{1,0:T(8,128)(2,1)S(1)}, bf16[272,384]{1,0:T(8,128)(2,1)S(1)}, u32[]{:S(2)}, u32[]{:S(2)}) collective-permute-start(bf16[272,384]{1,0:T(8,128)(2,1)S(1)} %collective-permute-done.refs_1_), channel_id=1, source_target_pairs={{0,4},{4,8},{8,12},{12,16},{16,20},{20,24},{24,28},{28,32},{32,36}... | collective-permute-start | bytes 626696 | tf_op jit(solution)/shard_map/ppermute | solution.py:267
  55.9 0.0 collective-permute-done.1.refs_2_
  55.9 9.1 %collective-permute-start.3 = (bf16[272,384]{1,0:T(8,128)(2,1)S(1)}, bf16[272,384]{1,0:T(8,128)(2,1)S(1)}, u32[]{:S(2)}, u32[]{:S(2)}) collective-permute-start(bf16[272,384]{1,0:T(8,128)(2,1)S(1)} %collective-permute-done.1.refs_2_), channel_id=1, source_target_pairs={{4,0},{8,4},{12,8},{16,12},{20,16},{24,20},{28,24},{32,28},{36,32}... | collective-permute-start | bytes 626696 | tf_op jit(solution)/shard_map/ppermute | solution.py:267
  65.0 0.8 shard_map.113
  65.8 4.2 %all-to-all-start.2 = ((bf16[8,72,384]{2,1,0:T(8,128)(2,1)}), bf16[8,72,384]{2,1,0:T(8,128)(2,1)S(1)}, u32[]{:S(2)}, u32[]{:S(2)}) async-start(bf16[8,72,384]{2,1,0:T(8,128)(2,1)} %shard_map.113), calls=%async_computation.2 | async-start | bytes 884736 | tf_op jit(solution)/shard_map/all_to_all | solution.py:335
  70.1 0.0 collective-permute-done.2.refs_3_
  70.1 1.9 %collective-permute-start.4 = (bf16[272,384]{1,0:T(8,128)(2,1)S(1)}, bf16[272,384]{1,0:T(8,128)(2,1)S(1)}, u32[]{:S(2)}, u32[]{:S(2)}) collective-permute-start(bf16[272,384]{1,0:T(8,128)(2,1)S(1)} %collective-permute-done.2.refs_3_), channel_id=1, source_target_pairs={{0,4},{4,8},{8,12},{12,16},{16,20},{20,24},{24,28},{28,32},{32,36}... | collective-permute-start | bytes 626696 | tf_op jit(solution)/shard_map/ppermute | solution.py:267
  72.0 0.0 collective-permute-done.3.refs_4_
  72.0 9.1 %collective-permute-start.5 = (bf16[272,384]{1,0:T(8,128)(2,1)S(1)}, bf16[272,384]{1,0:T(8,128)(2,1)S(1)}, u32[]{:S(2)}, u32[]{:S(2)}) collective-permute-start(bf16[272,384]{1,0:T(8,128)(2,1)S(1)} %collective-permute-done.3.refs_4_), channel_id=1, source_target_pairs={{4,0},{8,4},{12,8},{16,12},{20,16},{24,20},{28,24},{32,28},{36,32}... | collective-permute-start | bytes 626696 | tf_op jit(solution)/shard_map/ppermute | solution.py:267
  81.1 0.9 collective-permute-start.8
  82.0 0.4 collective-permute-done.4.refs_5_
  82.4 1.9 %collective-permute-start.6 = (bf16[272,384]{1,0:T(8,128)(2,1)S(1)}, bf16[272,384]{1,0:T(8,128)(2,1)S(1)}, u32[]{:S(2)}, u32[]{:S(2)}) collective-permute-start(bf16[272,384]{1,0:T(8,128)(2,1)S(1)} %collective-permute-done.4.refs_5_), channel_id=1, source_target_pairs={{0,4},{4,8},{8,12},{12,16},{16,20},{20,24},{24,28},{28,32},{32,36}... | collective-permute-start | bytes 626696 | tf_op jit(solution)/shard_map/ppermute | solution.py:267
  84.4 0.0 collective-permute-done.5.refs_6_
  84.4 9.1 %collective-permute-start.7 = (bf16[272,384]{1,0:T(8,128)(2,1)S(1)}, bf16[272,384]{1,0:T(8,128)(2,1)S(1)}, u32[]{:S(2)}, u32[]{:S(2)}) collective-permute-start(bf16[272,384]{1,0:T(8,128)(2,1)S(1)} %collective-permute-done.5.refs_6_), channel_id=1, source_target_pairs={{4,0},{8,4},{12,8},{16,12},{20,16},{24,20},{28,24},{32,28},{36,32}... | collective-permute-start | bytes 626696 | tf_op jit(solution)/shard_map/ppermute | solution.py:267
  93.5 5.7 %shard_map.114.fresh = bf16[3,192,384]{2,1,0:T(8,128)(2,1)S(1)} custom-call(bf16[576,384]{1,0:T(8,128)(2,1)S(1)} %bitcast.6, f32[2,192,384]{2,1,0:T(8,128)} %gate_hbm.1, f32[2,192,384]{2,1,0:T(8,128)} %up_hbm.1, f32[2,192,384]{2,1,0:T(8,128)} %down_hbm.1, f32[2]{0:T(128)} %step_hbm.1), custom_call_target="tpu_custom_call" | custom-call | flops 10000000000 | bytes 3145728 | tf_op jit(solution)/shard_map/pallas_call | solution.py:249
  99.2 2.5 %shard_map.115 = bf16[256,192]{1,0:T(8,128)(2,1)S(1)} custom-call(bf16[256,192]{1,0:T(8,128)(2,1)S(1)} %get-tuple-element.19.query_ref, bf16[3,192,384]{2,1,0:T(8,128)(2,1)S(1)} %shard_map.114.fresh, bf16[272,384]{1,0:T(8,128)(2,1)S(1)} %get-tuple-element.20.packed.refs_0_, bf16[272,384]{1,0:T(8,128)(2,1)S(1)} %collective-permute-done.refs_1_, ...), custom_call_target="tpu_custom_call" | custom-call | flops 603979776 | bytes 3145728 | tf_op jit(solution)/shard_map/pallas_call | solution.py:249
  101.8 0.0 copy-start
  101.8 11.5 %all-gather = bf16[1024,192]{1,0:T(8,128)(2,1)S(1)} all-gather(bf16[256,192]{1,0:T(8,128)(2,1)S(1)} %shard_map.115), channel_id=2, replica_groups=mesh['xh'=2,'y'=4,'z'=8,'core'=2,'xl'=2] {'xl','core'}, dimensions={0}, use_global_device_ids=true | all-gather | bytes 491520 | tf_op jit(solution)/shard_map/all_gather | solution.py:361
  113.3 0.9 shard_map.116
  (9 shorter events, 0.0 us)
Async XLA Ops:
  1.5 7.9 %copy-start.3 = (f32[2,192,384]{2,1,0:T(8,128)S(1)}, f32[2,192,384]{2,1,0:T(8,128)}, u32[]{:S(2)}) copy-start(f32[2,192,384]{2,1,0:T(8,128)} %down_hbm.1) | copy-start | bytes 1769476
  8.6 1.1 copy-start.1
  8.6 1.2 %copy-start.2 = (f32[2,192,384]{2,1,0:T(8,128)S(1)}, f32[2,192,384]{2,1,0:T(8,128)}, u32[]{:S(2)}) copy-start(f32[2,192,384]{2,1,0:T(8,128)} %up_hbm.1) | copy-start | bytes 1769476
  26.6 38.4 %all-to-all-start.1 = ((bf16[8,72,384]{2,1,0:T(8,128)(2,1)}), bf16[8,72,384]{2,1,0:T(8,128)(2,1)S(1)}, u32[]{:S(2)}, u32[]{:S(2)}) async-start(bf16[8,72,384]{2,1,0:T(8,128)(2,1)} %shard_map.112), calls=%async_computation.1 | async-start | bytes 884736 | tf_op jit(solution)/shard_map/all_to_all | solution.py:333
  34.8 19.2 %collective-permute-start = (bf16[272,384]{1,0:T(8,128)(2,1)S(1)}, bf16[272,384]{1,0:T(8,128)(2,1)S(1)}, u32[]{:S(2)}, u32[]{:S(2)}) collective-permute-start(bf16[272,384]{1,0:T(8,128)(2,1)S(1)} %get-tuple-element.20.packed.refs_0_), channel_id=1, source_target_pairs={{0,4},{4,8},{8,12},{12,16},{16,20},{20,24},{24,28},{28,32},{32,36}... | collective-permute-start | bytes 626696 | tf_op jit(solution)/shard_map/ppermute | solution.py:267
  38.1 17.7 %collective-permute-start.1 = (bf16[272,384]{1,0:T(8,128)(2,1)S(1)}, bf16[272,384]{1,0:T(8,128)(2,1)S(1)}, u32[]{:S(2)}, u32[]{:S(2)}) collective-permute-start(bf16[272,384]{1,0:T(8,128)(2,1)S(1)} %get-tuple-element.20.packed.refs_0_), channel_id=1, source_target_pairs={{4,0},{8,4},{12,8},{16,12},{20,16},{24,20},{28,24},{32,28},{36,32}... | collective-permute-start | bytes 626696 | tf_op jit(solution)/shard_map/ppermute | solution.py:267
  54.0 16.1 %collective-permute-start.2 = (bf16[272,384]{1,0:T(8,128)(2,1)S(1)}, bf16[272,384]{1,0:T(8,128)(2,1)S(1)}, u32[]{:S(2)}, u32[]{:S(2)}) collective-permute-start(bf16[272,384]{1,0:T(8,128)(2,1)S(1)} %collective-permute-done.refs_1_), channel_id=1, source_target_pairs={{0,4},{4,8},{8,12},{12,16},{16,20},{20,24},{24,28},{28,32},{32,36}... | collective-permute-start | bytes 626696 | tf_op jit(solution)/shard_map/ppermute | solution.py:267
  55.9 16.1 %collective-permute-start.3 = (bf16[272,384]{1,0:T(8,128)(2,1)S(1)}, bf16[272,384]{1,0:T(8,128)(2,1)S(1)}, u32[]{:S(2)}, u32[]{:S(2)}) collective-permute-start(bf16[272,384]{1,0:T(8,128)(2,1)S(1)} %collective-permute-done.1.refs_2_), channel_id=1, source_target_pairs={{4,0},{8,4},{12,8},{16,12},{20,16},{24,20},{28,24},{32,28},{36,32}... | collective-permute-start | bytes 626696 | tf_op jit(solution)/shard_map/ppermute | solution.py:267
  65.8 27.6 %all-to-all-start.2 = ((bf16[8,72,384]{2,1,0:T(8,128)(2,1)}), bf16[8,72,384]{2,1,0:T(8,128)(2,1)S(1)}, u32[]{:S(2)}, u32[]{:S(2)}) async-start(bf16[8,72,384]{2,1,0:T(8,128)(2,1)} %shard_map.113), calls=%async_computation.2 | async-start | bytes 884736 | tf_op jit(solution)/shard_map/all_to_all | solution.py:335
  70.1 12.4 %collective-permute-start.4 = (bf16[272,384]{1,0:T(8,128)(2,1)S(1)}, bf16[272,384]{1,0:T(8,128)(2,1)S(1)}, u32[]{:S(2)}, u32[]{:S(2)}) collective-permute-start(bf16[272,384]{1,0:T(8,128)(2,1)S(1)} %collective-permute-done.2.refs_3_), channel_id=1, source_target_pairs={{0,4},{4,8},{8,12},{12,16},{16,20},{20,24},{24,28},{28,32},{32,36}... | collective-permute-start | bytes 626696 | tf_op jit(solution)/shard_map/ppermute | solution.py:267
  72.0 12.3 %collective-permute-start.5 = (bf16[272,384]{1,0:T(8,128)(2,1)S(1)}, bf16[272,384]{1,0:T(8,128)(2,1)S(1)}, u32[]{:S(2)}, u32[]{:S(2)}) collective-permute-start(bf16[272,384]{1,0:T(8,128)(2,1)S(1)} %collective-permute-done.3.refs_4_), channel_id=1, source_target_pairs={{4,0},{8,4},{12,8},{16,12},{20,16},{24,20},{28,24},{32,28},{36,32}... | collective-permute-start | bytes 626696 | tf_op jit(solution)/shard_map/ppermute | solution.py:267
  81.1 32.2 %collective-permute-start.8 = (bf16[384,384]{1,0:T(8,128)(2,1)S(1)}, bf16[384,384]{1,0:T(8,128)(2,1)S(1)}, u32[]{:S(2)}, u32[]{:S(2)}) collective-permute-start(bf16[384,384]{1,0:T(8,128)(2,1)S(1)} %get-tuple-element.22), channel_id=1, source_target_pairs={{0,1},{1,0},{2,3},{3,2},{4,5},{5,4},{6,7},{7,6},{8,9},{9,8},{10,11... | collective-permute-start | bytes 884744 | tf_op jit(solution)/shard_map/ppermute | solution.py:360
  82.4 16.8 %collective-permute-start.6 = (bf16[272,384]{1,0:T(8,128)(2,1)S(1)}, bf16[272,384]{1,0:T(8,128)(2,1)S(1)}, u32[]{:S(2)}, u32[]{:S(2)}) collective-permute-start(bf16[272,384]{1,0:T(8,128)(2,1)S(1)} %collective-permute-done.4.refs_5_), channel_id=1, source_target_pairs={{0,4},{4,8},{8,12},{12,16},{16,20},{20,24},{24,28},{28,32},{32,36}... | collective-permute-start | bytes 626696 | tf_op jit(solution)/shard_map/ppermute | solution.py:267
  84.4 14.9 %collective-permute-start.7 = (bf16[272,384]{1,0:T(8,128)(2,1)S(1)}, bf16[272,384]{1,0:T(8,128)(2,1)S(1)}, u32[]{:S(2)}, u32[]{:S(2)}) collective-permute-start(bf16[272,384]{1,0:T(8,128)(2,1)S(1)} %collective-permute-done.5.refs_6_), channel_id=1, source_target_pairs={{4,0},{8,4},{12,8},{16,12},{20,16},{24,20},{28,24},{32,28},{36,32}... | collective-permute-start | bytes 626696 | tf_op jit(solution)/shard_map/ppermute | solution.py:267
  101.8 11.5 %copy-start = (bf16[384,768]{1,0:T(8,128)(2,1)S(1)}, bf16[384,768]{1,0:T(8,128)(2,1)}, u32[]{:S(2)}) copy-start(bf16[384,768]{1,0:T(8,128)(2,1)} %weight.1) | copy-start | bytes 1769476
